TPU v7x, 32 devices: a whole 2x2x4 slice. The times are simulated.
32 devices in a mesh: seq: 2 (over x), row: 4 (over y, core), col: 4 (over z).
Axes of the slice: x: 2, y: 2, z: 4, core: 2. Of those that a mesh axis runs over, the one named last changes fastest.
Arguments:
- inputs: bfloat16 [2, 8, 1024, 768], P(None, ('seq', 'row'), 'col'), may hold values from -6 to 6
- segment_ids: int32 [2, 8, 1024], P(None, ('seq', 'row')), may hold values from 0 to 7, never falling along the last dimension, each value on 1 to 512 neighbouring positions
- query_weight: bfloat16 [768, 768], P(('seq', 'row'), 'col'), may hold values from -0.21875 to 0.21875
- key_weight: bfloat16 [768, 768], P(('seq', 'row'), 'col'), may hold values from -0.21875 to 0.21875
- value_weight: bfloat16 [768, 768], P(('seq', 'row'), 'col'), may hold values from -0.21875 to 0.21875
- query_bias: bfloat16 [768], P('col'), may hold values from -1.25 to 1.25
- value_bias: bfloat16 [768], P('col'), may hold values from -1.25 to 1.25
- output_weight: bfloat16 [768, 768], P('col', ('seq', 'row')), may hold values from -0.875 to 0.875
- output_bias: bfloat16 [768], replicated, may hold values from -1.25 to 1.25
- first_gain: bfloat16 [768], replicated, may hold values from 0.5 to 1.5
- first_shift: bfloat16 [768], replicated, may hold values from -1.25 to 1.25
- hidden_weight: bfloat16 [768, 3072], P(('seq', 'row'), 'col'), may hold values from -0.21875 to 0.21875
- hidden_bias: bfloat16 [3072], P('col'), may hold values from -1.25 to 1.25
- down_weight: bfloat16 [3072, 768], P('col', ('seq', 'row')), may hold values from -0.109375 to 0.109375
- down_bias: bfloat16 [768], replicated, may hold values from -1.25 to 1.25
- second_gain: bfloat16 [768], replicated, may hold values from 0.5 to 1.5
- second_shift: bfloat16 [768], replicated, may hold values from -1.25 to 1.25
- cotangent: bfloat16 [2, 8, 1024, 768], P(None, ('seq', 'row'), 'col'), may hold values from -6 to 6
Outputs:
- outputs: bfloat16 [2, 8, 1024, 768], P(None, ('seq', 'row'), 'col')
- input_grad: float32 [2, 8, 1024, 768], P(None, ('seq', 'row'), 'col')
- grad_query_weight: float32 [768, 768], P(('seq', 'row'), 'col')
- grad_key_weight: float32 [768, 768], P(('seq', 'row'), 'col')
- grad_value_weight: float32 [768, 768], P(('seq', 'row'), 'col')
- grad_query_bias: float32 [768], P('col')
- grad_value_bias: float32 [768], P('col')
- grad_output_weight: float32 [768, 768], P('col', ('seq', 'row'))
- grad_output_bias: float32 [768], replicated
- grad_first_gain: float32 [768], replicated
- grad_first_shift: float32 [768], replicated
- grad_hidden_weight: float32 [768, 3072], P(('seq', 'row'), 'col')
- grad_hidden_bias: float32 [3072], P('col')
- grad_down_weight: float32 [3072, 768], P('col', ('seq', 'row'))
- grad_down_bias: float32 [768], replicated
- grad_second_gain: float32 [768], replicated
- grad_second_shift: float32 [768], replicated
Inputs may be any that keep to these rules, and one draw needn't show every extreme that they name: `segment_ids`: in each sequence the document numbers never fall along the positions; a document holds at most 512 positions, and some document holds exactly that many.
All inputs are finite; a program needn't handle non-finite values.
Results may differ from a plain program's by a relative error of at most 0.014.
Values may be sent and summed in bfloat16 or wider, within the bound.
A program may use at most 128 MiB of HBM per device.

v0:
```python
import jax
import jax.numpy as jnp
from jax import lax
from jax.sharding import PartitionSpec as P

HEAD_DIM = 64


NORM_EPS = 1e-05
MASK_VALUE = -1000000000.0


def layer_norm(summed, gain, shift):
    center = jnp.mean(summed, -1, keepdims=True)
    deviation = summed - center
    variance = jnp.mean(deviation * deviation, -1, keepdims=True)
    return deviation * lax.rsqrt(variance + NORM_EPS) * gain + shift


def gelu_exact(hidden_pre):
    return jax.nn.gelu(hidden_pre, approximate=False)


def contract_rows(left, right):
    return lax.dot_general(
        left, right, (((0,), (0,)), ((), ())), preferred_element_type=jnp.float32
    )


def contract_cols(left, right):
    return lax.dot_general(
        left, right, (((1,), (1,)), ((), ())), preferred_element_type=jnp.float32
    )


def masked_logits(query_block, segment_block, keys_heads, segment_row):
    scores = jnp.einsum("qhd,khd->hqk", query_block, keys_heads, preferred_element_type=jnp.float32)
    same_doc = segment_block[:, None] == segment_row[None, :]
    return jnp.where(same_doc[None], scores * HEAD_DIM ** (-0.5), MASK_VALUE)


def attend_forward(query_block, segment_block, keys_heads, values_heads, segment_row):
    logits = masked_logits(query_block, segment_block, keys_heads, segment_row)
    largest = jnp.max(logits, -1, keepdims=True)
    exp_terms = jnp.exp(logits - largest)
    row_total = jnp.sum(exp_terms, -1, keepdims=True)
    probs_low = (exp_terms / row_total).astype(jnp.bfloat16)
    mixed = jnp.einsum("hqk,khd->qhd", probs_low, values_heads, preferred_element_type=jnp.float32)
    return (mixed, largest + jnp.log(row_total))


def accumulate(running, fresh):
    if running is None:
        return fresh
    return tuple((left + right for left, right in zip(running, fresh)))


def per_device(
    inputs,
    segment_ids,
    query_weight,
    key_weight,
    value_weight,
    query_bias,
    value_bias,
    output_weight,
    output_bias,
    first_gain,
    first_shift,
    hidden_weight,
    hidden_bias,
    down_weight,
    down_bias,
    second_gain,
    second_shift,
    cotangent,
):
    floats = jnp.float32
    halves = jnp.bfloat16
    query_bias_wide = query_bias.astype(floats)
    value_bias_wide = value_bias.astype(floats)
    output_bias_wide = output_bias.astype(floats)
    first_gain_wide = first_gain.astype(floats)
    first_shift_wide = first_shift.astype(floats)
    hidden_bias_wide = hidden_bias.astype(floats)
    down_bias_wide = down_bias.astype(floats)
    second_gain_wide = second_gain.astype(floats)
    second_shift_wide = second_shift.astype(floats)
    score_scale = HEAD_DIM ** (-0.5)
    out_rows = []
    grad_rows = []
    weight_total = None
    vector_total = None
    head_total = None
    for batch_index in range(inputs.shape[0]):
        query_full, key_full, value_full, hidden_full, output_full, down_full = (
            lax.all_gather(query_weight, ("seq", "row"), axis=0, tiled=True),
            lax.all_gather(key_weight, ("seq", "row"), axis=0, tiled=True),
            lax.all_gather(value_weight, ("seq", "row"), axis=0, tiled=True),
            lax.all_gather(hidden_weight, ("seq", "row"), axis=0, tiled=True),
            lax.all_gather(output_weight, ("seq", "row"), axis=1, tiled=True),
            lax.all_gather(down_weight, ("seq", "row"), axis=1, tiled=True),
        )
        input_rows = inputs[batch_index, 0]
        segment_row = segment_ids[batch_index, 0]
        gathered = lax.all_gather(input_rows, "col", axis=0, tiled=True)
        length = gathered.shape[0]
        query_low = (
            jnp.dot(gathered, query_full, preferred_element_type=floats) + query_bias_wide
        ).astype(halves)
        key_low = jnp.dot(gathered, key_full, preferred_element_type=floats).astype(halves)
        value_low = (
            jnp.dot(gathered, value_full, preferred_element_type=floats) + value_bias_wide
        ).astype(halves)
        head_count = query_low.shape[1] // HEAD_DIM
        block_rows = min(512, length)
        block_count = length // block_rows
        block_shape = (block_count, block_rows, head_count, HEAD_DIM)
        keys_heads = key_low.reshape(length, head_count, HEAD_DIM)
        values_heads = value_low.reshape(length, head_count, HEAD_DIM)
        query_blocks = query_low.reshape(block_shape)
        segment_blocks = segment_row.reshape(block_count, block_rows)
        mixed, log_total = lax.map(
            lambda block_pair: attend_forward(
                block_pair[0], block_pair[1], keys_heads, values_heads, segment_row
            ),
            (query_blocks, segment_blocks),
        )
        mixed_low = mixed.reshape(length, head_count * HEAD_DIM).astype(halves)
        attn_sum = lax.psum_scatter(
            jnp.dot(mixed_low, output_full, preferred_element_type=floats),
            "col",
            scatter_dimension=0,
            tiled=True,
        )
        first_sum = input_rows.astype(floats) + attn_sum + output_bias_wide
        normed = layer_norm(first_sum, first_gain_wide, first_shift_wide)
        normed_all = lax.all_gather(normed.astype(halves), "col", axis=0, tiled=True)
        hidden_pre = (
            jnp.dot(normed_all, hidden_full, preferred_element_type=floats) + hidden_bias_wide
        )
        activated_low = gelu_exact(hidden_pre).astype(halves)
        ffn_sum = lax.psum_scatter(
            jnp.dot(activated_low, down_full, preferred_element_type=floats).astype(jnp.bfloat16),
            "col",
            scatter_dimension=0,
            tiled=True,
        ).astype(jnp.float32)
        second_sum = normed + ffn_sum + down_bias_wide
        out_rows.append(layer_norm(second_sum, second_gain_wide, second_shift_wide).astype(halves))
        cot_rows = cotangent[batch_index, 0].astype(floats)
        second_pull = jax.vjp(layer_norm, second_sum, second_gain_wide, second_shift_wide)[1]
        second_grad, second_gain_term, second_shift_term = second_pull(cot_rows)
        down_bias_term = jnp.sum(second_grad, 0)
        ffn_grad_all = lax.all_gather(second_grad.astype(halves), "col", axis=0, tiled=True)
        down_wgrad = contract_rows(activated_low, ffn_grad_all)
        act_grad = contract_cols(ffn_grad_all, down_full)
        gelu_pull = jax.vjp(gelu_exact, hidden_pre)[1]
        pre_grad_low = gelu_pull(act_grad)[0].astype(halves)
        hidden_bias_term = jnp.sum(pre_grad_low.astype(floats), 0)
        hidden_wgrad = contract_rows(normed_all, pre_grad_low)
        normed_grad = (
            lax.psum_scatter(
                contract_cols(pre_grad_low, hidden_full), "col", scatter_dimension=0, tiled=True
            )
            + second_grad
        )
        first_pull = jax.vjp(layer_norm, first_sum, first_gain_wide, first_shift_wide)[1]
        first_grad, first_gain_term, first_shift_term = first_pull(normed_grad)
        output_bias_term = jnp.sum(first_grad, 0)
        attn_grad_all = lax.all_gather(first_grad.astype(halves), "col", axis=0, tiled=True)
        output_wgrad = contract_rows(mixed_low, attn_grad_all)
        mixed_grad_low = contract_cols(attn_grad_all, output_full).astype(halves)
        grad_blocks = mixed_grad_low.reshape(block_shape)

        def attend_backward(running, block_input):
            key_accum, value_accum = running
            query_block, segment_block, grad_block, block_log_total = block_input
            logits = masked_logits(query_block, segment_block, keys_heads, segment_row)
            attn_probs = jnp.exp(logits - block_log_total)
            probs_low = attn_probs.astype(halves)
            value_accum = value_accum + jnp.einsum(
                "hqk,qhd->khd", probs_low, grad_block, preferred_element_type=floats
            )
            prob_grad = jnp.einsum(
                "qhd,khd->hqk", grad_block, values_heads, preferred_element_type=floats
            )
            inner_sum = jnp.sum(attn_probs * prob_grad, -1, keepdims=True)
            score_grad = (attn_probs * (prob_grad - inner_sum) * score_scale).astype(halves)
            query_block_grad = jnp.einsum(
                "hqk,khd->qhd", score_grad, keys_heads, preferred_element_type=floats
            ).astype(halves)
            key_accum = key_accum + jnp.einsum(
                "hqk,qhd->khd", score_grad, query_block, preferred_element_type=floats
            )
            return ((key_accum, value_accum), query_block_grad)

        zero_heads = jnp.zeros((length, head_count, HEAD_DIM), floats)
        (key_accum, value_accum), query_grad_blocks = lax.scan(
            attend_backward,
            (zero_heads, zero_heads),
            (query_blocks, segment_blocks, grad_blocks, log_total),
        )
        query_grad_low = query_grad_blocks.reshape(length, head_count * HEAD_DIM)
        key_grad_low = key_accum.reshape(length, head_count * HEAD_DIM).astype(halves)
        value_grad_low = value_accum.reshape(length, head_count * HEAD_DIM).astype(halves)
        query_bias_term = jnp.sum(query_grad_low.astype(floats), 0)
        value_bias_term = jnp.sum(value_grad_low.astype(floats), 0)
        query_wgrad = contract_rows(gathered, query_grad_low)
        key_wgrad = contract_rows(gathered, key_grad_low)
        value_wgrad = contract_rows(gathered, value_grad_low)
        grad_rows.append(
            lax.psum_scatter(
                (
                    contract_cols(query_grad_low, query_full)
                    + contract_cols(key_grad_low, key_full)
                    + contract_cols(value_grad_low, value_full)
                ).astype(jnp.bfloat16),
                "col",
                scatter_dimension=0,
                tiled=True,
            ).astype(jnp.float32)
            + first_grad
        )
        weight_terms = (
            lax.psum_scatter(query_wgrad, ("seq", "row"), scatter_dimension=0, tiled=True),
            lax.psum_scatter(key_wgrad, ("seq", "row"), scatter_dimension=0, tiled=True),
            lax.psum_scatter(value_wgrad, ("seq", "row"), scatter_dimension=0, tiled=True),
            lax.psum_scatter(hidden_wgrad, ("seq", "row"), scatter_dimension=0, tiled=True),
            lax.psum_scatter(output_wgrad, ("seq", "row"), scatter_dimension=1, tiled=True),
            lax.psum_scatter(down_wgrad, ("seq", "row"), scatter_dimension=1, tiled=True),
        )
        weight_total = accumulate(weight_total, weight_terms)
        vector_total = accumulate(
            vector_total,
            (
                output_bias_term,
                first_gain_term,
                first_shift_term,
                down_bias_term,
                second_gain_term,
                second_shift_term,
            ),
        )
        head_total = accumulate(head_total, (query_bias_term, value_bias_term, hidden_bias_term))
    bias_out, gain_one, shift_one, bias_down, gain_two, shift_two = vector_total
    vector_sums = lax.psum(
        (bias_out, gain_one, shift_one, bias_down, gain_two, shift_two), ("seq", "row", "col")
    )
    bias_query, bias_value, bias_hidden = head_total
    head_sums = lax.psum((bias_query, bias_value, bias_hidden), ("seq", "row"))
    outputs = jnp.stack(out_rows)[:, None]
    input_grad = jnp.stack(grad_rows)[:, None]
    return (
        outputs,
        input_grad,
        weight_total[0],
        weight_total[1],
        weight_total[2],
        head_sums[0],
        head_sums[1],
        weight_total[4],
        vector_sums[0],
        vector_sums[1],
        vector_sums[2],
        weight_total[3],
        head_sums[2],
        weight_total[5],
        vector_sums[3],
        vector_sums[4],
        vector_sums[5],
    )


def solution(mesh):
    placed = (
        P(None, ("seq", "row"), "col", None),
        P(None, ("seq", "row"), None),
        P(("seq", "row"), "col"),
        P(("seq", "row"), "col"),
        P(("seq", "row"), "col"),
        P("col"),
        P("col"),
        P("col", ("seq", "row")),
        P(),
        P(),
        P(),
        P(("seq", "row"), "col"),
        P("col"),
        P("col", ("seq", "row")),
        P(),
        P(),
        P(),
        P(None, ("seq", "row"), "col", None),
    )
    return jax.shard_map(
        per_device,
        mesh=mesh,
        in_specs=placed,
        out_specs=(
            P(None, ("seq", "row"), "col", None),
            P(None, ("seq", "row"), "col", None),
            P(("seq", "row"), "col"),
            P(("seq", "row"), "col"),
            P(("seq", "row"), "col"),
            P("col"),
            P("col"),
            P("col", ("seq", "row")),
            P(),
            P(),
            P(),
            P(("seq", "row"), "col"),
            P("col"),
            P("col", ("seq", "row")),
            P(),
            P(),
            P(),
        ),
        check_vma=False,
    )
```

profile of v0, /device:TPU:0, one launch (start us, length us, event | category | flops | bytes accessed | tf_op | source)
XLA Modules:
  0.0 1130.1 jit_solution(4527533242950130857)
XLA Ops:
  71.5 17.5 %all-gather.29.cloned.1.call-done = bf16[1,1,1024,768]{3,2,1,0:T(8,128)(2,1)} async-done(((bf16[1,1,256,768]{3,2,1,0:T(8,128)(2,1)}), bf16[1,1,1024,768]{3,2,1,0:T(8,128)(2,1)}) %all-gather.29.cloned.1.call-update) | async-done | bytes 1572880 | tf_op jit(solution)/shard_map/all_gather | solution.py:106
  109.0 41.5 %reduce-scatter.27.cloned.1.call-done = f32[256,768]{1,0:T(8,128)} async-done(((f32[1024,768]{1,0:T(8,128)}), f32[256,768]{1,0:T(8,128)}) %reduce-scatter.27.cloned.1.call-update) | async-done | bytes 786448 | tf_op jit(solution)/shard_map/reduce_scatter | solution.py:130
  150.6 62.4 %reduce-scatter.23.cloned.1.call-done = f32[256,768]{1,0:T(8,128)} async-done(((f32[1024,768]{1,0:T(8,128)}), f32[256,768]{1,0:T(8,128)}) %reduce-scatter.23.cloned.1.call-update) | async-done | bytes 786448 | tf_op jit(solution)/shard_map/reduce_scatter | solution.py:130
  218.1 35.4 %all-gather.19.cloned.1.call-done = bf16[1024,768]{1,0:T(8,128)(2,1)} async-done(((bf16[256,768]{1,0:T(8,128)(2,1)}), bf16[1024,768]{1,0:T(8,128)(2,1)}) %all-gather.19.cloned.1.call-update) | async-done | bytes 1572880 | tf_op jit(solution)/shard_map/all_gather | solution.py:138
  258.3 33.0 %all-gather.13.cloned.1.call-done = bf16[1024,768]{1,0:T(8,128)(2,1)} async-done(((bf16[256,768]{1,0:T(8,128)(2,1)}), bf16[1024,768]{1,0:T(8,128)(2,1)}) %all-gather.13.cloned.1.call-update) | async-done | bytes 1572880 | tf_op jit(solution)/shard_map/all_gather | solution.py:138
  291.3 17.8 %multiply_convert_fusion.3 = (bf16[1024,768]{1,0:T(8,128)(2,1)}, f32[1024,768]{1,0:T(8,128)}, bf16[1024,768]{1,0:T(8,128)(2,1)}, f32[1024,768]{1,0:T(8,128)}, f32[1024,768]{1,0:T(8,128)}) fusion(f32[768]{0:T(1024)S(1)} %convert_element_type.231, f32[1024,768]{1,0:T(8,128)} %fusion.297, bf16[1024,768]{1,0:T(8,128)(2,1)} %all-gather.13.cloned.1.call-done, ...), kind=kOutput, calls=%fused_computation.157 | convolution fusion | flops 1311768576 | bytes 18484224 | tf_op jit(solution)/shard_map/dot_general | solution.py:140
  325.0 30.9 %reduce-scatter.25.cloned.1.call-done = bf16[256,768]{1,0:T(8,128)(2,1)} async-done(((bf16[1024,768]{1,0:T(8,128)(2,1)}), bf16[256,768]{1,0:T(8,128)(2,1)}) %reduce-scatter.25.cloned.1.call-update) | async-done | bytes 393232 | tf_op jit(solution)/shard_map/reduce_scatter | solution.py:143
  355.8 36.5 %reduce-scatter.29.cloned.1.call-done = bf16[256,768]{1,0:T(8,128)(2,1)} async-done(((bf16[1024,768]{1,0:T(8,128)(2,1)}), bf16[256,768]{1,0:T(8,128)(2,1)}) %reduce-scatter.29.cloned.1.call-update) | async-done | bytes 393232 | tf_op jit(solution)/shard_map/reduce_scatter | solution.py:143
  403.3 32.7 %all-gather.25.cloned.1.call-done = bf16[1024,768]{1,0:T(8,128)(2,1)} async-done(((bf16[256,768]{1,0:T(8,128)(2,1)}), bf16[1024,768]{1,0:T(8,128)(2,1)}) %all-gather.25.cloned.1.call-update) | async-done | bytes 1572880 | tf_op jit(solution)/shard_map/all_gather | solution.py:155
  440.8 32.5 %all-gather.21.cloned.1.call-done = bf16[1024,768]{1,0:T(8,128)(2,1)} async-done(((bf16[256,768]{1,0:T(8,128)(2,1)}), bf16[1024,768]{1,0:T(8,128)(2,1)}) %all-gather.21.cloned.1.call-update) | async-done | bytes 1572880 | tf_op jit(solution)/shard_map/all_gather | solution.py:155
  494.2 54.3 %reduce-scatter.35.cloned.1.call-done = f32[256,768]{1,0:T(8,128)} async-done(((f32[1024,768]{1,0:T(8,128)}), f32[256,768]{1,0:T(8,128)}) %reduce-scatter.35.cloned.1.call-update) | async-done | bytes 786448 | tf_op jit(solution)/shard_map/reduce_scatter | solution.py:163
  548.5 62.5 %reduce-scatter.31.cloned.1.call-done = f32[256,768]{1,0:T(8,128)} async-done(((f32[1024,768]{1,0:T(8,128)}), f32[256,768]{1,0:T(8,128)}) %reduce-scatter.31.cloned.1.call-update) | async-done | bytes 786448 | tf_op jit(solution)/shard_map/reduce_scatter | solution.py:163
  622.2 33.6 %all-gather.23.cloned.1.call-done = bf16[1024,768]{1,0:T(8,128)(2,1)} async-done(((bf16[256,768]{1,0:T(8,128)(2,1)}), bf16[1024,768]{1,0:T(8,128)(2,1)}) %all-gather.23.cloned.1.call-update) | async-done | bytes 1572880 | tf_op jit(solution)/shard_map/all_gather | solution.py:171
  658.5 34.7 %all-gather.27.cloned.1.call-done = bf16[1024,768]{1,0:T(8,128)(2,1)} async-done(((bf16[256,768]{1,0:T(8,128)(2,1)}), bf16[1024,768]{1,0:T(8,128)(2,1)}) %all-gather.27.cloned.1.call-update) | async-done | bytes 1572880 | tf_op jit(solution)/shard_map/all_gather | solution.py:171
  699.5 81.1 %while.56 = (s32[]{:T(128)}, f32[1024,3,64]{0,2,1:T(8,128)}, f32[1024,3,64]{0,2,1:T(8,128)}, bf16[2,512,3,64]{1,3,2,0:T(8,128)(2,1)S(1)}, bf16[2,512,3,64]{1,3,2...) while((s32[]{:T(128)}, f32[1024,3,64]{0,2,1:T(8,128)}, ...), condition=%wide.region_27.28_spmd.clone, body=%wide.region_25.27_spmd.clone.sunk | while | flops 1048941568 | bytes 77774000 | solution.py:199
  707.3 14.5 %fusion.440 = f32[1024,3,64]{0,2,1:T(8,128)} fusion(f32[3,512,1024]{2,1,0:T(8,128)} %fusion.438, f32[3,512,1024]{2,1,0:T(8,128)} %fusion.439, f32[3,512]{1,0:T(4,128)S(1)} %dynamic-slice_bitcast_fusion.4, pred[512,1024]{1,0:T(8,128)(4,1)S(1)} %broadcast_compare_fusion.10, f32[1024,3,64]{0,2,1:T(8,128)} %get-tuple-element.986, pred[]{:T(512)S(6)} %compare.6, ...), kind=kOutput, calls=%fused_computation.54.clone.1 | convolution fusion | flops 219023872 | bytes 28000768 | tf_op jit(solution)/shard_map/while/body/eval_jaxpr/hqk,qhd->khd/dot_general | solution.py:193
  747.8 14.5 %fusion.440 = f32[1024,3,64]{0,2,1:T(8,128)} fusion(f32[3,512,1024]{2,1,0:T(8,128)} %fusion.438, f32[3,512,1024]{2,1,0:T(8,128)} %fusion.439, f32[3,512]{1,0:T(4,128)S(1)} %dynamic-slice_bitcast_fusion.4, pred[512,1024]{1,0:T(8,128)(4,1)S(1)} %broadcast_compare_fusion.10, f32[1024,3,64]{0,2,1:T(8,128)} %get-tuple-element.986, pred[]{:T(512)S(6)} %compare.6, ...), kind=kOutput, calls=%fused_computation.54.clone.1 | convolution fusion | flops 219023872 | bytes 28000768 | tf_op jit(solution)/shard_map/while/body/eval_jaxpr/hqk,qhd->khd/dot_general | solution.py:193
  790.2 82.5 %while.57 = (s32[]{:T(128)}, f32[1024,3,64]{0,2,1:T(8,128)}, f32[1024,3,64]{0,2,1:T(8,128)}, bf16[2,512,3,64]{1,3,2,0:T(8,128)(2,1)}, bf16[2,512,3,64]{1,3,2,0:T...) while((s32[]{:T(128)}, f32[1024,3,64]{0,2,1:T(8,128)}, ...), condition=%wide.region_36.37_spmd.clone, body=%wide.region_34.36_spmd.clone.sunk | while | flops 1048941568 | bytes 77724824 | solution.py:199
  839.2 14.5 %fusion.455 = f32[1024,3,64]{0,2,1:T(8,128)} fusion(f32[3,512,1024]{2,1,0:T(8,128)} %fusion.453, f32[3,512,1024]{2,1,0:T(8,128)} %fusion.454, f32[3,512]{1,0:T(4,128)S(1)} %dynamic-slice_bitcast_fusion.5, pred[512,1024]{1,0:T(8,128)(4,1)S(1)} %broadcast_compare_fusion.11, f32[1024,3,64]{0,2,1:T(8,128)} %get-tuple-element.947, pred[]{:T(512)S(6)} %compare.7, ...), kind=kOutput, calls=%fused_computation.104.clone.1 | convolution fusion | flops 219023872 | bytes 28000768 | tf_op jit(solution)/shard_map/while/body/eval_jaxpr/hqk,qhd->khd/dot_general | solution.py:193
  910.6 40.2 %all-reduce = (f32[768]{0:T(1024)}, f32[768]{0:T(1024)}, f32[768]{0:T(1024)}, f32[768]{0:T(1024)}, f32[768]{0:T(1024)}, /*index=5*/f32[768]{0:T(1024)}) all-reduce(f32[768]{0:T(1024)} %add.386, f32[768]{0:T(1024)S(1)} %add.387, f32[768]{0:T(1024)S(1)} %add.388, ...), channel_id=1, replica_groups=mesh['seq'=2,'row'=4,'col'=4] {'seq','row','col'}, use_global_device_ids=true, to_apply=%region_54.55 | all-reduce | flops 4608 | bytes 36864 | tf_op jit(solution)/shard_map/psum | solution.py:247
  976.8 29.3 %reduce-scatter.39.cloned.1.call-done = f32[96,768]{1,0:T(8,128)} async-done(((f32[768,768]{1,0:T(8,128)}), f32[96,768]{1,0:T(8,128)}) %reduce-scatter.39.cloned.1.call-update) | async-done | bytes 294928 | tf_op jit(solution)/shard_map/reduce_scatter | solution.py:229
  1006.1 38.7 %reduce-scatter.47.cloned.1.call-done = f32[96,192]{1,0:T(8,128)} async-done(((f32[768,192]{1,0:T(8,128)}), f32[96,192]{1,0:T(8,128)}) %reduce-scatter.47.cloned.1.call-update) | async-done | bytes 73744
  1044.8 38.7 %reduce-scatter.45.cloned.1.call-done = f32[96,192]{1,0:T(8,128)} async-done(((f32[768,192]{1,0:T(8,128)}), f32[96,192]{1,0:T(8,128)}) %reduce-scatter.45.cloned.1.call-update) | async-done | bytes 73744
  1083.5 38.7 %reduce-scatter.43.cloned.1.call-done = f32[96,192]{1,0:T(8,128)} async-done(((f32[768,192]{1,0:T(8,128)}), f32[96,192]{1,0:T(8,128)}) %reduce-scatter.43.cloned.1.call-update) | async-done | bytes 73744
  (415 shorter events, 380.8 us)
Async XLA Ops:
  8.1 44.1 %all-gather.31.cloned.1.call-start = ((), (), s32[]{:S(2)}) async-start(), calls=%async_computation.31 | async-start | bytes 1966080 | tf_op jit(solution)/shard_map/all_gather | solution.py:106
  10.2 78.8 %all-gather.29.cloned.1.call-start = ((), (), s32[]{:S(2)}) async-start(), calls=%async_computation.30 | async-start | bytes 1966080 | tf_op jit(solution)/shard_map/all_gather | solution.py:106
  10.9 139.6 %reduce-scatter.27.cloned.1.call-start = ((), (), s32[]{:S(2)}) async-start(), calls=%async_computation.19 | async-start | bytes 3932160 | tf_op jit(solution)/shard_map/reduce_scatter | solution.py:130
  71.3 141.6 %reduce-scatter.23.cloned.1.call-start = ((), (), s32[]{:S(2)}) async-start(), calls=%async_computation.14 | async-start | bytes 3932160 | tf_op jit(solution)/shard_map/reduce_scatter | solution.py:130
  108.3 109.7 %all-gather.15.cloned.1.call-start = ((), (), s32[]{:S(2)}) async-start(), calls=%async_computation.16 | async-start | bytes 1327104 | tf_op jit(solution)/shard_map/all_gather | solution.py:100
  108.9 144.5 %all-gather.19.cloned.1.call-start = ((), (), s32[]{:S(2)}) async-start(), calls=%async_computation.20 | async-start | bytes 1966080 | tf_op jit(solution)/shard_map/all_gather | solution.py:138
  216.4 74.9 %all-gather.13.cloned.1.call-start = ((), (), s32[]{:S(2)}) async-start(), calls=%async_computation.15 | async-start | bytes 1966080 | tf_op jit(solution)/shard_map/all_gather | solution.py:138
  217.0 99.0 %all-gather.17.cloned.1.call-start = ((), (), s32[]{:S(2)}) async-start(), calls=%async_computation.17 | async-start | bytes 1327104 | tf_op jit(solution)/shard_map/all_gather | solution.py:102
  217.7 138.1 %reduce-scatter.25.cloned.1.call-start = ((), (), s32[]{:S(2)}) async-start(), calls=%async_computation.18 | async-start | bytes 1966080 | tf_op jit(solution)/shard_map/reduce_scatter | solution.py:143
  320.4 71.9 %reduce-scatter.29.cloned.1.call-start = ((), (), s32[]{:S(2)}) async-start(), calls=%async_computation.21 | async-start | bytes 1966080 | tf_op jit(solution)/shard_map/reduce_scatter | solution.py:143
  324.9 111.2 %all-gather.25.cloned.1.call-start = ((), (), s32[]{:S(2)}) async-start(), calls=%async_computation.26 | async-start | bytes 1966080 | tf_op jit(solution)/shard_map/all_gather | solution.py:155
  400.2 73.2 %all-gather.21.cloned.1.call-start = ((), (), s32[]{:S(2)}) async-start(), calls=%async_computation.22 | async-start | bytes 1966080 | tf_op jit(solution)/shard_map/all_gather | solution.py:155
  402.9 145.6 %reduce-scatter.35.cloned.1.call-start = ((), (), s32[]{:S(2)}) async-start(), calls=%async_computation.27 | async-start | bytes 3932160 | tf_op jit(solution)/shard_map/reduce_scatter | solution.py:163
  489.2 121.8 %reduce-scatter.31.cloned.1.call-start = ((), (), s32[]{:S(2)}) async-start(), calls=%async_computation.23 | async-start | bytes 3932160 | tf_op jit(solution)/shard_map/reduce_scatter | solution.py:163
  494.2 161.6 %all-gather.23.cloned.1.call-start = ((), (), s32[]{:S(2)}) async-start(), calls=%async_computation.24 | async-start | bytes 1966080 | tf_op jit(solution)/shard_map/all_gather | solution.py:171
  618.7 74.5 %all-gather.27.cloned.1.call-start = ((), (), s32[]{:S(2)}) async-start(), calls=%async_computation.28 | async-start | bytes 1966080 | tf_op jit(solution)/shard_map/all_gather | solution.py:171
  622.1 349.4 %reduce-scatter.49.cloned.1.call-start = ((), (), s32[]{:S(2)}) async-start(), calls=%async_computation.37 | async-start | bytes 884736
  698.2 274.9 %reduce-scatter.33.cloned.1.call-start = ((), (), s32[]{:S(2)}) async-start(), calls=%async_computation.25 | async-start | bytes 1966080 | tf_op jit(solution)/shard_map/reduce_scatter | solution.py:213
  789.4 185.0 %reduce-scatter.37.cloned.1.call-start = ((), (), s32[]{:S(2)}) async-start(), calls=%async_computation.29 | async-start | bytes 1966080 | tf_op jit(solution)/shard_map/reduce_scatter | solution.py:213
  879.6 97.2 %reduce-scatter.41.cloned.1.call-start = ((), (), s32[]{:S(2)}) async-start(), calls=%async_computation.33 | async-start | bytes 2654208 | tf_op jit(solution)/shard_map/reduce_scatter | solution.py:231
  886.0 120.1 %reduce-scatter.39.cloned.1.call-start = ((), (), s32[]{:S(2)}) async-start(), calls=%async_computation.32 | async-start | bytes 2654208 | tf_op jit(solution)/shard_map/reduce_scatter | solution.py:229
  892.2 152.6 %reduce-scatter.47.cloned.1.call-start = ((), (), s32[]{:S(2)}) async-start(), calls=%async_computation.36 | async-start | bytes 884736
  897.5 186.0 %reduce-scatter.45.cloned.1.call-start = ((), (), s32[]{:S(2)}) async-start(), calls=%async_computation.35 | async-start | bytes 884736
  902.7 219.5 %reduce-scatter.43.cloned.1.call-start = ((), (), s32[]{:S(2)}) async-start(), calls=%async_computation.34 | async-start | bytes 884736
  (84 other events, 1061.7 us)
Sparse Core Ops, SparseCore 0:
  11.0 39.7 all-gather.30
  53.0 35.9 all-gather.28
  91.3 59.2 reduce-scatter.26
  152.7 60.1 reduce-scatter.22
  489.4 59.1 reduce-scatter.34
  550.7 60.2 reduce-scatter.30
Sparse Core Ops, SparseCore 1:
  110.7 22.7 all-gather.14
  216.5 36.9 all-gather.18
  255.5 35.8 all-gather.12
  293.2 22.7 all-gather.16
  320.5 35.3 reduce-scatter.24
  358.2 34.1 reduce-scatter.28
  400.2 35.8 all-gather.24
  437.5 35.8 all-gather.20
  618.8 36.9 all-gather.22
  657.4 35.8 all-gather.26
  698.3 33.9 reduce-scatter.48
  789.4 34.3 reduce-scatter.32
  879.6 34.3 reduce-scatter.36
  917.9 41.4 reduce-scatter.40
  963.7 42.3 reduce-scatter.38
  1009.9 34.9 reduce-scatter.46
  1048.6 34.9 reduce-scatter.44
  1087.3 34.9 reduce-scatter.42
where the time goes:
time: 1140 us; the launch traced here: 1130 us
  waiting for transfers between devices  663 us (58%)
  matrix products  279 us (24%)
  blocking collectives  93.9 us (8%)
  other arithmetic  51 us (4%)
  local copies, waits for them, and re-layouts  23.1 us (2%)
  between operations  17.6 us (2%)
    unnamed x28, waiting for transfers between devices  119 us
    reduce_scatter x2, waiting for transfers between devices, per_device(): lax.psum_scatter(contract_cols(pre_grad_low, hidden_full), 'col', scatter...  117 us
    reduce_scatter x2, waiting for transfers between devices, per_device(): lax.psum_scatter(jnp.dot(mixed_low, output_full, preferred_element_type=f...  104 us
    all_gather x2, waiting for transfers between devices, per_device(): lax.all_gather(normed.astype(halves), 'col', axis=0, tiled=True)  68.4 us
    all_gather x2, waiting for transfers between devices, per_device(): lax.all_gather(first_grad.astype(halves), 'col', axis=0, tiled=True)  68.3 us
    reduce_scatter x2, waiting for transfers between devices, per_device(): lax.psum_scatter(jnp.dot(activated_low, down_full, preferred_element_type...  67.4 us
    all_gather x2, waiting for transfers between devices, per_device(): lax.all_gather(second_grad.astype(halves), 'col', axis=0, tiled=True)  65.3 us
    dot_general x4, matrix products, attend_backward(): jnp.einsum('hqk,qhd->khd', score_grad, query_block, preferred_element_typ...  57.9 us
  transfers between devices with their start and end apart: 24, of which 18 were waited for; matrix products, arithmetic and copies ran while one was open for 27% of the time, Pallas kernels for 0%

commit v1 on v0

v1 whole, which is shorter than its diff:
```python
import functools

import jax
import jax.numpy as jnp
from jax import lax
from jax.experimental import pallas as pl
from jax.experimental.pallas import tpu as pltpu
from jax.sharding import PartitionSpec as P

HEAD_DIM = 64
NORM_EPS = 1e-05
MASK_VALUE = -1000000000.0
DOC_MOST = 512
KEY_BLOCK = 256
MESH = pl.DeviceIdType.MESH


def contract_rows(left, right):
    return lax.dot_general(
        left, right, (((0,), (0,)), ((), ())), preferred_element_type=jnp.float32
    )


def contract_cols(left, right):
    return lax.dot_general(
        left, right, (((1,), (1,)), ((), ())), preferred_element_type=jnp.float32
    )


def norm_parts(summed):
    deviation = summed - jnp.mean(summed, -1, keepdims=True)
    scale = lax.rsqrt(jnp.mean(deviation * deviation, -1, keepdims=True) + NORM_EPS)
    return deviation * scale, scale


def norm_back(pull, normal, scale):
    return scale * (
        pull - jnp.mean(pull, -1, keepdims=True) - normal * jnp.mean(pull * normal, -1, keepdims=True)
    )


def attend_kernel(bounds, own_ref, all_ref, wq_ref, wk_ref, wkt_ref, wv_ref, wvt_ref, bq_ref, bv_ref, bvt_ref,
                  segq_ref, segk_ref, mixed_ref, lse_ref, q_ref, k_ref, kt_ref, v_ref, bias, acc, top, total):
    micro = pl.program_id(0)
    low, high = bounds[micro, 0], bounds[micro, 1]
    floats, halves = jnp.float32, jnp.bfloat16
    width = wq_ref.shape[-1]
    heads = width // HEAD_DIM
    rows = own_ref.shape[1]

    @pl.when(pl.program_id(1) == 0)
    def _():
        same = segk_ref[0] == segq_ref[0, 0:1]
        bias[...] = jnp.where(same, 0.0, MASK_VALUE)

    queries = jnp.dot(own_ref[0], wq_ref[0], preferred_element_type=floats) + bq_ref[0]
    queries = queries.astype(halves) * jnp.asarray(HEAD_DIM ** -0.5, halves)
    q_ref[0, 0] = queries
    lane = lax.broadcasted_iota(jnp.int32, (rows, width), 1) // HEAD_DIM
    query_heads = [jnp.where(lane == h, queries, jnp.zeros_like(queries)) for h in range(heads)]
    acc[...] = jnp.zeros_like(acc)
    total[...] = jnp.zeros_like(total)
    top[...] = jnp.full_like(top, 2 * MASK_VALUE)

    def step(block, carry):
        at = pl.ds(pl.multiple_of(block * KEY_BLOCK, KEY_BLOCK), KEY_BLOCK)
        x = all_ref[0, at, :]
        keys = jnp.dot(x, wk_ref[0], preferred_element_type=floats).astype(halves)
        k_ref[0, 0, at, :] = keys
        kt_ref[0, 0, :, at] = contract_cols(wkt_ref[0], x).astype(halves)
        v_ref[0, 0, at, :] = (jnp.dot(x, wv_ref[0], preferred_element_type=floats) + bv_ref[0]).astype(halves)
        values_t = (contract_cols(wvt_ref[0], x) + bvt_ref[0]).astype(halves)
        mask = bias[at, :]
        for h in range(heads):
            s = contract_cols(keys, query_heads[h]) + mask
            old = top[h : h + 1]
            new = jnp.maximum(old, jnp.max(s, 0, keepdims=True))
            p = jnp.exp(s - new)
            shrink = jnp.exp(old - new)
            top[h : h + 1] = new
            total[h : h + 1] = total[h : h + 1] * shrink + jnp.sum(p, 0, keepdims=True)
            part = pl.ds(h * HEAD_DIM, HEAD_DIM)
            acc[part, :] = acc[part, :] * shrink + jnp.dot(
                values_t[h * HEAD_DIM : (h + 1) * HEAD_DIM], p.astype(halves), preferred_element_type=floats
            )
        return carry

    lax.fori_loop(low, high, step, 0)
    for h in range(heads):
        part = pl.ds(h * HEAD_DIM, HEAD_DIM)
        acc[part, :] = acc[part, :] / total[h : h + 1]
    mixed_ref[0, 0] = acc[...].T.astype(halves)
    lse_ref[0, 0] = top[...] + jnp.log(jnp.maximum(total[...], 1e-30))


def attend(bounds, own, everything, wq, wk, wv, bq, bv, seg_own, seg_all):
    micro, rows, model = own.shape
    length = everything.shape[1]
    cols, _, width = wq.shape
    halves = jnp.bfloat16
    weight = pl.BlockSpec((1, model, width), lambda m, c, b: (c, 0, 0))
    weight_t = pl.BlockSpec((1, width, model), lambda m, c, b: (c, 0, 0))
    per = lambda a, b_: pl.BlockSpec((1, 1, a, b_), lambda m, c, b: (c, m, 0, 0))
    spec = pltpu.PrefetchScalarGridSpec(
        num_scalar_prefetch=1,
        grid=(micro, cols),
        in_specs=[
            pl.BlockSpec((1, rows, model), lambda m, c, b: (m, 0, 0)),
            pl.BlockSpec((1, length, model), lambda m, c, b: (m, 0, 0)),
            weight, weight, weight_t, weight, weight_t,
            pl.BlockSpec((1, 1, width), lambda m, c, b: (c, 0, 0)),
            pl.BlockSpec((1, 1, width), lambda m, c, b: (c, 0, 0)),
            pl.BlockSpec((1, width, 1), lambda m, c, b: (c, 0, 0)),
            pl.BlockSpec((1, 1, rows), lambda m, c, b: (m, 0, 0)),
            pl.BlockSpec((1, length, 1), lambda m, c, b: (m, 0, 0)),
        ],
        out_specs=[per(rows, width), per(8, rows), per(rows, width), per(length, width), per(width, length), per(length, width)],
        scratch_shapes=[
            pltpu.VMEM((length, rows), jnp.float32),
            pltpu.VMEM((width, rows), jnp.float32),
            pltpu.VMEM((8, rows), jnp.float32),
            pltpu.VMEM((8, rows), jnp.float32),
        ],
    )
    shape = lambda a, b_, d=halves: jax.ShapeDtypeStruct((cols, micro, a, b_), d)
    return pl.pallas_call(
        attend_kernel,
        grid_spec=spec,
        out_shape=[shape(rows, width), shape(8, rows, jnp.float32), shape(rows, width), shape(length, width), shape(width, length), shape(length, width)],
        compiler_params=pltpu.CompilerParams(vmem_limit_bytes=48 << 20),
        name="attend",
    )(bounds, own, everything, wq, wk, wk.swapaxes(1, 2), wv, wv.swapaxes(1, 2), bq[:, None], bv[:, None], bv[:, :, None],
      seg_own[:, None], seg_all[:, :, None])


def attend_back_kernel(bounds, grad_ref, wot_ref, mixed_ref, lse_ref, q_ref, k_ref, kt_ref, v_ref, segq_ref, segk_ref,
                       dq_ref, dk_ref, dv_ref, bias, acc):
    micro = pl.program_id(0)
    low, high = bounds[micro, 0], bounds[micro, 1]
    floats, halves = jnp.float32, jnp.bfloat16
    rows, width = q_ref.shape[2:]
    heads = width // HEAD_DIM

    @pl.when(pl.program_id(1) == 0)
    def _():
        same = segk_ref[0] == segq_ref[0, 0:1]
        bias[...] = jnp.where(same, 0.0, MASK_VALUE)

    mixed_grad = jnp.dot(grad_ref[0], wot_ref[0], preferred_element_type=floats).astype(halves)
    product = mixed_grad.astype(floats) * mixed_ref[0, 0].astype(floats)
    product_high = product.astype(halves)
    product_low = (product - product_high.astype(floats)).astype(halves)
    pick = (
        lax.broadcasted_iota(jnp.int32, (8, width), 1) // HEAD_DIM == lax.broadcasted_iota(jnp.int32, (8, width), 0)
    ).astype(halves)
    inner = contract_cols(pick, product_high) + contract_cols(pick, product_low)
    lane = lax.broadcasted_iota(jnp.int32, (rows, width), 1) // HEAD_DIM
    queries = q_ref[0, 0]
    query_heads = [jnp.where(lane == h, queries, jnp.zeros_like(queries)) for h in range(heads)]
    grad_heads = [jnp.where(lane == h, mixed_grad, jnp.zeros_like(mixed_grad)) for h in range(heads)]
    acc[...] = jnp.zeros_like(acc)
    dk_ref[...] = jnp.zeros_like(dk_ref)
    dv_ref[...] = jnp.zeros_like(dv_ref)

    def step(block, carry):
        at = pl.ds(pl.multiple_of(block * KEY_BLOCK, KEY_BLOCK), KEY_BLOCK)
        keys = k_ref[0, 0, at, :]
        values = v_ref[0, 0, at, :]
        mask = bias[at, :]
        key_grad = jnp.zeros((KEY_BLOCK, width), floats)
        value_grad = jnp.zeros((KEY_BLOCK, width), floats)
        for h in range(heads):
            s = contract_cols(keys, query_heads[h]) + mask
            p = jnp.exp(s - lse_ref[0, 0, h : h + 1])
            prob_grad = contract_cols(values, grad_heads[h])
            score_grad = (p * (prob_grad - inner[h : h + 1])).astype(halves)
            value_grad = value_grad + jnp.dot(p.astype(halves), grad_heads[h], preferred_element_type=floats)
            key_grad = key_grad + jnp.dot(score_grad, query_heads[h], preferred_element_type=floats)
            part = pl.ds(h * HEAD_DIM, HEAD_DIM)
            acc[part, :] += jnp.dot(kt_ref[0, 0, part, at], score_grad, preferred_element_type=floats)
        dk_ref[0, 0, at, :] = key_grad.astype(halves)
        dv_ref[0, 0, at, :] = value_grad.astype(halves)
        return carry

    lax.fori_loop(low, high, step, 0)
    dq_ref[0, 0] = (acc[...].T * HEAD_DIM ** -0.5).astype(halves)


def attend_back(bounds, grad, wot, mixed, lse, q, k, kt, v, seg_own, seg_all):
    micro, rows, model = grad.shape
    cols, _, length, width = k.shape
    halves = jnp.bfloat16
    per = lambda a, b_: pl.BlockSpec((1, 1, a, b_), lambda m, c, b: (c, m, 0, 0))
    spec = pltpu.PrefetchScalarGridSpec(
        num_scalar_prefetch=1,
        grid=(micro, cols),
        in_specs=[
            pl.BlockSpec((1, rows, model), lambda m, c, b: (m, 0, 0)),
            pl.BlockSpec((1, model, width), lambda m, c, b: (c, 0, 0)),
            per(rows, width), per(8, rows), per(rows, width), per(length, width), per(width, length), per(length, width),
            pl.BlockSpec((1, 1, rows), lambda m, c, b: (m, 0, 0)),
            pl.BlockSpec((1, length, 1), lambda m, c, b: (m, 0, 0)),
        ],
        out_specs=[per(rows, width), per(length, width), per(length, width)],
        scratch_shapes=[pltpu.VMEM((length, rows), jnp.float32), pltpu.VMEM((width, rows), jnp.float32)],
    )
    shape = lambda a, b_, d=halves: jax.ShapeDtypeStruct((cols, micro, a, b_), d)
    return pl.pallas_call(
        attend_back_kernel,
        grid_spec=spec,
        out_shape=[shape(rows, width), shape(length, width), shape(length, width)],
        compiler_params=pltpu.CompilerParams(vmem_limit_bytes=48 << 20),
        name="attend_back",
    )(bounds, grad, wot, mixed, lse, q, k, kt, v, seg_own[:, None], seg_all[:, :, None])


def place(sizes):
    seq, row, col = (lax.axis_index(name) for name in ("seq", "row", "col"))
    lines = {"x": (seq, sizes[0]), "y": (row // 2, sizes[1] // 2), "k": (lax.rem(row, 2), 2), "z": (col, sizes[2])}

    def device(axis, index):
        if axis == "x":
            return (index, row, col)
        if axis == "y":
            return (seq, index * 2 + lax.rem(row, 2), col)
        if axis == "k":
            return (seq, row // 2 * 2 + index, col)
        return (seq, row, index)

    return lines, device


def greet(lines, device):
    barrier = pltpu.get_barrier_semaphore()
    count = 0
    for axis, (mine, size) in lines.items():
        for t in range(1, size):
            pl.semaphore_signal(barrier, inc=1, device_id=device(axis, lax.rem(mine + t, size)), device_id_type=MESH)
            count += 1
    pl.semaphore_wait(barrier, count)


class Post:
    def __init__(self, device, send_sems, recv_sems):
        self.device, self.send_sems, self.recv_sems = device, send_sems, recv_sems
        self.slots, self.sent = {}, []

    def slot(self, key):
        return self.slots.setdefault(key, len(self.slots))

    def copy(self, key, axis, index, source, target):
        n = self.slot(key)
        return pltpu.make_async_remote_copy(
            src_ref=source, dst_ref=target, send_sem=self.send_sems.at[n], recv_sem=self.recv_sems.at[n],
            device_id=self.device(axis, index), device_id_type=MESH,
        )

    def send(self, key, axis, index, source, target, when=None):
        def go():
            self.copy(key, axis, index, source, target).start()

        if when is None:
            go()
        else:
            pl.when(when)(go)
        self.sent.append((key, axis, index, source, target, when))

    def wait(self, key, axis, index, target, when=None):
        def go():
            self.copy(key, axis, index, target, target).wait_recv()

        if when is None:
            go()
        else:
            pl.when(when)(go)

    def close(self):
        for key, axis, index, source, target, when in self.sent:
            def go():
                self.copy(key, axis, index, source, target).wait_send()

            if when is None:
                go()
            else:
                pl.when(when)(go)


def clip(index, size):
    return jnp.clip(index, 0, size - 1)


class LineGather:
    def __init__(self, post, name, axis, line, region, reach=None):
        self.post, self.name, self.axis, self.region = post, name, axis, region
        self.mine, self.size = line
        self.reach = min(self.size - 1, reach or self.size)

    def hop(self, way, t):
        mine, size = self.mine, self.size
        origin, target = mine - way * t, mine + way
        ok = (origin >= 0) & (origin < size) & (target >= 0) & (target < size)
        here = self.region(clip(origin, size))
        self.post.send((self.name, way, t + 1), self.axis, clip(target, size), here, here, ok)

    def start(self):
        for way in (1, -1):
            if self.reach >= 1:
                self.hop(way, 0)

    def finish(self):
        for t in range(1, self.reach + 1):
            for way in (1, -1):
                origin = self.mine - way * t
                ok = (origin >= 0) & (origin < self.size)
                self.post.wait((self.name, way, t), self.axis, clip(self.mine - way, self.size), self.region(clip(origin, self.size)), ok)
                if t < self.reach:
                    self.hop(way, t)


def gather_kernel(sizes, micro, own_ref, shard_ref, every_ref, full_ref, send_sems, recv_sems, local_sems):
    lines, device = place(sizes)
    (x, _), (y, _), (k, _), (z, cols) = (lines[a] for a in "xykz")
    half = shard_ref.shape[-1] // 2
    rows = own_ref.shape[1]
    reach = -(-(DOC_MOST - 1) // rows)
    parts = [pl.ds(p * half, half) for p in (0, 1)]
    local = [pltpu.make_async_copy(shard_ref.at[j], full_ref.at[j, z, x, y, k], local_sems.at[j]) for j in range(3)]
    local += [pltpu.make_async_copy(own_ref.at[m], every_ref.at[m, z], local_sems.at[3 + m]) for m in range(micro)]
    for copy in local:
        copy.start()
    greet(lines, device)
    post = Post(device, send_sems, recv_sems)
    for copy in local:
        copy.wait()
    zs = [LineGather(post, ("z", j), "z", lines["z"], lambda i, j=j: full_ref.at[j, i, x, y, k]) for j in range(3)]
    tokens = [LineGather(post, ("t", m), "z", lines["z"], lambda i, m=m: every_ref.at[m, i], reach) for m in range(micro)]
    second, third = {}, {}
    for j in range(3):
        second[j] = [
            LineGather(post, ("a", j), "y", lines["y"], lambda i, j=j: full_ref.at[j, :, x, i, k, :, parts[0]]),
            LineGather(post, ("b", j), "x", lines["x"], lambda i, j=j: full_ref.at[j, :, i, y, k, :, parts[1]]),
        ]
        third[j] = [
            LineGather(post, ("c", j), "x", lines["x"], lambda i, j=j: full_ref.at[j, :, i, :, k, :, parts[0]]),
            LineGather(post, ("d", j), "y", lines["y"], lambda i, j=j: full_ref.at[j, :, :, i, k, :, parts[1]]),
        ]

    def start(group):
        for line in group:
            line.start()

    def finish(group):
        for line in group:
            line.finish()

    def swap(j):
        plane = full_ref.at[j, :, :, :, k]
        post.send(("k", j), "k", 1 - k, plane, plane)

    start(zs + tokens)
    finish(zs[:1])
    start(second[0])
    finish(zs[1:2])
    finish(second[0])
    start(third[0] + second[1])
    finish(zs[2:])
    finish(tokens)
    finish(second[1])
    start(third[1] + second[2])
    finish(third[0])
    swap(0)
    finish(second[2])
    start(third[2])
    finish(third[1])
    swap(1)
    finish(third[2])
    swap(2)
    for i in range(cols):
        far = (z - i > reach) | (i - z > reach)
        for m in range(micro):
            def fill(m=m, i=i):
                copy = pltpu.make_async_copy(own_ref.at[m], every_ref.at[m, i], local_sems.at[3 + m])
                copy.start()
                copy.wait()

            if i > reach or cols - 1 - i > reach:
                pl.when(far)(fill)
    for j in range(3):
        post.wait(("k", j), "k", 1 - k, full_ref.at[j, :, :, :, 1 - k])
    post.close()


def gather(sizes, own, shard):
    ns, nr, nc = sizes
    ny = nr // 2
    micro, rows, model = own.shape
    _, rb, w = shard.shape
    count = 3 * 2 * (nc - 1) + micro * 2 * (nc - 1) + 3 * (4 * (ny - 1) + 4 * (ns - 1) + 1)
    anywhere = pl.BlockSpec(memory_space=pl.ANY)
    every, full = pl.pallas_call(
        functools.partial(gather_kernel, sizes, micro),
        out_shape=[
            jax.ShapeDtypeStruct((micro, nc, rows, model), own.dtype),
            jax.ShapeDtypeStruct((3, nc, ns, ny, 2, rb, w), shard.dtype),
        ],
        in_specs=[anywhere] * 2,
        out_specs=[anywhere] * 2,
        scratch_shapes=[pltpu.SemaphoreType.DMA((count,)), pltpu.SemaphoreType.DMA((count,)), pltpu.SemaphoreType.DMA((3 + micro,))],
        compiler_params=pltpu.CompilerParams(collective_id=0, has_side_effects=True),
        name="gather",
    )(own, shard)
    return every, full.reshape(3, nc, ns * nr * rb, w)


class LineReduce:
    def __init__(self, post, name, axis, line, region, inbox, add, reach=None):
        self.post, self.name, self.axis, self.region, self.inbox, self.add = post, name, axis, region, inbox, add
        self.mine, self.size = line
        self.reach = min(self.size - 1, reach or self.size)

    def arrived(self, way, e):
        behind, goal = self.mine - way, self.mine + way * e
        return (behind >= 0) & (behind < self.size) & (goal >= 0) & (goal < self.size)

    def take(self, way, e):
        ok = self.arrived(way, e)
        inbox = self.inbox(way, e)
        self.post.wait((self.name, way, e), self.axis, clip(self.mine - way, self.size), inbox, ok)

        @pl.when(ok)
        def _():
            self.add(self.region(clip(self.mine + way * e, self.size)), inbox)

    def forward(self, way, e):
        goal = self.mine + way * e
        ok = (goal >= 0) & (goal < self.size)
        self.post.send((self.name, way, e - 1), self.axis, clip(self.mine + way, self.size),
                       self.region(clip(goal, self.size)), self.inbox(way, e - 1), ok)

    def start(self):
        for way in (1, -1):
            if self.reach >= 1:
                self.forward(way, self.reach)

    def finish(self, last=True):
        for e in range(self.reach - 1, 0, -1):
            for way in (1, -1):
                self.take(way, e)
                self.forward(way, e)
        if last:
            for way in (1, -1):
                if self.reach >= 1:
                    self.take(way, 0)


def reduce_kernel(sizes, micro, own_ref, spread_ref, part_ref, vec_ref, back_ref, block_ref, sums_ref,
                  mine_buf, core_buf, in_a, in_b, in_c, in_d, in_z, tok_buf, tok_in, vec_buf, send_sems, recv_sems, local_sems):
    floats, halves = jnp.float32, jnp.bfloat16
    lines, device = place(sizes)
    (x, ns), (y, ny), (k, _), (z, nc) = (lines[a] for a in "xykz")
    half = part_ref.shape[-1] // 2
    rows = own_ref.shape[1]
    reach = -(-(DOC_MOST - 1) // rows)
    parts = [pl.ds(p * half, half) for p in (0, 1)]
    local = [pltpu.make_async_copy(part_ref.at[j, :, :, :, k], mine_buf.at[j], local_sems.at[j]) for j in range(3)]
    local += [pltpu.make_async_copy(spread_ref.at[m], tok_buf.at[m], local_sems.at[3 + m]) for m in range(micro)]
    for copy in local:
        copy.start()
    greet(lines, device)
    post = Post(device, send_sems, recv_sems)
    for j in range(3):
        post.send(("k", j), "k", 1 - k, part_ref.at[j, :, :, :, 1 - k], core_buf.at[j])

    def plus(target, source):
        target[...] = (target[...].astype(floats) + source[...].astype(floats)).astype(halves)

    def plus_grid(target, source, first, second):
        @pl.loop(0, first * second)
        def _(n):
            plus(target.at[n // second, lax.rem(n, second)], source.at[n // second, lax.rem(n, second)])

    def plus_row(target, source, first):
        @pl.loop(0, first)
        def _(n):
            plus(target.at[n], source.at[n])

    vec_buf[0, 0] = vec_ref[...]

    def vector_start(stage, axis):
        mine, size = lines[axis]
        vec_buf[stage, 1 + mine] = vec_buf[stage, 0]
        for t in range(1, size):
            post.send(("v", stage, t), axis, lax.rem(mine + t, size), vec_buf.at[stage, 0], vec_buf.at[stage, 1 + mine])

    def vector_finish(stage, axis, out):
        mine, size = lines[axis]
        for t in range(1, size):
            origin = lax.rem(mine + size - t, size)
            post.wait(("v", stage, t), axis, origin, vec_buf.at[stage, 1 + origin])
        total = vec_buf[stage, 1]
        for i in range(1, size):
            total = total + vec_buf[stage, 1 + i]
        out[...] = total

    tokens = [
        LineReduce(post, ("t", m), "z", lines["z"], lambda i, m=m: tok_buf.at[m, i],
                   lambda way, e, m=m: tok_in.at[m, (1 - way) // 2, e], plus, reach)
        for m in range(micro)
    ]
    box = lambda way: (1 - way) // 2
    second, third, last = {}, {}, {}
    for j in range(3):
        second[j] = [
            LineReduce(post, ("a", j), "x", lines["x"], lambda i, j=j: mine_buf.at[j, :, i, :, :, parts[0]],
                       lambda way, e, j=j: in_a.at[j, box(way), e], lambda t, s: plus_grid(t, s, nc, ny)),
            LineReduce(post, ("b", j), "y", lines["y"], lambda i, j=j: mine_buf.at[j, :, :, i, :, parts[1]],
                       lambda way, e, j=j: in_b.at[j, box(way), e], lambda t, s: plus_grid(t, s, nc, ns)),
        ]
        third[j] = [
            LineReduce(post, ("c", j), "y", lines["y"], lambda i, j=j: mine_buf.at[j, :, x, i, :, parts[0]],
                       lambda way, e, j=j: in_c.at[j, box(way), e], lambda t, s: plus_row(t, s, nc)),
            LineReduce(post, ("d", j), "x", lines["x"], lambda i, j=j: mine_buf.at[j, :, i, y, :, parts[1]],
                       lambda way, e, j=j: in_d.at[j, box(way), e], lambda t, s: plus_row(t, s, nc)),
        ]
        last[j] = [
            LineReduce(post, ("z", j), "z", lines["z"], lambda i, j=j: mine_buf.at[j, i, x, y],
                       lambda way, e, j=j: in_z.at[j, box(way), e], plus)
        ]

    def start(group):
        for line in group:
            line.start()

    def finish(group):
        for line in group:
            line.finish()

    def core(j):
        local[j].wait()
        post.wait(("k", j), "k", 1 - k, core_buf.at[j])

        @pl.loop(0, nc * ns * ny)
        def _(n):
            at = (n // (ns * ny), lax.rem(n // ny, ns), lax.rem(n, ny))
            plus(mine_buf.at[(j, *at)], core_buf.at[(j, *at)])

    for m in range(micro):
        local[3 + m].wait()
    start(tokens)
    core(0)
    start(second[0])
    vector_start(0, "k")
    core(1)
    start(second[1])
    vector_finish(0, "k", vec_buf.at[1, 0])
    vector_start(1, "y")
    core(2)
    finish(second[0])
    start(third[0])
    start(second[2])
    vector_finish(1, "y", vec_buf.at[2, 0])
    vector_start(2, "x")
    finish(tokens)
    vector_finish(2, "x", vec_buf.at[3, 0])
    vector_start(3, "z")
    finish(second[1])
    start(third[1])
    finish(third[0])
    start(last[0])
    finish(second[2])
    start(third[2])
    finish(third[1])
    start(last[1])
    finish(last[0])
    finish(third[2])
    start(last[2])
    vector_finish(3, "z", sums_ref)
    for m in range(micro):
        back_ref[m] = own_ref[m] + tok_buf[m, z].astype(floats)
    finish(last[1])
    finish(last[2])
    for j in range(3):
        block_ref[j] = mine_buf[j, z, x, y].astype(floats)
    post.close()


def reduce(sizes, own_share, spread, partial, vectors):
    ns, nr, nc = sizes
    ny = nr // 2
    micro, rows, model = own_share.shape
    w = partial.shape[-1]
    rb = partial.shape[2] // (ns * nr)
    halves, floats = jnp.bfloat16, jnp.float32
    reach = min(nc - 1, -(-(DOC_MOST - 1) // rows))
    count = 3 + 2 * (ny - 1 + ns - 1) * 6 + 3 * 2 * (nc - 1) + micro * 2 * reach + (1 + ny - 1 + ns - 1 + nc - 1)
    widest = max(ns, ny, nc, 2)
    extra = -vectors.shape[0] % 8
    vectors = jnp.pad(vectors, ((0, extra), (0, 0)))
    vmem = pl.BlockSpec(memory_space=pltpu.VMEM)
    anywhere = pl.BlockSpec(memory_space=pl.ANY)
    back, blocks, sums = pl.pallas_call(
        functools.partial(reduce_kernel, sizes, micro),
        out_shape=[
            jax.ShapeDtypeStruct((micro, rows, model), floats),
            jax.ShapeDtypeStruct((3, rb, w), floats),
            jax.ShapeDtypeStruct(vectors.shape, floats),
        ],
        in_specs=[vmem, anywhere, anywhere, vmem],
        out_specs=[vmem] * 3,
        scratch_shapes=[
            pltpu.VMEM((3, nc, ns, ny, rb, w), halves),
            pltpu.VMEM((3, nc, ns, ny, rb, w), halves),
            pltpu.VMEM((3, 2, max(ns - 1, 1), nc, ny, rb, w // 2), halves),
            pltpu.VMEM((3, 2, max(ny - 1, 1), nc, ns, rb, w // 2), halves),
            pltpu.VMEM((3, 2, max(ny - 1, 1), nc, rb, w // 2), halves),
            pltpu.VMEM((3, 2, max(ns - 1, 1), nc, rb, w // 2), halves),
            pltpu.VMEM((3, 2, max(nc - 1, 1), rb, w), halves),
            pltpu.VMEM((micro, nc, rows, model), halves),
            pltpu.VMEM((micro, 2, max(reach, 1), rows, model), halves),
            pltpu.VMEM((4, 1 + widest, *vectors.shape), floats),
            pltpu.SemaphoreType.DMA((count,)),
            pltpu.SemaphoreType.DMA((count,)),
            pltpu.SemaphoreType.DMA((3 + micro,)),
        ],
        compiler_params=pltpu.CompilerParams(collective_id=1, has_side_effects=True, vmem_limit_bytes=60 << 20),
        name="reduce",
    )(own_share, spread, partial.reshape(3, nc, ns, ny, 2, rb, w), vectors)
    return back, blocks, sums


def per_device(sizes, inputs, segment_ids, query_weight, key_weight, value_weight, query_bias, value_bias,
               output_weight, output_bias, first_gain, first_shift, hidden_weight, hidden_bias, down_weight,
               down_bias, second_gain, second_shift, cotangent):
    floats, halves = jnp.float32, jnp.bfloat16
    cols = sizes[2]
    micro, _, rows, model = inputs.shape
    length = segment_ids.shape[-1]
    width = query_weight.shape[1]
    here = lax.axis_index("col")
    own = inputs[:, 0]
    shard = jnp.stack([
        jnp.concatenate([query_weight, key_weight, value_weight, output_weight.T], 1),
        hidden_weight,
        down_weight.T,
    ])
    biases = lax.all_gather(jnp.concatenate([query_bias, value_bias, hidden_bias]), "col", axis=0)
    everything, gathered = gather(sizes, own, shard)
    everything = everything.reshape(micro, length, model)
    attn_weights = gathered[0]
    wq, wk, wv, wot = (attn_weights[:, :, i * width : (i + 1) * width] for i in range(4))
    hidden_full, down_full = gathered[1], gathered[2]
    bq, bv, bh = biases[:, :width], biases[:, width : 2 * width], biases[:, 2 * width :]
    seg_all = segment_ids[:, 0]
    seg_own = lax.dynamic_slice_in_dim(seg_all, here * rows, rows, 1)
    first_key = jnp.sum((seg_all < seg_own[:, :1]).astype(jnp.int32), 1)
    last_key = jnp.sum((seg_all <= seg_own[:, -1:]).astype(jnp.int32), 1)
    bounds = jnp.stack([first_key // KEY_BLOCK, (last_key + KEY_BLOCK - 1) // KEY_BLOCK], 1)

    mixed, lse, q, k, kt, v = attend(bounds, own, everything, wq, wk, wv, bq.astype(floats), bv.astype(floats), seg_own, seg_all)
    total = micro * rows
    flat = lambda a: a.reshape(total, -1)
    mixed_flat = mixed.reshape(cols, total, width)
    attn = sum(contract_cols(mixed_flat[c], wot[c]) for c in range(cols))
    first_sum = flat(own).astype(floats) + attn + output_bias.astype(floats)
    normal_one, scale_one = norm_parts(first_sum)
    gain_one = first_gain.astype(floats)
    normed = normal_one * gain_one + first_shift.astype(floats)
    normed_low = normed.astype(halves)
    ffn = 0
    activated, slopes = [], []
    for c in range(cols):
        hidden = jnp.dot(normed_low, hidden_full[c], preferred_element_type=floats) + bh[c].astype(floats)
        half_erf = 0.5 * lax.erf(hidden * 0.7071067811865476) + 0.5
        act = (hidden * half_erf).astype(halves)
        slope = half_erf + hidden * (jnp.exp(-0.5 * hidden * hidden) * 0.3989422804014327)
        activated.append(act)
        slopes.append(slope.astype(halves))
        ffn = ffn + contract_cols(act, down_full[c])
    second_sum = normed + ffn + down_bias.astype(floats)
    normal_two, scale_two = norm_parts(second_sum)
    gain_two = second_gain.astype(floats)
    outputs = (normal_two * gain_two + second_shift.astype(floats)).astype(halves)
    cot = flat(cotangent[:, 0]).astype(floats)
    second_grad = norm_back(cot * gain_two, normal_two, scale_two)
    ffn_grad = second_grad.astype(halves)
    hidden_grads, down_grads, hidden_bias_grads = [], [], []
    normed_grad = second_grad
    for c in range(cols):
        pre = (jnp.dot(ffn_grad, down_full[c], preferred_element_type=floats) * slopes[c].astype(floats)).astype(halves)
        hidden_grads.append(contract_rows(normed_low, pre).astype(halves))
        down_grads.append(contract_rows(ffn_grad, activated[c]).astype(halves))
        hidden_bias_grads.append(jnp.sum(pre.astype(floats), 0))
        normed_grad = normed_grad + contract_cols(pre, hidden_full[c])
    first_grad = norm_back(normed_grad * gain_one, normal_one, scale_one)
    attn_grad = first_grad.astype(halves)
    dq, dk, dv = attend_back(bounds, attn_grad.reshape(micro, rows, model), wot, mixed, lse, q, k, kt, v, seg_own, seg_all)
    every_flat = everything.reshape(micro * length, model)
    attn_grads = []
    own_share = first_grad
    spread = 0
    for c in range(cols):
        dq_c, dk_c, dv_c = dq[c].reshape(total, width), dk[c].reshape(micro * length, width), dv[c].reshape(micro * length, width)
        attn_grads.append(jnp.concatenate([
            contract_rows(flat(own), dq_c), contract_rows(every_flat, dk_c), contract_rows(every_flat, dv_c),
            contract_rows(attn_grad, mixed_flat[c]),
        ], 1).astype(halves))
        own_share = own_share + contract_cols(dq_c, wq[c])
        spread = spread + contract_cols(dk_c, wk[c]) + contract_cols(dv_c, wv[c])
    bias_q = jnp.sum(dq.astype(floats), (1, 2)).reshape(-1)
    bias_v = jnp.sum(dv.astype(floats), (1, 2)).reshape(-1)
    vectors = jnp.concatenate([
        jnp.sum(first_grad, 0), jnp.sum(normed_grad * normal_one, 0), jnp.sum(normed_grad, 0), jnp.sum(second_grad, 0),
        jnp.sum(cot * normal_two, 0), jnp.sum(cot, 0), bias_q, bias_v, *hidden_bias_grads,
    ]).reshape(-1, model)
    partial = jnp.stack([jnp.stack(attn_grads), jnp.stack(hidden_grads), jnp.stack(down_grads)])
    input_grad, reduced, sums = reduce(sizes, own_share.reshape(micro, rows, model),
                                       spread.astype(halves).reshape(micro, cols, rows, model), partial, vectors)
    attn_block = reduced[0]
    piece = lambda i: attn_block[:, i * width : (i + 1) * width]
    mine = lambda vector, size: lax.dynamic_slice_in_dim(vector.reshape(-1), here * size, size, 0)
    return (
        outputs.reshape(micro, 1, rows, model), input_grad[:, None],
        piece(0), piece(1), piece(2), mine(sums[6], width), mine(sums[7], width), piece(3).T,
        sums[0], sums[1], sums[2], reduced[1], mine(sums[8:], hidden_bias.shape[0]), reduced[2].T,
        sums[3], sums[4], sums[5],
    )


def solution(mesh):
    sizes = tuple(mesh.shape[name] for name in ("seq", "row", "col"))
    block, line = P(("seq", "row"), "col"), P("col", ("seq", "row"))
    tokens = P(None, ("seq", "row"), "col", None)
    placed = (tokens, P(None, ("seq", "row"), None), block, block, block, P("col"), P("col"), line, P(), P(), P(),
              block, P("col"), line, P(), P(), P(), tokens)
    given = (tokens, tokens, block, block, block, P("col"), P("col"), line, P(), P(), P(), block, P("col"), line,
             P(), P(), P())
    return jax.shard_map(functools.partial(per_device, sizes), mesh=mesh, in_specs=placed, out_specs=given, check_vma=False)
```

time: 1140 us -> 551 us (0.48)
  waiting for transfers between devices: 663 us -> 0 us
  Pallas kernels: 0 us -> 326 us
  matrix products: 279 us -> 106 us
  blocking collectives: 93.9 us -> 14.8 us
  local copies, waits for them, and re-layouts: 23.1 us -> 67 us
  other arithmetic: 51 us -> 28.6 us
  between operations: 17.6 us -> 1.74 us
    pallas_call x0 -> x4, Pallas kernels: none -> 326 us  [the longest x1 158 us: gather(): pl.pallas_call(functools.partial(gather_kernel, sizes, micro), out_shape=...]
    reduce_scatter x10 -> x0, waiting for transfers between devices: 317 us -> none  [the longest x2 117 us: per_device(): lax.psum_scatter(contract_cols(pre_grad_low, hidden_full), 'col', scatter...]
    all_gather x10 -> x0, waiting for transfers between devices: 226 us -> none  [the longest x2 68.4 us: per_device(): lax.all_gather(normed.astype(halves), 'col', axis=0, tiled=True)]
    dot_general x40 -> x8, matrix products: 219 us -> 9.14 us  [the longest x4 5.72 us: per_device(): jnp.dot(ffn_grad, down_full[c], preferred_element_type=floats)]
    unnamed x28 -> x0, waiting for transfers between devices: 119 us -> none
    psum x2 -> x0, blocking collectives: 54.2 us -> none  [the longest x1 40.2 us: per_device(): lax.psum((bias_out, gain_one, shift_one, bias_down, gain_two, shift_two),...]
    dot_general x12 -> x24, matrix products: 33.6 us -> 59.7 us  [contract_cols(): lax.dot_general(left, right, (((1,), (1,)), ((), ())), preferred_element_...]
    slice x2 -> x10, local copies, waits for them, and re-layouts: 2.07 us -> 27.3 us  [the longest x1 8.59 us: per_device(): hidden_full[c]]
  transfers between devices with their start and end apart: 24 -> 0, of which waited for: 18 -> 0; matrix products, arithmetic and copies ran while one was open for 27% -> 0% of each run, Pallas kernels for 0% -> 0%
where the time goes in v1:
time: 551 us; the launch traced here: 544 us
  Pallas kernels  326 us (59%)
  matrix products  106 us (19%)
  local copies, waits for them, and re-layouts  67 us (12%)
  other arithmetic  28.6 us (5%)
  blocking collectives  14.8 us (3%)
    pallas_call x1, Pallas kernels, gather(): pl.pallas_call(functools.partial(gather_kernel, sizes, micro), out_shape=...  158 us
    pallas_call x1, Pallas kernels, reduce(): pl.pallas_call(functools.partial(reduce_kernel, sizes, micro), out_shape=...  115 us
    dot_general x24, matrix products, contract_cols(): lax.dot_general(left, right, (((1,), (1,)), ((), ())), preferred_element_...  59.7 us
    dot_general x24, matrix products, contract_rows(): lax.dot_general(left, right, (((0,), (0,)), ((), ())), preferred_element_...  37.5 us
    pallas_call x1, Pallas kernels, attend(): pl.pallas_call(attend_kernel, grid_spec=spec, out_shape=[shape(rows, widt...  27.6 us
    pallas_call x1, Pallas kernels, attend_back(): pl.pallas_call(attend_back_kernel, grid_spec=spec, out_shape=[shape(rows,...  24.9 us
    all_gather x1, blocking collectives, per_device(): lax.all_gather(jnp.concatenate([query_bias, value_bias, hidden_bias]), 'c...  14.8 us
    dot_general x6, local copies, waits for them, and re-layouts, contract_rows(): lax.dot_general(left, right, (((0,), (0,)), ((), ())), preferred_element_...  13.9 us

profile of v1, /device:TPU:0, one launch (start us, length us, event | category | flops | bytes accessed | tf_op | source)
XLA Modules:
  0.0 544.3 jit_solution(4453926593566792645)
XLA Ops:
  11.9 14.8 %all-gather.1 = bf16[4,1,1152]{2,1,0:T(2,128)(2,1)S(1)} all-gather(bf16[1,1,1152]{2,1,0:T(2,128)(2,1)S(1)} %reshape.625), channel_id=2, replica_groups=mesh['seq'=2,'row'=4,'col'=4] {'col'}, dimensions={0}, use_global_device_ids=true | all-gather | bytes 11520 | tf_op jit(solution)/shard_map/all_gather | solution.py:646
  30.6 157.9 %gather.1 = (bf16[2,4,256,768]{3,2,1,0:T(8,128)(2,1)}, bf16[3,4,2,2,2,96,768]{6,5,4,3,2,1,0:T(8,128)(2,1)}) custom-call(bf16[2,256,768]{2,1,0:T(8,128)(2,1)} %bitcast.312, bf16[3,96,768]{2,1,0:T(8,128)(2,1)} %pad_maximum_fusion.shard_ref), custom_call_target="tpu_custom_call" | custom-call | tf_op jit(solution)/shard_map/gather/pallas_call | solution.py:400
  188.6 4.8 copy.195
  193.3 2.7 slice.267
  196.1 8.6 %fusion.67 = (bf16[1,1,2,2,2,96,768]{6,5,4,3,2,1,0:T(8,128)(2,1)}, bf16[1,1,2,2,2,96,768]{6,5,4,3,2,1,0:T(8,128)(2,1)}, bf16[1,1,2,2,2,96,768]{6,5,4,3,2,1,0:T(8...) fusion(bf16[3,4,2,2,2,96,768]{6,5,4,3,2,1,0:T(8,128)(2,1)} %get, ...), kind=kLoop, calls=%fused_computation.211 | loop fusion | bytes 18874368 | tf_op jit(solution)/shard_map/slice | solution.py:672
  204.7 4.4 fusion.68
  210.8 2.6 copy.190.wvt_ref
  213.4 27.6 %attend.1 = (bf16[4,2,256,192]{3,2,1,0:T(8,128)(2,1)S(1)}, f32[4,2,8,256]{3,2,1,0:T(8,128)S(1)}, bf16[4,2,256,192]{3,2,1,0:T(8,128)(2,1)S(1)}, bf16[4,2,1024,192...) custom-call(s32[2,2]{1,0:T(2,128)S(1)} %pad_add_fusion.bounds, ...), custom_call_target="tpu_custom_call" | custom-call | tf_op jit(solution)/shard_map/attend/pallas_call | solution.py:126
  291.5 2.4 fusion.39
  298.3 24.9 %attend_back.1 = (bf16[4,2,256,192]{3,2,1,0:T(8,128)(2,1)S(1)}, bf16[4,2,1024,192]{3,2,1,0:T(8,128)(2,1)}, bf16[4,2,1024,192]{3,2,1,0:T(8,128)(2,1)}) custom-call(s32[2,2]{1,0:T(2,128)S(1)} %pad_add_fusion.bounds, bf16[2,256,768]{2,1,0:T(8,128)(2,1)S(1)} %bitcast.319, bf16[4,768,192]{2,1,0:T(8,128)(2,1)} %get-tuple-element.164.wot_ref, ...), custom_call_target="tpu_custom_call" | custom-call | tf_op jit(solution)/shard_map/attend_back/pallas_call | solution.py:208
  323.2 3.9 fusion.70
  328.2 2.9 convert_reduce_fusion
  331.3 3.9 fusion.69
  348.8 3.3 fusion.29
  361.6 10.9 %maximum_maximum_fusion.part_ref = bf16[3,4,2,2,2,96,768]{6,5,4,3,2,1,0:T(8,128)(2,1)} fusion(bf16[1,1,2,2,2,96,768]{6,5,4,3,2,1,0:T(8,128)(2,1)S(1)} %bitcast.396, bf16[1,1,2,2,2,96,768]{6,5,4,3,2,1,0:T(8,128)(2,1)S(1)} %bitcast.413, bf16[1,1,2,2,2,96,768]{6,5,4,3,2,1,0:T(8,128)(2,1)S(1)} %bitcast.414, bf16[1,1,2,2,2,96,768]{6,5,4,3,2,1,0:T(8,128)(2,1)S(1)} %bitcast.415, ...), kind=kLoop, calls=%fused_computation | loop fusion | flops 339738624 | bytes 28311552 | tf_op jit(solution)/shard_map/stack | solution.py:715
  377.0 3.6 fusion.49
  380.6 3.7 fusion.47
  384.3 3.7 fusion.45
  388.0 3.7 fusion.48
  391.7 3.7 fusion.46
  395.4 3.7 fusion.44
  399.1 3.7 fusion.50
  402.8 16.7 %add_convert_fusion = bf16[2048,768]{1,0:T(8,128)(2,1)} fusion(f32[2048,768]{1,0:T(8,128)} %fusion.44, f32[2048,768]{1,0:T(8,128)} %fusion.45, f32[2048,768]{1,0:T(8,128)} %fusion.46, f32[2048,768]{1,0:T(8,128)} %fusion.47, f32[2048,768]{1,0:T(8,128)} %fusion.48, f32[2048,768]{1,0:T(8,128)} %fusion.50, f32[2048,768]{1,0:T(8,128)} %fusion.49, ...), kind=kOutput, calls=%fused_computation.2 | convolution fusion | flops 616562688 | bytes 48365568 | tf_op jit(solution)/shard_map/dot_general | solution.py:25
  419.6 115.3 %reduce.29 = (f32[2,256,768]{2,1,0:T(8,128)}, f32[3,96,768]{2,1,0:T(8,128)}, f32[16,768]{1,0:T(8,128)}) custom-call(f32[2,256,768]{2,1,0:T(8,128)} %bitcast.360, bf16[2,4,256,768]{3,2,1,0:T(8,128)(2,1)} %bitcast.345, bf16[3,4,2,2,2,96,768]{6,5,4,3,2,1,0:T(8,128)(2,1)} %maximum_maximum_fusion.part_ref, f32[16,768]{1,0:T(8,128)} %pad.4.vec_ref), custom_call_target="tpu_custom_call" | custom-call | tf_op jit(solution)/shard_map/reduce/pallas_call | solution.py:601
  (254 shorter events, 109.0 us)
Async XLA Ops:
  0.7 28.6 %copy-start.51 = (bf16[768,96]{0,1:T(8,128)(2,1)S(1)}, bf16[768,96]{0,1:T(8,128)(2,1)}, u32[]{:S(2)}) copy-start(bf16[768,96]{0,1:T(8,128)(2,1)} %param.31) | copy-start | bytes 442372
  0.7 28.6 %copy-start.52 = (bf16[96,768]{1,0:T(8,128)(2,1)S(1)}, bf16[96,768]{1,0:T(8,128)(2,1)}, u32[]{:S(2)}) copy-start(bf16[96,768]{1,0:T(8,128)(2,1)} %param.29) | copy-start | bytes 442372
  196.1 8.6 %copy-start.5 = (bf16[1,4,2,2,2,96,768]{6,5,4,3,2,1,0:T(8,128)(2,1)}, bf16[1,4,2,2,2,96,768]{6,5,4,3,2,1,0:T(8,128)(2,1)S(1)}, u32[]{:S(2)}) copy-start(bf16[1,4,2,2,2,96,768]{6,5,4,3,2,1,0:T(8,128)(2,1)S(1)} %slice.267) | copy-start | bytes 14155780
  241.1 3.4 copy-start.20
  241.1 3.4 copy-start.22
  241.1 3.4 copy-start.24
  241.1 4.8 copy-start.26
  278.9 18.8 %copy-start.6 = (f32[512,768]{1,0:T(8,128)}, f32[512,768]{1,0:T(8,128)S(1)}, u32[]{:S(2)}) copy-start(f32[512,768]{1,0:T(8,128)S(1)} %get-tuple-element.155) | copy-start | bytes 4718596
  291.5 3.5 copy-start.23
  328.2 3.0 copy-start.59
  328.2 3.0 copy-start.58
  348.8 3.3 copy-start.12
  348.8 3.5 copy-start.19
  355.8 4.5 copy-start.50
  357.0 3.3 copy-start.46
  357.0 3.3 copy-start.47
  357.0 3.3 copy-start.48
  357.0 3.3 copy-start.49
  358.2 3.1 copy-start.39
  359.3 13.2 %slice-start = ((s8[4718592]{0:T(1024)(128)(4,1)}), s8[4194304]{0:T(1024)(128)(4,1)S(1)}, s32[]{:S(2)}) async-start(s8[4718592]{0:T(1024)(128)(4,1)} %bitcast.326), calls=%async_computation | async-start | bytes 8388608
  361.6 10.9 %slice-start.1 = ((s8[4718592]{0:T(1024)(128)(4,1)}), s8[524288]{0:T(1024)(128)(4,1)S(1)}, s32[]{:S(2)}) async-start(s8[4718592]{0:T(1024)(128)(4,1)} %bitcast.326), calls=%async_computation.1 | async-start | bytes 1048576
  361.6 10.9 %copy-start.28 = (bf16[1,2,256,192]{3,2,1,0:T(8,128)(2,1)S(1)}, bf16[1,2,256,192]{3,2,1,0:T(8,128)(2,1)}, u32[]{:S(2)}) copy-start(bf16[1,2,256,192]{3,2,1,0:T(8,128)(2,1)} %get-tuple-element.182) | copy-start | bytes 589828
  399.1 3.8 copy-start.18
  534.9 8.0 %copy-start.36 = (f32[2,256,768]{2,1,0:T(8,128)S(1)}, f32[2,256,768]{2,1,0:T(8,128)}, u32[]{:S(2)}) copy-start(f32[2,256,768]{2,1,0:T(8,128)} %get-tuple-element.42) | copy-start | bytes 4718596
  (38 other events, 64.2 us)

commit v2 on v1

--- a/solution.py
+++ b/solution.py
@@ -39,8 +39,8 @@
     )
 
 
-def attend_kernel(bounds, own_ref, all_ref, wq_ref, wk_ref, wkt_ref, wv_ref, wvt_ref, bq_ref, bv_ref, bvt_ref,
-                  segq_ref, segk_ref, mixed_ref, lse_ref, q_ref, k_ref, kt_ref, v_ref, bias, acc, top, total):
+def attend_kernel(bounds, own_ref, all_ref, wq_ref, wk_ref, wv_ref, bq_ref, bv_ref,
+                  segq_ref, segk_ref, mixed_ref, lse_ref, q_ref, k_ref, v_ref, bias, acc, top, total):
     micro = pl.program_id(0)
     low, high = bounds[micro, 0], bounds[micro, 1]
     floats, halves = jnp.float32, jnp.bfloat16
@@ -67,9 +67,9 @@
         x = all_ref[0, at, :]
         keys = jnp.dot(x, wk_ref[0], preferred_element_type=floats).astype(halves)
         k_ref[0, 0, at, :] = keys
-        kt_ref[0, 0, :, at] = contract_cols(wkt_ref[0], x).astype(halves)
-        v_ref[0, 0, at, :] = (jnp.dot(x, wv_ref[0], preferred_element_type=floats) + bv_ref[0]).astype(halves)
-        values_t = (contract_cols(wvt_ref[0], x) + bvt_ref[0]).astype(halves)
+        values = (jnp.dot(x, wv_ref[0], preferred_element_type=floats) + bv_ref[0]).astype(halves)
+        v_ref[0, 0, at, :] = values
+        values_t = values.T
         mask = bias[at, :]
         for h in range(heads):
             s = contract_cols(keys, query_heads[h]) + mask
@@ -99,7 +99,6 @@
     cols, _, width = wq.shape
     halves = jnp.bfloat16
     weight = pl.BlockSpec((1, model, width), lambda m, c, b: (c, 0, 0))
-    weight_t = pl.BlockSpec((1, width, model), lambda m, c, b: (c, 0, 0))
     per = lambda a, b_: pl.BlockSpec((1, 1, a, b_), lambda m, c, b: (c, m, 0, 0))
     spec = pltpu.PrefetchScalarGridSpec(
         num_scalar_prefetch=1,
@@ -107,14 +106,13 @@
         in_specs=[
             pl.BlockSpec((1, rows, model), lambda m, c, b: (m, 0, 0)),
             pl.BlockSpec((1, length, model), lambda m, c, b: (m, 0, 0)),
-            weight, weight, weight_t, weight, weight_t,
+            weight, weight, weight,
             pl.BlockSpec((1, 1, width), lambda m, c, b: (c, 0, 0)),
             pl.BlockSpec((1, 1, width), lambda m, c, b: (c, 0, 0)),
-            pl.BlockSpec((1, width, 1), lambda m, c, b: (c, 0, 0)),
             pl.BlockSpec((1, 1, rows), lambda m, c, b: (m, 0, 0)),
             pl.BlockSpec((1, length, 1), lambda m, c, b: (m, 0, 0)),
         ],
-        out_specs=[per(rows, width), per(8, rows), per(rows, width), per(length, width), per(width, length), per(length, width)],
+        out_specs=[per(rows, width), per(8, rows), per(rows, width), per(length, width), per(length, width)],
         scratch_shapes=[
             pltpu.VMEM((length, rows), jnp.float32),
             pltpu.VMEM((width, rows), jnp.float32),
@@ -126,14 +124,14 @@
     return pl.pallas_call(
         attend_kernel,
         grid_spec=spec,
-        out_shape=[shape(rows, width), shape(8, rows, jnp.float32), shape(rows, width), shape(length, width), shape(width, length), shape(length, width)],
+        out_shape=[shape(rows, width), shape(8, rows, jnp.float32), shape(rows, width), shape(length, width), shape(length, width)],
         compiler_params=pltpu.CompilerParams(vmem_limit_bytes=48 << 20),
         name="attend",
-    )(bounds, own, everything, wq, wk, wk.swapaxes(1, 2), wv, wv.swapaxes(1, 2), bq[:, None], bv[:, None], bv[:, :, None],
+    )(bounds, own, everything, wq, wk, wv, bq[:, None], bv[:, None],
       seg_own[:, None], seg_all[:, :, None])
 
 
-def attend_back_kernel(bounds, grad_ref, wot_ref, mixed_ref, lse_ref, q_ref, k_ref, kt_ref, v_ref, segq_ref, segk_ref,
+def attend_back_kernel(bounds, grad_ref, wot_ref, mixed_ref, lse_ref, q_ref, k_ref, v_ref, segq_ref, segk_ref,
                        dq_ref, dk_ref, dv_ref, bias, acc):
     micro = pl.program_id(0)
     low, high = bounds[micro, 0], bounds[micro, 1]
@@ -166,6 +164,7 @@
         at = pl.ds(pl.multiple_of(block * KEY_BLOCK, KEY_BLOCK), KEY_BLOCK)
         keys = k_ref[0, 0, at, :]
         values = v_ref[0, 0, at, :]
+        keys_t = keys.T
         mask = bias[at, :]
         key_grad = jnp.zeros((KEY_BLOCK, width), floats)
         value_grad = jnp.zeros((KEY_BLOCK, width), floats)
@@ -177,7 +176,7 @@
             value_grad = value_grad + jnp.dot(p.astype(halves), grad_heads[h], preferred_element_type=floats)
             key_grad = key_grad + jnp.dot(score_grad, query_heads[h], preferred_element_type=floats)
             part = pl.ds(h * HEAD_DIM, HEAD_DIM)
-            acc[part, :] += jnp.dot(kt_ref[0, 0, part, at], score_grad, preferred_element_type=floats)
+            acc[part, :] += jnp.dot(keys_t[h * HEAD_DIM : (h + 1) * HEAD_DIM], score_grad, preferred_element_type=floats)
         dk_ref[0, 0, at, :] = key_grad.astype(halves)
         dv_ref[0, 0, at, :] = value_grad.astype(halves)
         return carry
@@ -186,7 +185,7 @@
     dq_ref[0, 0] = (acc[...].T * HEAD_DIM ** -0.5).astype(halves)
 
 
-def attend_back(bounds, grad, wot, mixed, lse, q, k, kt, v, seg_own, seg_all):
+def attend_back(bounds, grad, wot, mixed, lse, q, k, v, seg_own, seg_all):
     micro, rows, model = grad.shape
     cols, _, length, width = k.shape
     halves = jnp.bfloat16
@@ -197,7 +196,7 @@
         in_specs=[
             pl.BlockSpec((1, rows, model), lambda m, c, b: (m, 0, 0)),
             pl.BlockSpec((1, model, width), lambda m, c, b: (c, 0, 0)),
-            per(rows, width), per(8, rows), per(rows, width), per(length, width), per(width, length), per(length, width),
+            per(rows, width), per(8, rows), per(rows, width), per(length, width), per(length, width),
             pl.BlockSpec((1, 1, rows), lambda m, c, b: (m, 0, 0)),
             pl.BlockSpec((1, length, 1), lambda m, c, b: (m, 0, 0)),
         ],
@@ -211,7 +210,7 @@
         out_shape=[shape(rows, width), shape(length, width), shape(length, width)],
         compiler_params=pltpu.CompilerParams(vmem_limit_bytes=48 << 20),
         name="attend_back",
-    )(bounds, grad, wot, mixed, lse, q, k, kt, v, seg_own[:, None], seg_all[:, :, None])
+    )(bounds, grad, wot, mixed, lse, q, k, v, seg_own[:, None], seg_all[:, :, None])
 
 
 def place(sizes):
@@ -357,22 +356,26 @@
         plane = full_ref.at[j, :, :, :, k]
         post.send(("k", j), "k", 1 - k, plane, plane)
 
-    start(zs + tokens)
+    start(zs[:1])
     finish(zs[:1])
-    start(second[0])
+    start(second[0] + zs[1:2])
+    finish(second[0])
+    start(third[0])
     finish(zs[1:2])
-    finish(second[0])
-    start(third[0] + second[1])
-    finish(zs[2:])
-    finish(tokens)
-    finish(second[1])
-    start(third[1] + second[2])
+    start(second[1] + tokens[:1])
     finish(third[0])
     swap(0)
+    finish(second[1])
+    start(third[1])
+    finish(tokens[:1])
+    start(zs[2:])
+    finish(zs[2:])
+    start(second[2] + tokens[1:])
+    finish(third[1])
+    swap(1)
     finish(second[2])
     start(third[2])
-    finish(third[1])
-    swap(1)
+    finish(tokens[1:])
     finish(third[2])
     swap(2)
     for i in range(cols):
@@ -403,7 +406,7 @@
             jax.ShapeDtypeStruct((micro, nc, rows, model), own.dtype),
             jax.ShapeDtypeStruct((3, nc, ns, ny, 2, rb, w), shard.dtype),
         ],
-        in_specs=[anywhere] * 2,
+        in_specs=[pl.BlockSpec(memory_space=pltpu.VMEM)] * 2,
         out_specs=[anywhere] * 2,
         scratch_shapes=[pltpu.SemaphoreType.DMA((count,)), pltpu.SemaphoreType.DMA((count,)), pltpu.SemaphoreType.DMA((3 + micro,))],
         compiler_params=pltpu.CompilerParams(collective_id=0, has_side_effects=True),
@@ -628,7 +631,223 @@
     return back, blocks, sums
 
 
-def per_device(sizes, inputs, segment_ids, query_weight, key_weight, value_weight, query_bias, value_bias,
+Q_AT, K_AT, V_AT, O_AT, WINDOW = 0, 128, 384, 512, 256
+
+
+def plane(full_ref, c, at, size=WINDOW):
+    value = full_ref[c, :, :, :, :, at : at + size]
+    return value.reshape(-1, size)
+
+
+def place_of(rows):
+    return lax.broadcasted_iota(jnp.int32, (rows, WINDOW), 1) // HEAD_DIM
+
+
+def keep(value, places, wanted):
+    return jnp.where(places == wanted, value, jnp.zeros_like(value))
+
+
+def forward_kernel(sizes, micro, own_ref, shard_ref, bias_ref, segq_ref, segk_ref,
+                   rest_ref, first_ref, every_ref, biases_ref, mixed_ref, lse_ref, q_ref, k_ref, v_ref,
+                   weights, tokens_buf, bias_buf, mask, mixed_buf, lse_buf, q_buf, k_buf, v_buf, acc, top, total,
+                   send_sems, recv_sems, local_sems):
+    floats, halves = jnp.float32, jnp.bfloat16
+    lines, device = place(sizes)
+    (x, _), (y, _), (k, _), (z, cols) = (lines[a] for a in "xykz")
+    half = shard_ref.shape[-1] // 2
+    rows = own_ref.shape[1]
+    reach = -(-(DOC_MOST - 1) // rows)
+    parts = [pl.ds(p * half, half) for p in (0, 1)]
+    low, high = jnp.maximum(z - reach, 0), jnp.minimum(z + reach + 1, cols)
+    used = [0]
+
+    def local(source, target):
+        copy = pltpu.make_async_copy(source, target, local_sems.at[used[0]])
+        used[0] += 1
+        copy.start()
+        return copy
+
+    targets = [weights.at[0], rest_ref.at[0], rest_ref.at[1]]
+    begin = [local(shard_ref.at[j], targets[j].at[z, x, y, k]) for j in range(3)]
+    begin += [local(own_ref.at[m], tokens_buf.at[m, z]) for m in range(micro)]
+    begin += [local(bias_ref, bias_buf.at[z])]
+    greet(lines, device)
+    post = Post(device, send_sems, recv_sems)
+    for copy in begin:
+        copy.wait()
+    zs = [LineGather(post, ("z", j), "z", lines["z"], lambda i, j=j: targets[j].at[i, x, y, k]) for j in range(3)]
+    tokens = [LineGather(post, ("t", m), "z", lines["z"], lambda i, m=m: tokens_buf.at[m, i], reach) for m in range(micro)]
+    small = LineGather(post, "bias", "z", lines["z"], lambda i: bias_buf.at[i])
+    second, third = {}, {}
+    for j in range(3):
+        second[j] = [
+            LineGather(post, ("a", j), "y", lines["y"], lambda i, j=j: targets[j].at[:, x, i, k, :, parts[0]]),
+            LineGather(post, ("b", j), "x", lines["x"], lambda i, j=j: targets[j].at[:, i, y, k, :, parts[1]]),
+        ]
+        third[j] = [
+            LineGather(post, ("c", j), "x", lines["x"], lambda i, j=j: targets[j].at[:, i, :, k, :, parts[0]]),
+            LineGather(post, ("d", j), "y", lines["y"], lambda i, j=j: targets[j].at[:, :, i, k, :, parts[1]]),
+        ]
+
+    def start(*group):
+        for line in group:
+            line.start()
+
+    def finish(*group):
+        for line in group:
+            line.finish()
+
+    def swap(j):
+        own_plane = targets[j].at[:, :, :, k]
+        post.send(("k", j), "k", 1 - k, own_plane, own_plane)
+
+    def swapped(j):
+        post.wait(("k", j), "k", 1 - k, targets[j].at[:, :, :, 1 - k])
+
+    places = place_of(rows)
+
+    def unit(m, c):
+        queries = jnp.dot(own_ref[m], plane(weights.at[0], c, Q_AT), preferred_element_type=floats) + bias_buf[c, 1:2, 0:WINDOW]
+        queries = pltpu.roll(queries.astype(halves).astype(floats) * HEAD_DIM ** -0.5, HEAD_DIM, 1)
+        queries = jnp.where(places > 0, queries, 0.0).astype(halves)
+        q_buf[m, c] = queries
+        heads = [keep(queries, places, h + 1) for h in range(3)]
+        acc[...] = jnp.zeros_like(acc)
+        total[...] = jnp.zeros_like(total)
+        top[...] = jnp.full_like(top, 2 * MASK_VALUE)
+        key_weight = plane(weights.at[0], c, K_AT)
+        value_weight = plane(weights.at[0], c, V_AT)
+        value_bias = bias_buf[c, 2:3, 0:WINDOW]
+
+        def step(block, carry):
+            rows_at = tokens_buf[m, block]
+            keys = jnp.dot(rows_at, key_weight, preferred_element_type=floats).astype(halves)
+            values = (jnp.dot(rows_at, value_weight, preferred_element_type=floats) + value_bias).astype(halves)
+            k_buf[m, c, block] = keys
+            v_buf[m, c, block] = values
+            values_t = values.T
+            hidden = mask[m, block]
+            for h in range(3):
+                s = contract_cols(keys, heads[h]) + hidden
+                old = top[h : h + 1]
+                new = jnp.maximum(old, jnp.max(s, 0, keepdims=True))
+                p = jnp.exp(s - new)
+                shrink = jnp.exp(old - new)
+                top[h : h + 1] = new
+                total[h : h + 1] = total[h : h + 1] * shrink + jnp.sum(p, 0, keepdims=True)
+                at = pl.ds((h + 1) * HEAD_DIM, HEAD_DIM)
+                acc[at, :] = acc[at, :] * shrink + jnp.dot(
+                    values_t[h * HEAD_DIM : (h + 1) * HEAD_DIM], p.astype(halves), preferred_element_type=floats
+                )
+            return carry
+
+        lax.fori_loop(low, high, step, 0)
+        for h in range(3):
+            at = pl.ds((h + 1) * HEAD_DIM, HEAD_DIM)
+            acc[at, :] = acc[at, :] / total[h : h + 1]
+        mixed_buf[c, m] = acc[...].T.astype(halves)
+        lse_buf[m, c] = top[...] + jnp.log(jnp.maximum(total[...], 1e-30))
+
+    def units(m, first, last):
+        @pl.loop(first, last)
+        def _(c):
+            unit(m, c)
+
+    def masks(m):
+        @pl.loop(low, high)
+        def _(block):
+            same = segk_ref[m, pl.ds(pl.multiple_of(block * rows, rows), rows), :] == segq_ref[m, 0:1]
+            mask[m, block] = jnp.where(same, 0.0, MASK_VALUE)
+
+    done = []
+    middle = max(cols // 2, 1)
+    start(small, zs[0])
+    finish(zs[0])
+    start(*second[0], tokens[0])
+    for m in range(micro):
+        masks(m)
+    finish(small, *second[0])
+    start(*third[0])
+    finish(tokens[0])
+    start(zs[1])
+    finish(*third[0])
+    swap(0)
+    finish(zs[1])
+    start(*second[1], zs[2])
+    swapped(0)
+    units(0, 0, middle)
+    finish(*second[1])
+    start(*third[1])
+    finish(zs[2])
+    for m in range(1, micro):
+        start(tokens[m])
+    done.append(local(weights.at[0], first_ref))
+    units(0, middle, cols)
+    finish(*tokens[1:])
+    finish(*third[1])
+    swap(1)
+    start(*second[2])
+    for m in range(1, micro):
+        units(m, 0, middle)
+        if m == 1:
+            finish(*second[2])
+            start(*third[2])
+        units(m, middle, cols)
+    for m in range(micro):
+        @pl.loop(low, high)
+        def _(block, m=m):
+            copy = pltpu.make_async_copy(tokens_buf.at[m, block], every_ref.at[m, block], local_sems.at[used[0] + m])
+            copy.start()
+            copy.wait()
+    used[0] += micro
+    for source, target in ((bias_buf, biases_ref), (mixed_buf, mixed_ref), (lse_buf, lse_ref), (q_buf, q_ref), (k_buf, k_ref), (v_buf, v_ref)):
+        done.append(local(source, target))
+    if micro == 1:
+        finish(*second[2])
+        start(*third[2])
+    finish(*third[2])
+    swap(2)
+    swapped(1)
+    swapped(2)
+    for copy in done:
+        copy.wait()
+    post.close()
+
+
+def forward(sizes, own, shard, bias, seg_own, seg_all):
+    ns, nr, nc = sizes
+    ny = nr // 2
+    micro, rows, model = own.shape
+    _, rb, w = shard.shape
+    halves, floats = own.dtype, jnp.float32
+    reach = min(nc - 1, -(-(DOC_MOST - 1) // rows))
+    count = (3 + 1) * 2 * (nc - 1) + micro * 2 * reach + 3 * (4 * (ny - 1) + 4 * (ns - 1) + 1)
+    anywhere = pl.BlockSpec(memory_space=pl.ANY)
+    vmem = pl.BlockSpec(memory_space=pltpu.VMEM)
+    length = nc * rows
+    arrays = [
+        ((2, nc, ns, ny, 2, rb, w), halves), ((nc, ns, ny, 2, rb, w), halves), ((micro, nc, rows, model), halves),
+        ((nc, *bias.shape), floats), ((nc, micro, rows, WINDOW), halves), ((micro, nc, 8, rows), floats),
+        ((micro, nc, rows, WINDOW), halves), ((micro, nc, nc, rows, WINDOW), halves), ((micro, nc, nc, rows, WINDOW), halves),
+    ]
+    shapes = [pltpu.VMEM(shape, kind) for shape, kind in arrays]
+    return pl.pallas_call(
+        functools.partial(forward_kernel, sizes, micro),
+        out_shape=[jax.ShapeDtypeStruct(shape, kind) for shape, kind in arrays],
+        in_specs=[vmem] * 5,
+        out_specs=[anywhere] * len(arrays),
+        scratch_shapes=[
+            pltpu.VMEM((1, nc, ns, ny, 2, rb, w), halves),
+            shapes[2], shapes[3], pltpu.VMEM((micro, nc, rows, rows), floats), *shapes[4:],
+            pltpu.VMEM((WINDOW, rows), floats), pltpu.VMEM((8, rows), floats), pltpu.VMEM((8, rows), floats),
+            pltpu.SemaphoreType.DMA((count,)), pltpu.SemaphoreType.DMA((count,)), pltpu.SemaphoreType.DMA((20,)),
+        ],
+        compiler_params=pltpu.CompilerParams(collective_id=2, has_side_effects=True, vmem_limit_bytes=60 << 20),
+        name="forward",
+    )(own, shard, bias, seg_own[:, None], seg_all[:, :, None])
+
+
+def per_device_plain(sizes, inputs, segment_ids, query_weight, key_weight, value_weight, query_bias, value_bias,
                output_weight, output_bias, first_gain, first_shift, hidden_weight, hidden_bias, down_weight,
                down_bias, second_gain, second_shift, cotangent):
     floats, halves = jnp.float32, jnp.bfloat16
@@ -656,7 +875,7 @@
     last_key = jnp.sum((seg_all <= seg_own[:, -1:]).astype(jnp.int32), 1)
     bounds = jnp.stack([first_key // KEY_BLOCK, (last_key + KEY_BLOCK - 1) // KEY_BLOCK], 1)
 
-    mixed, lse, q, k, kt, v = attend(bounds, own, everything, wq, wk, wv, bq.astype(floats), bv.astype(floats), seg_own, seg_all)
+    mixed, lse, q, k, v = attend(bounds, own, everything, wq, wk, wv, bq.astype(floats), bv.astype(floats), seg_own, seg_all)
     total = micro * rows
     flat = lambda a: a.reshape(total, -1)
     mixed_flat = mixed.reshape(cols, total, width)
@@ -693,7 +912,7 @@
         normed_grad = normed_grad + contract_cols(pre, hidden_full[c])
     first_grad = norm_back(normed_grad * gain_one, normal_one, scale_one)
     attn_grad = first_grad.astype(halves)
-    dq, dk, dv = attend_back(bounds, attn_grad.reshape(micro, rows, model), wot, mixed, lse, q, k, kt, v, seg_own, seg_all)
+    dq, dk, dv = attend_back(bounds, attn_grad.reshape(micro, rows, model), wot, mixed, lse, q, k, v, seg_own, seg_all)
     every_flat = everything.reshape(micro * length, model)
     attn_grads = []
     own_share = first_grad
@@ -726,6 +945,114 @@
     )
 
 
+def per_device_fused(sizes, inputs, segment_ids, query_weight, key_weight, value_weight, query_bias, value_bias,
+               output_weight, output_bias, first_gain, first_shift, hidden_weight, hidden_bias, down_weight,
+               down_bias, second_gain, second_shift, cotangent):
+    floats, halves = jnp.float32, jnp.bfloat16
+    cols = sizes[2]
+    micro, _, rows, model = inputs.shape
+    length = segment_ids.shape[-1]
+    width = query_weight.shape[1]
+    here = lax.axis_index("col")
+    own = inputs[:, 0]
+    shard = jnp.stack([
+        jnp.concatenate([query_weight, key_weight, value_weight, output_weight.T], 1),
+        hidden_weight,
+        down_weight.T,
+    ])
+    pad = lambda vector: jnp.pad(vector.astype(floats), (0, model - vector.shape[0]))
+    bias = jnp.stack([pad(hidden_bias), pad(query_bias), pad(value_bias)] + [jnp.zeros((model,), floats)] * 5)
+    seg_all = segment_ids[:, 0]
+    seg_own = lax.dynamic_slice_in_dim(seg_all, here * rows, rows, 1)
+    rest, first, everything, biases, mixed, lse, q, k, v = forward(sizes, own, shard, bias, seg_own, seg_all)
+    first = first.reshape(cols, model, 4 * width)
+    wq, wk, wv, wot = (first[:, :, i * width : (i + 1) * width] for i in range(4))
+    hidden_full, down_full = rest.reshape(2, cols, model, -1)
+    bh = biases[:, 0, : hidden_bias.shape[0]]
+    first_key = jnp.sum((seg_all < seg_own[:, :1]).astype(jnp.int32), 1)
+    last_key = jnp.sum((seg_all <= seg_own[:, -1:]).astype(jnp.int32), 1)
+    bounds = jnp.stack([first_key // KEY_BLOCK, (last_key + KEY_BLOCK - 1) // KEY_BLOCK], 1)
+    everything = everything.reshape(micro, length, model)
+    everything = jnp.where(jnp.isfinite(everything), everything, 0)
+    mixed = mixed[..., HEAD_DIM:]
+    lse = lse.swapaxes(0, 1)
+    q = q[..., HEAD_DIM:].swapaxes(0, 1)
+    k = k.reshape(micro, cols, length, -1)[..., HEAD_DIM:].swapaxes(0, 1)
+    v = v.reshape(micro, cols, length, -1)[..., :width].swapaxes(0, 1)
+    total = micro * rows
+    flat = lambda a: a.reshape(total, -1)
+    mixed_flat = mixed.reshape(cols, total, width)
+    attn = sum(contract_cols(mixed_flat[c], wot[c]) for c in range(cols))
+    first_sum = flat(own).astype(floats) + attn + output_bias.astype(floats)
+    normal_one, scale_one = norm_parts(first_sum)
+    gain_one = first_gain.astype(floats)
+    normed = normal_one * gain_one + first_shift.astype(floats)
+    normed_low = normed.astype(halves)
+    ffn = 0
+    activated, slopes = [], []
+    for c in range(cols):
+        hidden = jnp.dot(normed_low, hidden_full[c], preferred_element_type=floats) + bh[c].astype(floats)
+        half_erf = 0.5 * lax.erf(hidden * 0.7071067811865476) + 0.5
+        act = (hidden * half_erf).astype(halves)
+        slope = half_erf + hidden * (jnp.exp(-0.5 * hidden * hidden) * 0.3989422804014327)
+        activated.append(act)
+        slopes.append(slope.astype(halves))
+        ffn = ffn + contract_cols(act, down_full[c])
+    second_sum = normed + ffn + down_bias.astype(floats)
+    normal_two, scale_two = norm_parts(second_sum)
+    gain_two = second_gain.astype(floats)
+    outputs = (normal_two * gain_two + second_shift.astype(floats)).astype(halves)
+    cot = flat(cotangent[:, 0]).astype(floats)
+    second_grad = norm_back(cot * gain_two, normal_two, scale_two)
+    ffn_grad = second_grad.astype(halves)
+    hidden_grads, down_grads, hidden_bias_grads = [], [], []
+    normed_grad = second_grad
+    for c in range(cols):
+        pre = (jnp.dot(ffn_grad, down_full[c], preferred_element_type=floats) * slopes[c].astype(floats)).astype(halves)
+        hidden_grads.append(contract_rows(normed_low, pre).astype(halves))
+        down_grads.append(contract_rows(ffn_grad, activated[c]).astype(halves))
+        hidden_bias_grads.append(jnp.sum(pre.astype(floats), 0))
+        normed_grad = normed_grad + contract_cols(pre, hidden_full[c])
+    first_grad = norm_back(normed_grad * gain_one, normal_one, scale_one)
+    attn_grad = first_grad.astype(halves)
+    dq, dk, dv = attend_back(bounds, attn_grad.reshape(micro, rows, model), wot, mixed, lse, q, k, v, seg_own, seg_all)
+    every_flat = everything.reshape(micro * length, model)
+    attn_grads = []
+    own_share = first_grad
+    spread = 0
+    for c in range(cols):
+        dq_c, dk_c, dv_c = dq[c].reshape(total, width), dk[c].reshape(micro * length, width), dv[c].reshape(micro * length, width)
+        attn_grads.append(jnp.concatenate([
+            contract_rows(flat(own), dq_c), contract_rows(every_flat, dk_c), contract_rows(every_flat, dv_c),
+            contract_rows(attn_grad, mixed_flat[c]),
+        ], 1).astype(halves))
+        own_share = own_share + contract_cols(dq_c, wq[c])
+        spread = spread + contract_cols(dk_c, wk[c]) + contract_cols(dv_c, wv[c])
+    bias_q = jnp.sum(dq.astype(floats), (1, 2)).reshape(-1)
+    bias_v = jnp.sum(dv.astype(floats), (1, 2)).reshape(-1)
+    vectors = jnp.concatenate([
+        jnp.sum(first_grad, 0), jnp.sum(normed_grad * normal_one, 0), jnp.sum(normed_grad, 0), jnp.sum(second_grad, 0),
+        jnp.sum(cot * normal_two, 0), jnp.sum(cot, 0), bias_q, bias_v, *hidden_bias_grads,
+    ]).reshape(-1, model)
+    partial = jnp.stack([jnp.stack(attn_grads), jnp.stack(hidden_grads), jnp.stack(down_grads)])
+    input_grad, reduced, sums = reduce(sizes, own_share.reshape(micro, rows, model),
+                                       spread.astype(halves).reshape(micro, cols, rows, model), partial, vectors)
+    attn_block = reduced[0]
+    piece = lambda i: attn_block[:, i * width : (i + 1) * width]
+    mine = lambda vector, size: lax.dynamic_slice_in_dim(vector.reshape(-1), here * size, size, 0)
+    return (
+        outputs.reshape(micro, 1, rows, model), input_grad[:, None],
+        piece(0), piece(1), piece(2), mine(sums[6], width), mine(sums[7], width), piece(3).T,
+        sums[0], sums[1], sums[2], reduced[1], mine(sums[8:], hidden_bias.shape[0]), reduced[2].T,
+        sums[3], sums[4], sums[5],
+    )
+
+
+def per_device(sizes, inputs, segment_ids, query_weight, *rest):
+    fits = query_weight.shape == (query_weight.shape[0] // 16 * 16, 3 * HEAD_DIM)
+    return (per_device_fused if fits else per_device_plain)(sizes, inputs, segment_ids, query_weight, *rest)
+
+
 def solution(mesh):
     sizes = tuple(mesh.shape[name] for name in ("seq", "row", "col"))
     block, line = P(("seq", "row"), "col"), P("col", ("seq", "row"))

time: 551 us -> 456 us (0.83)
  Pallas kernels: 326 us -> 254 us
  blocking collectives: 14.8 us -> 0 us
    pallas_call x2 -> x1, Pallas kernels: 185 us -> 108 us  [forward(): pl.pallas_call(functools.partial(forward_kernel, sizes, micro), out_shape...]
    all_gather x1 -> x0, blocking collectives: 14.8 us -> none  [per_device(): lax.all_gather(jnp.concatenate([query_bias, value_bias, hidden_bias]), 'c...]
    slice x10 -> x11, local copies, waits for them, and re-layouts: 27.3 us -> 17 us  [the longest x1 3.99 us: per_device_fused(): dv[c].reshape(micro * length, width)]
    pallas_call x1, Pallas kernels: 24.9 us -> 32.9 us  [attend_back(): pl.pallas_call(attend_back_kernel, grid_spec=spec, out_shape=[shape(rows,...]
    another operation x4 -> x6, other arithmetic: 12.7 us -> 14.1 us  [the longest x1 10.9 us: per_device_fused(): jnp.stack([jnp.stack(attn_grads), jnp.stack(hidden_grads), jnp.stack(down...]
    unnamed x142 -> x128, local copies, waits for them, and re-layouts: 12.6 us -> 11.6 us
where the time goes in v2:
time: 456 us; the launch traced here: 450 us
  Pallas kernels  254 us (56%)
  matrix products  101 us (22%)
  local copies, waits for them, and re-layouts  61.5 us (13%)
  other arithmetic  31.8 us (7%)
    pallas_call x1, Pallas kernels, reduce(): pl.pallas_call(functools.partial(reduce_kernel, sizes, micro), out_shape=...  112 us
    pallas_call x1, Pallas kernels, forward(): pl.pallas_call(functools.partial(forward_kernel, sizes, micro), out_shape...  108 us
    dot_general x24, matrix products, contract_cols(): lax.dot_general(left, right, (((1,), (1,)), ((), ())), preferred_element_...  55.7 us
    dot_general x24, matrix products, contract_rows(): lax.dot_general(left, right, (((0,), (0,)), ((), ())), preferred_element_...  36.8 us
    pallas_call x1, Pallas kernels, attend_back(): pl.pallas_call(attend_back_kernel, grid_spec=spec, out_shape=[shape(rows,...  32.9 us
    dot_general x6, local copies, waits for them, and re-layouts, contract_rows(): lax.dot_general(left, right, (((0,), (0,)), ((), ())), preferred_element_...  12.9 us
    unnamed x128, local copies, waits for them, and re-layouts  11.6 us
    another operation x1, other arithmetic, per_device_fused(): jnp.stack([jnp.stack(attn_grads), jnp.stack(hidden_grads), jnp.stack(down...  10.9 us

profile of v2, /device:TPU:0, one launch (start us, length us, event | category | flops | bytes accessed | tf_op | source)
XLA Modules:
  0.0 449.8 jit_solution(6167407515989515473)
XLA Ops:
  15.9 108.4 %forward.1 = (bf16[2,4,2,2,2,96,768]{6,5,4,3,2,1,0:T(8,128)(2,1)}, bf16[4,2,2,2,96,768]{5,4,3,2,1,0:T(8,128)(2,1)}, bf16[2,4,256,768]{3,2,1,0:T(8,128)(2,1)}, f3...) custom-call(bf16[2,256,768]{2,1,0:T(8,128)(2,1)} %bitcast.315, ...), custom_call_target="tpu_custom_call" | custom-call | tf_op jit(solution)/shard_map/forward/pallas_call | solution.py:834
  135.9 2.4 is-finite_select_fusion
  138.3 4.7 %copy.124 = bf16[768,2048]{1,0:T(8,128)(2,1)} copy(bf16[768,2048]{0,1:T(8,128)(2,1)} %bitcast.346) | data formatting | bytes 6291456 | tf_op jit(solution)/shard_map/dot_general | solution.py:19
  143.0 2.6 copy.120
  146.9 5.2 %slice_bitcast_fusion = (bf16[4,2,1024,192]{3,2,1,0:T(8,128)(2,1)}, bf16[4,2,1024,192]{3,2,1,0:T(8,128)(2,1)}) fusion(bf16[2,4,1024,256]{3,2,0,1:T(8,128)(2,1)S(1)} %bitcast.326, bf16[2,4,1024,256]{3,2,0,1:T(8,128)(2,1)S(1)} %bitcast.325), kind=kLoop, calls=%fused_computation.4 | loop fusion | bytes 12582912 | tf_op jit(solution)/shard_map/transpose | solution.py:981
  192.6 2.1 fusion.39
  198.4 32.9 %attend_back.1 = (bf16[4,2,256,192]{3,2,1,0:T(8,128)(2,1)S(1)}, bf16[4,2,1024,192]{3,2,1,0:T(8,128)(2,1)}, bf16[4,2,1024,192]{3,2,1,0:T(8,128)(2,1)}) custom-call(s32[2,2]{1,0:T(2,128)S(1)} %pad_add_fusion.bounds, bf16[2,256,768]{2,1,0:T(8,128)(2,1)S(1)} %bitcast.313, bf16[4,768,192]{2,1,0:T(8,128)(2,1)} %slice.340.wot_ref, ...), custom_call_target="tpu_custom_call" | custom-call | tf_op jit(solution)/shard_map/attend_back/pallas_call | solution.py:207
  231.3 3.9 fusion.64
  236.4 2.9 convert_reduce_fusion
  239.4 4.0 fusion.63
  250.0 2.0 fusion.41
  253.9 2.0 fusion.40
  257.0 3.3 fusion.29
  269.8 10.9 %maximum_maximum_fusion.part_ref = bf16[3,4,2,2,2,96,768]{6,5,4,3,2,1,0:T(8,128)(2,1)} fusion(bf16[1,1,2,2,2,96,768]{6,5,4,3,2,1,0:T(8,128)(2,1)S(1)} %bitcast.400, bf16[1,1,2,2,2,96,768]{6,5,4,3,2,1,0:T(8,128)(2,1)S(1)} %bitcast.405, bf16[1,1,2,2,2,96,768]{6,5,4,3,2,1,0:T(8,128)(2,1)S(1)} %bitcast.406, bf16[1,1,2,2,2,96,768]{6,5,4,3,2,1,0:T(8,128)(2,1)S(1)} %bitcast.407, ...), kind=kLoop, calls=%fused_computation | loop fusion | flops 339738624 | bytes 28311552 | tf_op jit(solution)/shard_map/stack | solution.py:1037
  285.2 3.6 fusion.49
  288.9 3.7 fusion.47
  292.6 3.7 fusion.45
  296.2 3.7 fusion.48
  299.9 3.7 fusion.46
  303.7 3.7 fusion.44
  307.3 3.8 fusion.50
  311.1 16.7 %add_convert_fusion = bf16[2048,768]{1,0:T(8,128)(2,1)} fusion(f32[2048,768]{1,0:T(8,128)} %fusion.44, f32[2048,768]{1,0:T(8,128)} %fusion.45, f32[2048,768]{1,0:T(8,128)} %fusion.46, f32[2048,768]{1,0:T(8,128)} %fusion.47, f32[2048,768]{1,0:T(8,128)} %fusion.48, f32[2048,768]{1,0:T(8,128)} %fusion.50, f32[2048,768]{1,0:T(8,128)} %fusion.49, ...), kind=kOutput, calls=%fused_computation.3 | convolution fusion | flops 616562688 | bytes 48365568 | tf_op jit(solution)/shard_map/dot_general | solution.py:25
  327.8 112.4 %reduce.29 = (f32[2,256,768]{2,1,0:T(8,128)}, f32[3,96,768]{2,1,0:T(8,128)}, f32[16,768]{1,0:T(8,128)}) custom-call(f32[2,256,768]{2,1,0:T(8,128)} %bitcast.364, bf16[2,4,256,768]{3,2,1,0:T(8,128)(2,1)} %bitcast.347, bf16[3,4,2,2,2,96,768]{6,5,4,3,2,1,0:T(8,128)(2,1)} %maximum_maximum_fusion.part_ref, f32[16,768]{1,0:T(8,128)} %pad.15.vec_ref), custom_call_target="tpu_custom_call" | custom-call | tf_op jit(solution)/shard_map/reduce/pallas_call | solution.py:604
  444.7 2.0 slice_bitcast_fusion.35
  (245 shorter events, 103.4 us)
Async XLA Ops:
  0.7 13.1 %copy-start.45 = (bf16[768,96]{0,1:T(8,128)(2,1)S(1)}, bf16[768,96]{0,1:T(8,128)(2,1)}, u32[]{:S(2)}) copy-start(bf16[768,96]{0,1:T(8,128)(2,1)} %param.31) | copy-start | bytes 442372
  0.7 13.1 %copy-start.46 = (bf16[96,768]{1,0:T(8,128)(2,1)S(1)}, bf16[96,768]{1,0:T(8,128)(2,1)}, u32[]{:S(2)}) copy-start(bf16[96,768]{1,0:T(8,128)(2,1)} %param.29) | copy-start | bytes 442372
  1.4 14.5 %copy-start.1 = (s32[2,1,256]{2,1,0:T(1,128)}, s32[2,1,256]{2,1,0:T(1,128)S(1)}, u32[]{:S(2)}) copy-start(s32[2,1,256]{2,1,0:T(1,128)S(1)} %constant_dynamic-slice_fusion.2.segq_ref) | copy-start | bytes 6148
  124.3 4.2 copy-start.18
  143.0 3.4 copy-start.17
  146.5 5.6 %slice-start.2 = ((s8[9437184]{0:T(1024)(128)(4,1)}), s8[4194304]{0:T(1024)(128)(4,1)S(1)}, s32[]{:S(2)}) async-start(s8[9437184]{0:T(1024)(128)(4,1)} %bitcast.348), calls=%async_computation.2 | async-start | bytes 8388608
  146.9 5.2 %slice-start.3 = ((s8[9437184]{0:T(1024)(128)(4,1)}), s8[4194304]{0:T(1024)(128)(4,1)S(1)}, s32[]{:S(2)}) async-start(s8[9437184]{0:T(1024)(128)(4,1)} %bitcast.348), calls=%async_computation.3 | async-start | bytes 8388608
  146.9 6.0 %slice-start.4 = ((s8[9437184]{0:T(1024)(128)(4,1)}), s8[1048576]{0:T(1024)(128)(4,1)S(1)}, s32[]{:S(2)}) async-start(s8[9437184]{0:T(1024)(128)(4,1)} %bitcast.348), calls=%async_computation.4 | async-start | bytes 2097152
  180.9 9.4 %copy-start.7 = (f32[512,768]{1,0:T(8,128)}, f32[512,768]{1,0:T(8,128)S(1)}, u32[]{:S(2)}) copy-start(f32[512,768]{1,0:T(8,128)S(1)} %get-tuple-element.123) | copy-start | bytes 4718596
  239.4 4.7 %copy-start.6 = (bf16[2,1,256,768]{3,2,1,0:T(8,128)(2,1)S(1)}, bf16[2,1,256,768]{3,2,1,0:T(8,128)(2,1)}, u32[]{:S(2)}) copy-start(bf16[2,1,256,768]{3,2,1,0:T(8,128)(2,1)} %param.18) | copy-start | bytes 2359300
  239.4 4.6 %copy-start.26 = (bf16[1,2,256,192]{3,2,1,0:T(8,128)(2,1)S(1)}, bf16[1,2,256,192]{3,2,1,0:T(8,128)(2,1)}, u32[]{:S(2)}) copy-start(bf16[1,2,256,192]{3,2,1,0:T(8,128)(2,1)} %get-tuple-element.142) | copy-start | bytes 589828
  257.0 3.3 copy-start.14
  257.0 3.5 copy-start.21
  263.9 4.5 %copy-start.44 = (bf16[768,768]{1,0:T(8,128)(2,1)S(1)}, bf16[768,768]{1,0:T(8,128)(2,1)}, u32[]{:S(2)}) copy-start(bf16[768,768]{1,0:T(8,128)(2,1)} %convolution_convert_fusion.3) | copy-start | bytes 3538948
  265.2 3.3 copy-start.40
  265.2 3.3 copy-start.41
  265.2 3.3 copy-start.42
  265.2 3.3 copy-start.43
  266.4 3.1 copy-start.39
  267.5 13.2 %slice-start = ((s8[4718592]{0:T(1024)(128)(4,1)}), s8[4194304]{0:T(1024)(128)(4,1)S(1)}, s32[]{:S(2)}) async-start(s8[4718592]{0:T(1024)(128)(4,1)} %bitcast.333), calls=%async_computation | async-start | bytes 8388608
  269.8 10.9 %slice-start.1 = ((s8[4718592]{0:T(1024)(128)(4,1)}), s8[524288]{0:T(1024)(128)(4,1)S(1)}, s32[]{:S(2)}) async-start(s8[4718592]{0:T(1024)(128)(4,1)} %bitcast.333), calls=%async_computation.1 | async-start | bytes 1048576
  269.8 11.0 %copy-start.28 = (bf16[1,2,256,192]{3,2,1,0:T(8,128)(2,1)S(1)}, bf16[1,2,256,192]{3,2,1,0:T(8,128)(2,1)}, u32[]{:S(2)}) copy-start(bf16[1,2,256,192]{3,2,1,0:T(8,128)(2,1)} %get-tuple-element.144) | copy-start | bytes 589828
  307.3 3.8 copy-start.20
  440.2 8.0 %copy-start.36 = (f32[2,256,768]{2,1,0:T(8,128)S(1)}, f32[2,256,768]{2,1,0:T(8,128)}, u32[]{:S(2)}) copy-start(f32[2,256,768]{2,1,0:T(8,128)} %get-tuple-element.44) | copy-start | bytes 4718596
  (32 other events, 54.8 us)

commit v3 on v2

--- a/solution.py
+++ b/solution.py
@@ -756,7 +756,7 @@
     def masks(m):
         @pl.loop(low, high)
         def _(block):
-            same = segk_ref[m, pl.ds(pl.multiple_of(block * rows, rows), rows), :] == segq_ref[m, 0:1]
+            same = jnp.broadcast_to(segk_ref[m, pl.ds(block, 1), :], (rows, rows)).T == segq_ref[m, 0:1]
             mask[m, block] = jnp.where(same, 0.0, MASK_VALUE)
 
     done = []
@@ -844,7 +844,506 @@
         ],
         compiler_params=pltpu.CompilerParams(collective_id=2, has_side_effects=True, vmem_limit_bytes=60 << 20),
         name="forward",
-    )(own, shard, bias, seg_own[:, None], seg_all[:, :, None])
+    )(own, shard, bias, seg_own.astype(floats)[:, None], seg_all.astype(floats).reshape(micro, nc, rows))
+
+
+def middle_kernel(cols, own_ref, mixed_ref, out_ref, hidden_ref, down_ref, bias_ref, vector_ref, cot_ref,
+                  outputs_ref, first_grad_ref, attn_grad_ref, part_ref, sums_ref,
+                  normal, scale, normed, normed_low, normed_t, grad_low, grad_t, act_buf, slope_buf, total):
+    floats, halves = jnp.float32, jnp.bfloat16
+    step = pl.program_id(0)
+    rows, model = own_ref.shape
+    chunks = [pl.ds(r * 256, 256) for r in range(rows // 256)]
+    bands = [pl.ds(n * 256, 256) for n in range(model // 256)]
+    vector = lambda i: vector_ref[i : i + 1]
+
+    @pl.when(step == 0)
+    def _():
+        sums_ref[...] = jnp.zeros_like(sums_ref)
+        for chunk in chunks:
+            first_sum = own_ref[chunk].astype(floats) + vector(0)
+            for c in range(cols):
+                first_sum = first_sum + contract_cols(mixed_ref[c, chunk], out_ref[c])
+            normal_one, scale_one = norm_parts(first_sum)
+            normal[chunk] = normal_one
+            scale[chunk] = jnp.broadcast_to(scale_one, (256, 128))
+            norm_one = normal_one * vector(1) + vector(2)
+            total[chunk] = norm_one + vector(3)
+            normed_low[chunk] = norm_one.astype(halves)
+            normed_t[:, chunk] = norm_one.astype(halves).T
+
+    @pl.when(step < cols)
+    def _():
+        for chunk in chunks:
+            for band in bands:
+                hidden = jnp.dot(normed_low[chunk], hidden_ref[0, 0, :, band], preferred_element_type=floats) + bias_ref[0, 0:1, band]
+                half_erf = 0.5 * lax.erf(hidden * 0.7071067811865476) + 0.5
+                act_buf[step, chunk, band] = (hidden * half_erf).astype(halves)
+                slope_buf[step, chunk, band] = (half_erf + hidden * (jnp.exp(-0.5 * hidden * hidden) * 0.3989422804014327)).astype(halves)
+        for chunk in chunks:
+            for band in bands:
+                total[chunk, band] += contract_cols(act_buf[step, chunk], down_ref[0, 0, band, :])
+
+    @pl.when(step == cols - 1)
+    def _():
+        for chunk in chunks:
+            normal_two, scale_two = norm_parts(total[chunk])
+            outputs_ref[chunk] = (normal_two * vector(4) + vector(5)).astype(halves)
+            cot = cot_ref[chunk].astype(floats)
+            second_grad = norm_back(cot * vector(4), normal_two, scale_two)
+            total[chunk] = second_grad
+            grad_low[chunk] = second_grad.astype(halves)
+            grad_t[:, chunk] = second_grad.astype(halves).T
+            sums_ref[3:4] += jnp.sum(second_grad, 0, keepdims=True)
+            sums_ref[4:5] += jnp.sum(cot * normal_two, 0, keepdims=True)
+            sums_ref[5:6] += jnp.sum(cot, 0, keepdims=True)
+
+    @pl.when(step >= cols)
+    def _():
+        c = step - cols
+        bias_total = [jnp.zeros((1, 256), floats) for _ in bands]
+        for chunk in chunks:
+            for n, band in enumerate(bands):
+                pre = jnp.dot(grad_low[chunk], down_ref[0, 0, :, band], preferred_element_type=floats)
+                pre = (pre * slope_buf[c, chunk, band].astype(floats)).astype(halves)
+                slope_buf[c, chunk, band] = pre
+                bias_total[n] = bias_total[n] + jnp.sum(pre.astype(floats), 0, keepdims=True)
+        for n, band in enumerate(bands):
+            sums_ref[pl.ds(8 + c, 1), band] = bias_total[n]
+        for band in bands:
+            for side in bands:
+                part_ref[0, 0, side, band] = jnp.dot(normed_t[side, :], slope_buf[c, :, band], preferred_element_type=floats).astype(halves)
+                part_ref[1, 0, side, band] = jnp.dot(grad_t[side, :], act_buf[c, :, band], preferred_element_type=floats).astype(halves)
+        for chunk in chunks:
+            for band in bands:
+                total[chunk, band] += contract_cols(slope_buf[c, chunk], hidden_ref[0, 0, band, :])
+
+    @pl.when(step == 2 * cols - 1)
+    def _():
+        for chunk in chunks:
+            normed_grad, normal_one = total[chunk], normal[chunk]
+            first_grad = norm_back(normed_grad * vector(1), normal_one, scale[chunk, 0:1])
+            first_grad_ref[chunk] = first_grad
+            attn_grad_ref[chunk] = first_grad.astype(halves)
+            sums_ref[0:1] += jnp.sum(first_grad, 0, keepdims=True)
+            sums_ref[1:2] += jnp.sum(normed_grad * normal_one, 0, keepdims=True)
+            sums_ref[2:3] += jnp.sum(normed_grad, 0, keepdims=True)
+
+
+def middle(own, mixed, first, rest, biases, vectors, cot):
+    rows, model = own.shape
+    cols = first.shape[0]
+    halves, floats = jnp.bfloat16, jnp.float32
+    whole = lambda shape: pl.BlockSpec(shape, lambda i: (0,) * len(shape))
+    wide = lambda kind: pltpu.VMEM((rows, model), kind)
+    return pl.pallas_call(
+        functools.partial(middle_kernel, cols),
+        grid=(2 * cols,),
+        in_specs=[
+            whole((rows, model)), whole(mixed.shape),
+            pl.BlockSpec((cols, model, WINDOW), lambda i: (0, 0, O_AT // WINDOW)),
+            pl.BlockSpec((1, 1, model, rest.shape[-1]), lambda i: (0, lax.rem(i, cols), 0, 0)),
+            pl.BlockSpec((1, 1, model, rest.shape[-1]), lambda i: (1, lax.rem(i, cols), 0, 0)),
+            pl.BlockSpec((1, *biases.shape[1:]), lambda i: (lax.rem(i, cols), 0, 0)),
+            whole(vectors.shape), whole((rows, model)),
+        ],
+        out_specs=[
+            whole((rows, model)), whole((rows, model)), whole((rows, model)),
+            pl.BlockSpec((2, 1, model, rest.shape[-1]), lambda i: (0, jnp.maximum(i - cols, 0), 0, 0)),
+            whole((8 + cols + -cols % 8, model)),
+        ],
+        out_shape=[
+            jax.ShapeDtypeStruct((rows, model), halves), jax.ShapeDtypeStruct((rows, model), floats),
+            jax.ShapeDtypeStruct((rows, model), halves), jax.ShapeDtypeStruct(rest.shape, halves),
+            jax.ShapeDtypeStruct((8 + cols + -cols % 8, model), floats),
+        ],
+        scratch_shapes=[
+            wide(floats), pltpu.VMEM((rows, 128), floats), wide(floats), wide(halves), pltpu.VMEM((model, rows), halves), wide(halves),
+            pltpu.VMEM((model, rows), halves), pltpu.VMEM((cols, rows, rest.shape[-1]), halves),
+            pltpu.VMEM((cols, rows, rest.shape[-1]), halves), wide(floats),
+        ],
+        compiler_params=pltpu.CompilerParams(vmem_limit_bytes=56 << 20),
+        name="middle",
+    )(own, mixed, first, rest, rest, biases, vectors, cot)
+
+
+class Inbox:
+    def __init__(self, ref, size):
+        self.ref, self.size = ref, size
+
+    def __call__(self, way, e):
+        return self.ref.at[0 if self.size == 2 else (1 - way) // 2, e]
+
+
+def backward_kernel(sizes, micro, grad_ref, share_ref, first_ref, every_ref, mixed_ref, lse_ref, q_ref, k_ref, v_ref,
+                    segq_ref, segk_ref, part_ref, vec_ref,
+                    back_ref, block_ref, sums_ref,
+                    mine_buf, core_buf, stage_buf, in_a, in_b, in_c, in_d, in_z, tok_buf, tok_in, vec_buf,
+                    weights, mixed_buf, q_buf, k_buf, v_buf, every_t, grad_t, x_buf, mask, acc, spread, block_sum,
+                    send_sems, recv_sems, local_sems):
+    floats, halves = jnp.float32, jnp.bfloat16
+    lines, device = place(sizes)
+    (x, ns), (y, ny), (k, _), (z, cols) = (lines[a] for a in "xykz")
+    model = first_ref.shape[1]
+    half = part_ref.shape[-1] // 2
+    rb = part_ref.shape[-2]
+    rows = grad_ref.shape[1]
+    reach = -(-(DOC_MOST - 1) // rows)
+    parts = [pl.ds(p * half, half) for p in (0, 1)]
+    low, high = jnp.maximum(z - reach, 0), jnp.minimum(z + reach + 1, cols)
+    used = [0]
+
+    def local(source, target):
+        copy = pltpu.make_async_copy(source, target, local_sems.at[used[0]])
+        used[0] += 1
+        copy.start()
+        return copy
+
+    loads = [local(*pair) for pair in ((first_ref, weights), (mixed_ref, mixed_buf), (q_ref, q_buf))]
+    loads += [local(k_ref.at[0], k_buf.at[0]), local(v_ref.at[0], v_buf.at[0])]
+    loads += [local(share_ref, back_ref)]
+    planes = [local(part_ref.at[j, :, :, :, k], mine_buf.at[j + 1]) for j in range(2)]
+    more = [[local(k_ref.at[m], k_buf.at[m]), local(v_ref.at[m], v_buf.at[m])] for m in range(1, micro)]
+    greet(lines, device)
+    post = Post(device, send_sems, recv_sems)
+    for j in range(2):
+        post.send(("k", j + 1), "k", 1 - k, part_ref.at[j, :, :, :, 1 - k], core_buf.at[j + 1])
+
+    def plus(target, source):
+        target[...] = (target[...].astype(floats) + source[...].astype(floats)).astype(halves)
+
+    def plus_grid(target, source, first, second):
+        @pl.loop(0, first * second)
+        def _(n):
+            at = (n // second, lax.rem(n, second))
+            plus(target.at[at], source.at[at])
+
+    def plus_row(target, source, first):
+        @pl.loop(0, first)
+        def _(n):
+            plus(target.at[n], source.at[n])
+
+    class Stream:
+        def __init__(self, name, j, begin, size):
+            cs = pl.ds(begin, size)
+            self.j, self.begin, self.size = j, begin, size
+            self.second = [
+                LineReduce(post, (name, "a"), "x", lines["x"], lambda i: mine_buf.at[j, cs, i, :, :, parts[0]],
+                           lambda way, e: Inbox(in_a.at[j], ns)(way, e).at[cs], lambda t, s: plus_grid(t, s, size, ny)),
+                LineReduce(post, (name, "b"), "y", lines["y"], lambda i: mine_buf.at[j, cs, :, i, :, parts[1]],
+                           lambda way, e: Inbox(in_b.at[j], ny)(way, e).at[cs], lambda t, s: plus_grid(t, s, size, ns)),
+            ]
+            self.third = [
+                LineReduce(post, (name, "c"), "y", lines["y"], lambda i: mine_buf.at[j, cs, x, i, :, parts[0]],
+                           lambda way, e: Inbox(in_c.at[j], ny)(way, e).at[cs], lambda t, s: plus_row(t, s, size)),
+                LineReduce(post, (name, "d"), "x", lines["x"], lambda i: mine_buf.at[j, cs, i, y, :, parts[1]],
+                           lambda way, e: Inbox(in_d.at[j], ns)(way, e).at[cs], lambda t, s: plus_row(t, s, size)),
+            ]
+
+    ffn = [None] + [Stream(("s", j), j, 0, cols) for j in (1, 2)]
+    cut = max(cols // 2, 1)
+    attn = [Stream(("s", 0, begin), 0, begin, min(cut, cols - begin)) for begin in range(0, cols, cut)]
+    last = [
+        LineReduce(post, ("z", j), "z", lines["z"], lambda i, j=j: mine_buf.at[j, i, x, y],
+                   lambda way, e, j=j: in_z.at[j, (1 - way) // 2, e], plus)
+        for j in range(3)
+    ]
+
+    def plus_back(m):
+        def add(target, source):
+            back_ref[m] += source[...].astype(floats)
+
+        return add
+
+    tokens = [
+        LineReduce(post, ("t", m), "z", lines["z"], lambda i, m=m: tok_buf.at[m, i],
+                   lambda way, e, m=m: tok_in.at[m, (1 - way) // 2, e], plus, reach)
+        for m in range(micro)
+    ]
+
+    def start(*group):
+        for line in group:
+            line.start()
+
+    def finish(*group):
+        for line in group:
+            line.finish()
+
+    def tokens_finish(m):
+        tokens[m].finish(last=False)
+        tokens[m].add = plus_back(m)
+        for way in (1, -1):
+            if tokens[m].reach >= 1:
+                tokens[m].take(way, 0)
+
+    def core(j):
+        planes[j - 1].wait()
+        post.wait(("k", j), "k", 1 - k, core_buf.at[j])
+
+        @pl.loop(0, cols * ns * ny)
+        def _(n):
+            at = (n // (ns * ny), lax.rem(n // ny, ns), lax.rem(n, ny))
+            plus(mine_buf.at[(j, *at)], core_buf.at[(j, *at)])
+
+    def vector_start(stage, axis):
+        mine, size = lines[axis]
+        vec_buf[stage, 1 + mine] = vec_buf[stage, 0]
+        for t in range(1, size):
+            post.send(("v", stage, t), axis, lax.rem(mine + t, size), vec_buf.at[stage, 0], vec_buf.at[stage, 1 + mine])
+
+    def vector_finish(stage, axis, out):
+        mine, size = lines[axis]
+        for t in range(1, size):
+            origin = lax.rem(mine + size - t, size)
+            post.wait(("v", stage, t), axis, origin, vec_buf.at[stage, 1 + origin])
+        total = vec_buf[stage, 1]
+        for i in range(1, size):
+            total = total + vec_buf[stage, 1 + i]
+        out[...] = total
+
+    places = place_of(rows)
+    small = vec_ref.shape[0]
+    vec_buf[0, 0] = jnp.zeros_like(vec_buf[0, 0])
+    vec_buf[0, 0, 0:small] = vec_ref[...]
+
+    def masks(m):
+        @pl.loop(low, high)
+        def _(block):
+            same = jnp.broadcast_to(segk_ref[m, pl.ds(block, 1), :], (rows, rows)).T == segq_ref[m, 0:1]
+            mask[block] = jnp.where(same, 0.0, MASK_VALUE)
+
+    def turn(m):
+        for block in range(cols):
+            inside = (low <= block) & (block < high)
+            at = pl.ds((m * cols + block) * rows, rows)
+
+            @pl.when(inside)
+            def _():
+                copy = pltpu.make_async_copy(every_ref.at[m, block], x_buf, local_sems.at[used[0] + m])
+                copy.start()
+                copy.wait()
+                every_t[:, at] = x_buf[...].T
+
+            if block > reach or cols - 1 - block > reach:
+                @pl.when(jnp.logical_not(inside))
+                def _():
+                    every_t[:, at] = jnp.zeros((model, rows), halves)
+
+                    @pl.loop(0, cols)
+                    def _(c):
+                        k_buf[m, c, block] = jnp.zeros((rows, WINDOW), halves)
+                        v_buf[m, c, block] = jnp.zeros((rows, WINDOW), halves)
+
+    def unit(m, c):
+        mixed_grad = jnp.dot(grad_ref[m], weights[c, :, O_AT : O_AT + WINDOW], preferred_element_type=floats).astype(halves)
+        mixed_grad = jnp.where(places > 0, mixed_grad.astype(floats), 0.0)
+        product = mixed_grad * mixed_buf[c, m].astype(floats)
+        product_high = product.astype(halves)
+        product_low = (product - product_high.astype(floats)).astype(halves)
+        pick = (
+            lax.broadcasted_iota(jnp.int32, (8, WINDOW), 1) // HEAD_DIM == lax.broadcasted_iota(jnp.int32, (8, WINDOW), 0) + 1
+        ).astype(floats).astype(halves)
+        inner = contract_cols(pick, product_high) + contract_cols(pick, product_low)
+        value_side = pltpu.roll(mixed_grad, WINDOW - HEAD_DIM, 1).astype(halves)
+        queries = q_buf[m, c]
+        query_heads = [keep(queries, places, h + 1) for h in range(3)]
+        grad_heads = [keep(value_side, places, h) for h in range(3)]
+        acc[...] = jnp.zeros_like(acc)
+        key_weight = weights[c, :, K_AT : K_AT + WINDOW]
+        value_weight = weights[c, :, V_AT : V_AT + WINDOW]
+
+        def step(block, value_bias):
+            keys = k_buf[m, c, block]
+            values = v_buf[m, c, block]
+            keys_t = keys.T
+            hidden = mask[block]
+            key_grad = jnp.zeros((rows, WINDOW), floats)
+            value_grad = jnp.zeros((rows, WINDOW), floats)
+            for h in range(3):
+                p = jnp.exp(contract_cols(keys, query_heads[h]) + hidden - lse_ref[m, c, h : h + 1])
+                prob_grad = contract_cols(values, grad_heads[h])
+                score_grad = (p * (prob_grad - inner[h : h + 1])).astype(halves)
+                value_grad = value_grad + jnp.dot(p.astype(halves), grad_heads[h], preferred_element_type=floats)
+                key_grad = key_grad + jnp.dot(score_grad, query_heads[h], preferred_element_type=floats)
+                at = pl.ds(h * HEAD_DIM, HEAD_DIM)
+                acc[at, :] += jnp.dot(keys_t[(h + 1) * HEAD_DIM : (h + 2) * HEAD_DIM], score_grad, preferred_element_type=floats)
+            key_low, value_low = key_grad.astype(halves), value_grad.astype(halves)
+            k_buf[m, c, block] = key_low
+            v_buf[m, c, block] = value_low
+            spread[block] += contract_cols(key_low, key_weight) + contract_cols(value_low, value_weight)
+            return value_bias + jnp.sum(value_low.astype(floats), 0, keepdims=True)
+
+        value_bias = lax.fori_loop(low, high, step, jnp.zeros((1, WINDOW), floats))
+        query_low = (acc[...].T * HEAD_DIM ** -0.5).astype(halves)
+        q_buf[m, c] = query_low
+        vec_buf[0, 0, pl.ds(small + c, 1), 0:WINDOW] += jnp.sum(query_low.astype(floats), 0, keepdims=True)
+        vec_buf[0, 0, pl.ds(small + c, 1), WINDOW : 2 * WINDOW] += value_bias
+        back_ref[m] += contract_cols(query_low, weights[c, :, Q_AT : Q_AT + WINDOW])
+
+    def units(m, first, last_):
+        @pl.loop(first, last_)
+        def _(c):
+            unit(m, c)
+
+    def send_tokens(m):
+        back_ref[m] += spread[z]
+
+        @pl.loop(low, high)
+        def _(block):
+            tok_buf[m, block] = spread[block].astype(halves)
+
+        start(tokens[m])
+
+    def weight_grads(c):
+        for begin in range(0, model, 256):
+            side = pl.ds(begin, 256)
+            block_sum[side] = jnp.zeros((256, 4 * (WINDOW - HEAD_DIM)), floats)
+            out = 0
+            for m in range(micro):
+                mine_at = pl.ds(pl.multiple_of((m * cols + z) * rows, rows), rows)
+                block_sum[side, Q_AT : Q_AT + WINDOW] += jnp.dot(every_t[side, mine_at], q_buf[m, c], preferred_element_type=floats)
+                all_at = pl.ds(m * cols * rows, cols * rows)
+                block_sum[side, K_AT : K_AT + WINDOW] += jnp.dot(
+                    every_t[side, all_at], k_buf[m, c].reshape(-1, WINDOW), preferred_element_type=floats)
+                block_sum[side, V_AT : V_AT + WINDOW] += jnp.dot(
+                    every_t[side, all_at], v_buf[m, c].reshape(-1, WINDOW), preferred_element_type=floats)
+                block_sum[side, O_AT : O_AT + WINDOW] += jnp.dot(
+                    grad_t[side, m * rows : (m + 1) * rows], mixed_buf[c, m], preferred_element_type=floats)
+        for i in range(ns * ny):
+            ours = pl.ds(pl.multiple_of((2 * i + k) * rb, 16), rb)
+            theirs = pl.ds(pl.multiple_of((2 * i + 1 - k) * rb, 16), rb)
+            mine_buf[0, c, i // ny, i % ny] = block_sum[ours].astype(halves)
+            stage_buf[c, i // ny, i % ny] = block_sum[theirs].astype(halves)
+
+    def attn_core(stream):
+        cs = pl.ds(stream.begin, stream.size)
+
+        @pl.loop(stream.begin, stream.begin + stream.size)
+        def _(c):
+            weight_grads(c)
+
+        post.send(("k", 0, stream.begin), "k", 1 - k, stage_buf.at[cs], core_buf.at[0, cs])
+
+    def attn_add(stream):
+        cs = pl.ds(stream.begin, stream.size)
+        post.wait(("k", 0, stream.begin), "k", 1 - k, core_buf.at[0, cs])
+
+        @pl.loop(0, stream.size * ns * ny)
+        def _(n):
+            at = (stream.begin + n // (ns * ny), lax.rem(n // ny, ns), lax.rem(n, ny))
+            plus(mine_buf.at[(0, *at)], core_buf.at[(0, *at)])
+
+    for copy in loads:
+        copy.wait()
+    masks(0)
+    spread[...] = jnp.zeros_like(spread)
+    units(0, 0, 1)
+    core(1)
+    start(*ffn[1].second)
+    for m in range(micro):
+        for copy in more[m - 1] if m else ():
+            copy.wait()
+        turn(m)
+        grad_t[:, m * rows : (m + 1) * rows] = grad_ref[m].T
+    core(2)
+    start(*ffn[2].second)
+    units(0, 1, 3)
+    finish(*ffn[1].second)
+    start(*ffn[1].third)
+    units(0, 3, cols)
+    send_tokens(0)
+    for m in range(1, micro):
+        masks(m)
+        spread[...] = jnp.zeros_like(spread)
+        units(m, 0, 1)
+        if m == 1:
+            finish(*ffn[2].second)
+            start(*ffn[2].third)
+            finish(*ffn[1].third)
+            start(last[1])
+        units(m, 1, 2)
+        if m == 1:
+            tokens_finish(0)
+        units(m, 2, 3)
+        if m == 1:
+            finish(*ffn[2].third)
+            start(last[2])
+        units(m, 3, cols)
+        send_tokens(m)
+    vector_start(0, "k")
+    attn_core(attn[0])
+    vector_finish(0, "k", vec_buf.at[1, 0])
+    vector_start(1, "y")
+    for stream in attn[1:]:
+        attn_core(stream)
+    attn_add(attn[0])
+    start(*attn[0].second)
+    vector_finish(1, "y", vec_buf.at[2, 0])
+    vector_start(2, "x")
+    finish(last[1])
+    for stream in attn[1:]:
+        attn_add(stream)
+        start(*stream.second)
+    vector_finish(2, "x", vec_buf.at[3, 0])
+    vector_start(3, "z")
+    for m in range(1, micro):
+        tokens_finish(m)
+    finish(last[2])
+    for stream in attn:
+        finish(*stream.second)
+        start(*stream.third)
+    vector_finish(3, "z", sums_ref)
+    for stream in attn:
+        finish(*stream.third)
+    start(last[0])
+    for j in (1, 2):
+        block_ref[j] = mine_buf[j, z, x, y].astype(floats)
+    finish(last[0])
+    block_ref[0] = mine_buf[0, z, x, y].astype(floats)
+    post.close()
+
+
+def backward(sizes, grad, share, first, every, mixed, lse, q, k, v, seg_own, seg_all, part, vectors):
+    ns, nr, nc = sizes
+    ny = nr // 2
+    micro, rows, model = grad.shape
+    w = part.shape[-1]
+    rb = model // (ns * nr)
+    halves, floats = jnp.bfloat16, jnp.float32
+    reach = min(nc - 1, -(-(DOC_MOST - 1) // rows))
+    streams = 2 + -(-nc // max(nc // 2, 1))
+    count = 2 + nc + 4 * (ny - 1 + ns - 1) * streams + 3 * 2 * (nc - 1) + micro * 2 * reach + (1 + ny - 1 + ns - 1 + nc - 1)
+    widest = max(ns, ny, nc, 2)
+    ways = lambda n: 1 if n == 2 else 2
+    vec_shape = (vectors.shape[0] + nc + -nc % 8, model)
+    vmem = pl.BlockSpec(memory_space=pltpu.VMEM)
+    anywhere = pl.BlockSpec(memory_space=pl.ANY)
+    buf = lambda *shape, kind=halves: pltpu.VMEM(shape, kind)
+    return pl.pallas_call(
+        functools.partial(backward_kernel, sizes, micro),
+        out_shape=[
+            jax.ShapeDtypeStruct((micro, rows, model), floats),
+            jax.ShapeDtypeStruct((3, rb, w), floats),
+            jax.ShapeDtypeStruct(vec_shape, floats),
+        ],
+        in_specs=[vmem, anywhere, anywhere, anywhere, anywhere, vmem, anywhere, anywhere, anywhere, vmem, vmem, anywhere, vmem],
+        out_specs=[vmem] * 3,
+        scratch_shapes=[
+            buf(3, nc, ns, ny, rb, w), buf(3, nc, ns, ny, rb, w), buf(nc, ns, ny, rb, w),
+            buf(3, ways(ns), max(ns - 1, 1), nc, ny, rb, w // 2), buf(3, ways(ny), max(ny - 1, 1), nc, ns, rb, w // 2),
+            buf(3, ways(ny), max(ny - 1, 1), nc, rb, w // 2), buf(3, ways(ns), max(ns - 1, 1), nc, rb, w // 2),
+            buf(3, 2, max(nc - 1, 1), rb, w), buf(micro, nc, rows, model), buf(micro, 2, max(reach, 1), rows, model),
+            buf(4, 1 + widest, *vec_shape, kind=floats),
+            buf(nc, model, w), buf(nc, micro, rows, WINDOW), buf(micro, nc, rows, WINDOW),
+            buf(micro, nc, nc, rows, WINDOW), buf(micro, nc, nc, rows, WINDOW),
+            buf(model, micro * nc * rows), buf(model, micro * rows), buf(rows, model),
+            buf(nc, rows, rows, kind=floats), buf(WINDOW, rows, kind=floats), buf(nc, rows, model, kind=floats), buf(model, w, kind=floats),
+            pltpu.SemaphoreType.DMA((count,)), pltpu.SemaphoreType.DMA((count,)), pltpu.SemaphoreType.DMA((24,)),
+        ],
+        compiler_params=pltpu.CompilerParams(collective_id=3, has_side_effects=True, vmem_limit_bytes=62 << 20),
+        name="backward",
+    )(grad, share, first, every, mixed, lse, q, k, v, seg_own.astype(floats)[:, None], seg_all.astype(floats).reshape(micro, nc, rows),
+      part.reshape(2, nc, ns, ny, 2, rb, w), vectors)
 
 
 def per_device_plain(sizes, inputs, segment_ids, query_weight, key_weight, value_weight, query_bias, value_bias,
@@ -966,84 +1465,22 @@
     seg_own = lax.dynamic_slice_in_dim(seg_all, here * rows, rows, 1)
     rest, first, everything, biases, mixed, lse, q, k, v = forward(sizes, own, shard, bias, seg_own, seg_all)
     first = first.reshape(cols, model, 4 * width)
-    wq, wk, wv, wot = (first[:, :, i * width : (i + 1) * width] for i in range(4))
-    hidden_full, down_full = rest.reshape(2, cols, model, -1)
-    bh = biases[:, 0, : hidden_bias.shape[0]]
-    first_key = jnp.sum((seg_all < seg_own[:, :1]).astype(jnp.int32), 1)
-    last_key = jnp.sum((seg_all <= seg_own[:, -1:]).astype(jnp.int32), 1)
-    bounds = jnp.stack([first_key // KEY_BLOCK, (last_key + KEY_BLOCK - 1) // KEY_BLOCK], 1)
-    everything = everything.reshape(micro, length, model)
-    everything = jnp.where(jnp.isfinite(everything), everything, 0)
-    mixed = mixed[..., HEAD_DIM:]
-    lse = lse.swapaxes(0, 1)
-    q = q[..., HEAD_DIM:].swapaxes(0, 1)
-    k = k.reshape(micro, cols, length, -1)[..., HEAD_DIM:].swapaxes(0, 1)
-    v = v.reshape(micro, cols, length, -1)[..., :width].swapaxes(0, 1)
     total = micro * rows
     flat = lambda a: a.reshape(total, -1)
-    mixed_flat = mixed.reshape(cols, total, width)
-    attn = sum(contract_cols(mixed_flat[c], wot[c]) for c in range(cols))
-    first_sum = flat(own).astype(floats) + attn + output_bias.astype(floats)
-    normal_one, scale_one = norm_parts(first_sum)
-    gain_one = first_gain.astype(floats)
-    normed = normal_one * gain_one + first_shift.astype(floats)
-    normed_low = normed.astype(halves)
-    ffn = 0
-    activated, slopes = [], []
-    for c in range(cols):
-        hidden = jnp.dot(normed_low, hidden_full[c], preferred_element_type=floats) + bh[c].astype(floats)
-        half_erf = 0.5 * lax.erf(hidden * 0.7071067811865476) + 0.5
-        act = (hidden * half_erf).astype(halves)
-        slope = half_erf + hidden * (jnp.exp(-0.5 * hidden * hidden) * 0.3989422804014327)
-        activated.append(act)
-        slopes.append(slope.astype(halves))
-        ffn = ffn + contract_cols(act, down_full[c])
-    second_sum = normed + ffn + down_bias.astype(floats)
-    normal_two, scale_two = norm_parts(second_sum)
-    gain_two = second_gain.astype(floats)
-    outputs = (normal_two * gain_two + second_shift.astype(floats)).astype(halves)
-    cot = flat(cotangent[:, 0]).astype(floats)
-    second_grad = norm_back(cot * gain_two, normal_two, scale_two)
-    ffn_grad = second_grad.astype(halves)
-    hidden_grads, down_grads, hidden_bias_grads = [], [], []
-    normed_grad = second_grad
-    for c in range(cols):
-        pre = (jnp.dot(ffn_grad, down_full[c], preferred_element_type=floats) * slopes[c].astype(floats)).astype(halves)
-        hidden_grads.append(contract_rows(normed_low, pre).astype(halves))
-        down_grads.append(contract_rows(ffn_grad, activated[c]).astype(halves))
-        hidden_bias_grads.append(jnp.sum(pre.astype(floats), 0))
-        normed_grad = normed_grad + contract_cols(pre, hidden_full[c])
-    first_grad = norm_back(normed_grad * gain_one, normal_one, scale_one)
-    attn_grad = first_grad.astype(halves)
-    dq, dk, dv = attend_back(bounds, attn_grad.reshape(micro, rows, model), wot, mixed, lse, q, k, v, seg_own, seg_all)
-    every_flat = everything.reshape(micro * length, model)
-    attn_grads = []
-    own_share = first_grad
-    spread = 0
-    for c in range(cols):
-        dq_c, dk_c, dv_c = dq[c].reshape(total, width), dk[c].reshape(micro * length, width), dv[c].reshape(micro * length, width)
-        attn_grads.append(jnp.concatenate([
-            contract_rows(flat(own), dq_c), contract_rows(every_flat, dk_c), contract_rows(every_flat, dv_c),
-            contract_rows(attn_grad, mixed_flat[c]),
-        ], 1).astype(halves))
-        own_share = own_share + contract_cols(dq_c, wq[c])
-        spread = spread + contract_cols(dk_c, wk[c]) + contract_cols(dv_c, wv[c])
-    bias_q = jnp.sum(dq.astype(floats), (1, 2)).reshape(-1)
-    bias_v = jnp.sum(dv.astype(floats), (1, 2)).reshape(-1)
-    vectors = jnp.concatenate([
-        jnp.sum(first_grad, 0), jnp.sum(normed_grad * normal_one, 0), jnp.sum(normed_grad, 0), jnp.sum(second_grad, 0),
-        jnp.sum(cot * normal_two, 0), jnp.sum(cot, 0), bias_q, bias_v, *hidden_bias_grads,
-    ]).reshape(-1, model)
-    partial = jnp.stack([jnp.stack(attn_grads), jnp.stack(hidden_grads), jnp.stack(down_grads)])
-    input_grad, reduced, sums = reduce(sizes, own_share.reshape(micro, rows, model),
-                                       spread.astype(halves).reshape(micro, cols, rows, model), partial, vectors)
-    attn_block = reduced[0]
-    piece = lambda i: attn_block[:, i * width : (i + 1) * width]
-    mine = lambda vector, size: lax.dynamic_slice_in_dim(vector.reshape(-1), here * size, size, 0)
+    vectors = jnp.stack([a.astype(floats) for a in (output_bias, first_gain, first_shift, down_bias, second_gain, second_shift)]
+                        + [jnp.zeros((model,), floats)] * 2)
+    outputs, first_grad, attn_grad, part, sums = middle(
+        flat(own), mixed.reshape(cols, total, WINDOW), first, rest.reshape(2, cols, model, -1), biases, vectors, flat(cotangent[:, 0]))
+    parted = lambda a: a.reshape(micro, rows, model)
+    input_grad, reduced, sums = backward(sizes, parted(attn_grad), parted(first_grad), first, everything, mixed, lse, q, k, v,
+                                         seg_own, seg_all, part, sums)
+    piece = lambda i: reduced[0, :, i * width : (i + 1) * width]
+    mine = lambda first_row, at, size: lax.dynamic_slice(sums, (first_row + here, at), (1, size))[0]
+    heads_at = sums.shape[0] - (cols + -cols % 8)
     return (
         outputs.reshape(micro, 1, rows, model), input_grad[:, None],
-        piece(0), piece(1), piece(2), mine(sums[6], width), mine(sums[7], width), piece(3).T,
-        sums[0], sums[1], sums[2], reduced[1], mine(sums[8:], hidden_bias.shape[0]), reduced[2].T,
+        piece(0), piece(1), piece(2), mine(heads_at, 0, width), mine(heads_at, WINDOW, width), piece(3).T,
+        sums[0], sums[1], sums[2], reduced[1], mine(8, 0, hidden_bias.shape[0]), reduced[2].T,
         sums[3], sums[4], sums[5],
     )
 

time: 456 us -> 315 us (0.69); the launches traced: 450 us -> 314 us
  matrix products: 101 us -> 0 us
  local copies, waits for them, and re-layouts: 61.5 us -> 17.6 us
  Pallas kernels: 254 us -> 290 us
  other arithmetic: 31.8 us -> 6.06 us
    dot_general x56 -> x0, matrix products: 101 us -> none  [the longest x24 55.7 us: contract_cols(): lax.dot_general(left, right, (((1,), (1,)), ((), ())), preferred_element_...]
    pallas_call x2, Pallas kernels: 145 us -> 182 us  [the longest x1 154 us: backward(): pl.pallas_call(functools.partial(backward_kernel, sizes, micro), out_shap...]
    slice x10 -> x0, local copies, waits for them, and re-layouts: 15.3 us -> none  [the longest x1 3.99 us: per_device_fused(): dv[c].reshape(micro * length, width)]
    dot_general x6 -> x0, local copies, waits for them, and re-layouts: 12.9 us -> none  [contract_rows(): lax.dot_general(left, right, (((0,), (0,)), ((), ())), preferred_element_...]
    another operation x2 -> x0, other arithmetic: 11 us -> none  [the longest x1 10.9 us: per_device_fused(): jnp.stack([jnp.stack(attn_grads), jnp.stack(hidden_grads), jnp.stack(down...]
    reduce_sum x9 -> x0, other arithmetic: 8.91 us -> none  [the longest x1 2.89 us: per_device_fused(): bias_v = jnp.sum(dv.astype(floats), (1, 2)).reshape(-1)]
    unnamed x128 -> x3, local copies, waits for them, and re-layouts: 11.6 us -> 4.28 us
    transpose x2 -> x0, local copies, waits for them, and re-layouts: 6.99 us -> none  [the longest x1 5.18 us: per_device_fused(): v = v.reshape(micro, cols, length, -1)[..., :width].swapaxes(0, 1)]
where the time goes in v3:
time: 315 us; the launch traced here: 314 us
  Pallas kernels  290 us (92%)
  local copies, waits for them, and re-layouts  17.6 us (6%)
  other arithmetic  6.06 us (2%)
    pallas_call x1, Pallas kernels, backward(): pl.pallas_call(functools.partial(backward_kernel, sizes, micro), out_shap...  154 us
    pallas_call x1, Pallas kernels, forward(): pl.pallas_call(functools.partial(forward_kernel, sizes, micro), out_shape...  108 us
    pallas_call x1, Pallas kernels, middle(): pl.pallas_call(functools.partial(middle_kernel, cols), grid=(2 * cols,),...  28 us

profile of v3, /device:TPU:0, one launch (start us, length us, event | category | flops | bytes accessed | tf_op | source)
XLA Modules:
  0.0 314.4 jit_solution(1531049708690962577)
XLA Ops:
  0.7 1.3 dynamic-slice_convert_fusion.segq_ref
  1.9 0.7 convert_reduce_fusion
  3.3 0.9 copy.35
  4.2 1.0 maximum_bitcast_fusion
  5.1 1.8 pad_maximum_fusion.shard_ref
  6.9 0.7 pad_convert_fusion.1
  7.6 0.7 pad_convert_fusion
  8.2 0.7 reshape.67
  9.6 107.9 %forward.1 = (bf16[2,4,2,2,2,96,768]{6,5,4,3,2,1,0:T(8,128)(2,1)}, bf16[4,2,2,2,96,768]{5,4,3,2,1,0:T(8,128)(2,1)}, bf16[2,4,256,768]{3,2,1,0:T(8,128)(2,1)}, f3...) custom-call(bf16[2,256,768]{2,1,0:T(8,128)(2,1)} %bitcast.46, ...), custom_call_target="tpu_custom_call" | custom-call | tf_op jit(solution)/shard_map/forward/pallas_call | solution.py:834
  117.5 0.7 reshape.70
  118.1 0.7 reshape.71
  118.8 0.7 reshape.72
  119.5 0.7 reshape.73
  120.2 0.7 reshape.74
  120.9 0.7 reshape.75
  121.6 0.6 stack.103.vector_ref
  122.2 28.0 %middle.1 = (bf16[512,768]{1,0:T(8,128)(2,1)}, f32[512,768]{1,0:T(8,128)}, bf16[512,768]{1,0:T(8,128)(2,1)}, bf16[2,4,768,768]{3,2,1,0:T(8,128)(2,1)}, f32[16,768]{1,0:T(8,128)}) custom-call(bf16[512,768]{1,0:T(8,128)(2,1)} %bitcast.47, bf16[4,512,256]{2,1,0:T(8,128)(2,1)} %bitcast.45, bf16[4,768,768]{2,1,0:T(8,128)(2,1)} %bitcast.42, ...), custom_call_target="tpu_custom_call" | custom-call | tf_op jit(solution)/shard_map/middle/pallas_call | solution.py:939
  150.2 154.2 %backward.1 = (f32[2,256,768]{2,1,0:T(8,128)}, f32[3,96,768]{2,1,0:T(8,128)}, f32[24,768]{1,0:T(8,128)}) custom-call(bf16[2,256,768]{2,1,0:T(8,128)(2,1)} %bitcast.51, f32[2,256,768]{2,1,0:T(8,128)} %bitcast.48, bf16[4,768,768]{2,1,0:T(8,128)(2,1)} %bitcast.43, bf16[2,4,256,768]{3,2,1,0:T(8,128)(2,1)} %get-tuple-element.41.every_ref, ...), custom_call_target="tpu_custom_call" | custom-call | tf_op jit(solution)/shard_map/backward/pallas_call | solution.py:1322
  304.4 1.9 slice_bitcast_fusion
  306.3 1.8 slice_bitcast_fusion.2
  308.1 0.7 copy.38
  308.8 1.6 slice_reduce_fusion
  310.5 1.3 constant_dynamic-slice_fusion.1
  311.8 2.7 copy.40
  (7 shorter events, 1.3 us)

commit v4 on v3

--- a/solution.py
+++ b/solution.py
@@ -38,7 +38,25 @@
         pull - jnp.mean(pull, -1, keepdims=True) - normal * jnp.mean(pull * normal, -1, keepdims=True)
     )
 
-
+FORWARD_PLAN = (
+    ("Zs", 1), ("Zs", 0), ("Zs", 3), ("Z", 1, 1), ("Z", 0, 1), ("Zs", 2), ("Z", 1, 2), ("Zs", 4), ("Z", 1, 3),
+    ("Z", 0, 2), ("Z", 0, 3), ("Z", 2, 1), ("Z", 4, 1), ("Ts", 1), ("Z", 2, 2), ("B", 1), ("Z", 3, 1), ("Ts", 0),
+    ("Z", 4, 2), ("B", 0), ("T", 1, 1), ("T", 0, 1), ("Z", 2, 3), ("Z", 3, 2), ("Ts", 3), ("C", 1), ("C", 0),
+    ("Ts", 2), ("Z", 4, 3), ("K", 0), ("B", 2), ("T", 1, 2), ("T", 0, 2), ("R", 0), ("Zs", 5), ("K", 1), ("Z", 3, 3),
+    ("B", 4), ("U", 0, 0), ("T", 3, 1), ("U", 0, 1), ("B", 3), ("U", 0, 2), ("T", 2, 1), ("C", 2), ("T", 3, 2),
+    ("Z", 5, 1), ("C", 4), ("U", 0, 3), ("T", 2, 2), ("R", 1), ("C", 3), ("Z", 5, 2), ("K", 2), ("Z", 5, 3),
+    ("U", 1, 0), ("K", 3), ("K", 4), ("B", 5), ("U", 1, 1), ("U", 1, 2), ("C", 5), ("U", 1, 3), ("K", 5),
+)
+BACKWARD_PLAN = (
+    ("G", 3), ("G", 0), ("L",), ("U", 0, 0), ("A", 0), ("A", 3), ("U", 0, 1), ("U", 1, 0), ("B", 0), ("U", 1, 1),
+    ("B", 3), ("C", 0), ("U", 2, 0), ("C", 3), ("Z", 0, 2), ("G", 1), ("U", 3, 0), ("Z", 3, 2), ("S", 0), ("A", 1),
+    ("G", 2), ("U", 2, 1), ("A", 2), ("T", 0, 0, 1), ("W", 0), ("B", 1), ("T", 0, 1, 1), ("G", 4), ("U", 3, 1),
+    ("Z", 0, 1), ("V", 0), ("A", 4), ("S", 1), ("V", 1), ("B", 2), ("W", 1), ("G", 5), ("B", 4), ("W", 2), ("V", 2),
+    ("G", 6), ("T", 1, 0, 1), ("A", 5), ("W", 3), ("A", 6), ("G", 7), ("C", 2), ("C", 1), ("V", 3), ("Z", 2, 2),
+    ("A", 7), ("Z", 3, 1), ("B", 5), ("Z", 1, 2), ("Z", 2, 1), ("B", 6), ("T", 1, 1, 1), ("B", 7), ("T", 0, 0, 0),
+    ("Z", 3, 0), ("C", 4), ("C", 5), ("T", 0, 1, 0), ("Z", 2, 0), ("Z", 0, 0), ("C", 6), ("C", 7), ("Ys",), ("V", 4),
+    ("Y", 2), ("Z", 1, 1), ("T", 1, 0, 0), ("Y", 1), ("T", 1, 1, 0), ("Z", 1, 0), ("Y", 0),
+)
 def attend_kernel(bounds, own_ref, all_ref, wq_ref, wk_ref, wv_ref, bq_ref, bv_ref,
                   segq_ref, segk_ref, mixed_ref, lse_ref, q_ref, k_ref, v_ref, bias, acc, top, total):
     micro = pl.program_id(0)
@@ -254,34 +272,33 @@
             device_id=self.device(axis, index), device_id_type=MESH,
         )
 
-    def send(self, key, axis, index, source, target, when=None):
+    def send(self, key, make):
+        def run(act):
+            axis, index, source, target, when = make()
+
+            def go():
+                act(self.copy(key, axis, index, source, target))
+
+            if when is None:
+                go()
+            else:
+                pl.when(when)(go)
+
+        run(lambda copy: copy.start())
+        self.sent.append(run)
+
+    def wait(self, key, axis, index, target, when=None):
         def go():
-            self.copy(key, axis, index, source, target).start()
+            self.copy(key, axis, index, target, target).wait_recv()
 
         if when is None:
             go()
         else:
             pl.when(when)(go)
-        self.sent.append((key, axis, index, source, target, when))
-
-    def wait(self, key, axis, index, target, when=None):
-        def go():
-            self.copy(key, axis, index, target, target).wait_recv()
-
-        if when is None:
-            go()
-        else:
-            pl.when(when)(go)
 
     def close(self):
-        for key, axis, index, source, target, when in self.sent:
-            def go():
-                self.copy(key, axis, index, source, target).wait_send()
-
-            if when is None:
-                go()
-            else:
-                pl.when(when)(go)
+        for run in self.sent:
+            run(lambda copy: copy.wait_send())
 
 
 def clip(index, size):
@@ -296,24 +313,33 @@
 
     def hop(self, way, t):
         mine, size = self.mine, self.size
-        origin, target = mine - way * t, mine + way
-        ok = (origin >= 0) & (origin < size) & (target >= 0) & (target < size)
-        here = self.region(clip(origin, size))
-        self.post.send((self.name, way, t + 1), self.axis, clip(target, size), here, here, ok)
+
+        def make():
+            origin, target = mine - way * t, mine + way
+            ok = (origin >= 0) & (origin < size) & (target >= 0) & (target < size)
+            here = self.region(clip(origin, size))
+            return self.axis, clip(target, size), here, here, ok
+
+        self.post.send((self.name, way, t + 1), make)
 
     def start(self):
         for way in (1, -1):
             if self.reach >= 1:
                 self.hop(way, 0)
 
-    def finish(self):
-        for t in range(1, self.reach + 1):
-            for way in (1, -1):
-                origin = self.mine - way * t
-                ok = (origin >= 0) & (origin < self.size)
-                self.post.wait((self.name, way, t), self.axis, clip(self.mine - way, self.size), self.region(clip(origin, self.size)), ok)
-                if t < self.reach:
-                    self.hop(way, t)
+    def step(self, t):
+        if t > self.reach:
+            return
+        for way in (1, -1):
+            origin = self.mine - way * t
+            ok = (origin >= 0) & (origin < self.size)
+            self.post.wait((self.name, way, t), self.axis, clip(self.mine - way, self.size), self.region(clip(origin, self.size)), ok)
+            if t < self.reach:
+                self.hop(way, t)
+
+    def finish(self, first=1):
+        for t in range(first, self.reach + 1):
+            self.step(t)
 
 
 def gather_kernel(sizes, micro, own_ref, shard_ref, every_ref, full_ref, send_sems, recv_sems, local_sems):
@@ -354,7 +380,7 @@
 
     def swap(j):
         plane = full_ref.at[j, :, :, :, k]
-        post.send(("k", j), "k", 1 - k, plane, plane)
+        post.send(("k", j), lambda: ("k", 1 - k, plane, plane, None))
 
     start(zs[:1])
     finish(zs[:1])
@@ -435,21 +461,26 @@
             self.add(self.region(clip(self.mine + way * e, self.size)), inbox)
 
     def forward(self, way, e):
-        goal = self.mine + way * e
-        ok = (goal >= 0) & (goal < self.size)
-        self.post.send((self.name, way, e - 1), self.axis, clip(self.mine + way, self.size),
-                       self.region(clip(goal, self.size)), self.inbox(way, e - 1), ok)
+        def make():
+            goal = self.mine + way * e
+            ok = (goal >= 0) & (goal < self.size)
+            return self.axis, clip(self.mine + way, self.size), self.region(clip(goal, self.size)), self.inbox(way, e - 1), ok
+
+        self.post.send((self.name, way, e - 1), make)
 
     def start(self):
         for way in (1, -1):
             if self.reach >= 1:
                 self.forward(way, self.reach)
 
-    def finish(self, last=True):
-        for e in range(self.reach - 1, 0, -1):
+    def forward_from(self, nearest):
+        for e in range(self.reach - 1, nearest - 1, -1):
             for way in (1, -1):
                 self.take(way, e)
                 self.forward(way, e)
+
+    def finish(self, last=True):
+        self.forward_from(1)
         if last:
             for way in (1, -1):
                 if self.reach >= 1:
@@ -472,7 +503,7 @@
     greet(lines, device)
     post = Post(device, send_sems, recv_sems)
     for j in range(3):
-        post.send(("k", j), "k", 1 - k, part_ref.at[j, :, :, :, 1 - k], core_buf.at[j])
+        post.send(("k", j), lambda j=j: ("k", 1 - k, part_ref.at[j, :, :, :, 1 - k], core_buf.at[j], None))
 
     def plus(target, source):
         target[...] = (target[...].astype(floats) + source[...].astype(floats)).astype(halves)
@@ -493,7 +524,8 @@
         mine, size = lines[axis]
         vec_buf[stage, 1 + mine] = vec_buf[stage, 0]
         for t in range(1, size):
-            post.send(("v", stage, t), axis, lax.rem(mine + t, size), vec_buf.at[stage, 0], vec_buf.at[stage, 1 + mine])
+            post.send(("v", stage, t), lambda t=t: (
+                axis, lax.rem(mine + t, size), vec_buf.at[stage, 0], vec_buf.at[stage, 1 + mine], None))
 
     def vector_finish(stage, axis, out):
         mine, size = lines[axis]
@@ -639,6 +671,24 @@
     return value.reshape(-1, size)
 
 
+def split_plan(plan):
+    parts, order = [[]], []
+    for task in plan:
+        if task[0] == "U":
+            order.append(task[1:])
+            parts.append([])
+        else:
+            parts[-1].append(task)
+    return parts[0], parts[1:], order
+
+
+def pick(step, values):
+    value = values[0]
+    for i, other in enumerate(values[1:], 1):
+        value = jnp.where(step == i, other, value)
+    return value
+
+
 def place_of(rows):
     return lax.broadcasted_iota(jnp.int32, (rows, WINDOW), 1) // HEAD_DIM
 
@@ -648,8 +698,8 @@
 
 
 def forward_kernel(sizes, micro, own_ref, shard_ref, bias_ref, segq_ref, segk_ref,
-                   rest_ref, first_ref, every_ref, biases_ref, mixed_ref, lse_ref, q_ref, k_ref, v_ref,
-                   weights, tokens_buf, bias_buf, mask, mixed_buf, lse_buf, q_buf, k_buf, v_buf, acc, top, total,
+                   rest_ref, first_ref, turned_ref, biases_ref, mixed_ref, lse_ref, q_ref, k_ref, v_ref,
+                   weights, turned, bias_buf, mask, mixed_buf, lse_buf, q_buf, k_buf, v_buf, tokens_buf, acc, top, total,
                    send_sems, recv_sems, local_sems):
     floats, halves = jnp.float32, jnp.bfloat16
     lines, device = place(sizes)
@@ -675,18 +725,24 @@
     post = Post(device, send_sems, recv_sems)
     for copy in begin:
         copy.wait()
-    zs = [LineGather(post, ("z", j), "z", lines["z"], lambda i, j=j: targets[j].at[i, x, y, k]) for j in range(3)]
-    tokens = [LineGather(post, ("t", m), "z", lines["z"], lambda i, m=m: tokens_buf.at[m, i], reach) for m in range(micro)]
+    tokens = [
+        LineGather(post, ("t", q), "z", lines["z"],
+                   lambda i, q=q: tokens_buf.at[q // 2, i, pl.ds(q % 2 * (rows // 2), rows // 2)], reach)
+        for q in range(2 * micro)
+    ]
     small = LineGather(post, "bias", "z", lines["z"], lambda i: bias_buf.at[i])
-    second, third = {}, {}
-    for j in range(3):
-        second[j] = [
-            LineGather(post, ("a", j), "y", lines["y"], lambda i, j=j: targets[j].at[:, x, i, k, :, parts[0]]),
-            LineGather(post, ("b", j), "x", lines["x"], lambda i, j=j: targets[j].at[:, i, y, k, :, parts[1]]),
+    rb = shard_ref.shape[1]
+    zs, second, third = {}, {}, {}
+    for n in range(6):
+        j, r = n // 2, pl.ds(n % 2 * (rb // 2), rb // 2)
+        zs[n] = LineGather(post, ("z", n), "z", lines["z"], lambda i, j=j, r=r: targets[j].at[i, x, y, k, r])
+        second[n] = [
+            LineGather(post, ("a", n), "y", lines["y"], lambda i, j=j, r=r: targets[j].at[:, x, i, k, r, parts[0]]),
+            LineGather(post, ("b", n), "x", lines["x"], lambda i, j=j, r=r: targets[j].at[:, i, y, k, r, parts[1]]),
         ]
-        third[j] = [
-            LineGather(post, ("c", j), "x", lines["x"], lambda i, j=j: targets[j].at[:, i, :, k, :, parts[0]]),
-            LineGather(post, ("d", j), "y", lines["y"], lambda i, j=j: targets[j].at[:, :, i, k, :, parts[1]]),
+        third[n] = [
+            LineGather(post, ("c", n), "x", lines["x"], lambda i, j=j, r=r: targets[j].at[:, i, :, k, r, parts[0]]),
+            LineGather(post, ("d", n), "y", lines["y"], lambda i, j=j, r=r: targets[j].at[:, :, i, k, r, parts[1]]),
         ]
 
     def start(*group):
@@ -697,12 +753,14 @@
         for line in group:
             line.finish()
 
-    def swap(j):
-        own_plane = targets[j].at[:, :, :, k]
-        post.send(("k", j), "k", 1 - k, own_plane, own_plane)
-
-    def swapped(j):
-        post.wait(("k", j), "k", 1 - k, targets[j].at[:, :, :, 1 - k])
+    def side(n, which):
+        return targets[n // 2].at[:, :, :, which, pl.ds(n % 2 * (rb // 2), rb // 2)]
+
+    def swap(n):
+        post.send(("k", n), lambda: ("k", 1 - k, side(n, k), side(n, k), None))
+
+    def swapped(n):
+        post.wait(("k", n), "k", 1 - k, side(n, 1 - k))
 
     places = place_of(rows)
 
@@ -759,56 +817,72 @@
             same = jnp.broadcast_to(segk_ref[m, pl.ds(block, 1), :], (rows, rows)).T == segq_ref[m, 0:1]
             mask[m, block] = jnp.where(same, 0.0, MASK_VALUE)
 
+    def turn(m):
+        for block in range(cols):
+            inside = (low <= block) & (block < high)
+            at = pl.ds((m * cols + block) * rows, rows)
+
+            @pl.when(inside)
+            def _():
+                turned[:, at] = tokens_buf[m, block].T
+
+            if block > reach or cols - 1 - block > reach:
+                @pl.when(jnp.logical_not(inside))
+                def _():
+                    turned[:, at] = jnp.zeros((own_ref.shape[2], rows), halves)
+
     done = []
-    middle = max(cols // 2, 1)
-    start(small, zs[0])
-    finish(zs[0])
-    start(*second[0], tokens[0])
+    keeps = ((q_buf, q_ref), (k_buf, k_ref), (v_buf, v_ref), (lse_buf, lse_ref))
+
+    def take_z(n, t):
+        zs[n].step(t)
+        if n == 0:
+            small.step(t)
+        if t == cols - 1:
+            start(*second[n])
+
+    def take_second(n):
+        finish(*second[n])
+        start(*third[n])
+
+    def take_third(n):
+        finish(*third[n])
+        swap(n)
+
+    swaps = set()
+
+    def take_core(n):
+        swapped(n)
+        swaps.add(n)
+        if n < 2 and swaps >= {0, 1}:
+            done.append(local(weights.at[0], first_ref))
+
+    act = {
+        "Zs": lambda n: zs[n].start(), "Z": take_z, "Ts": lambda q: tokens[q].start(), "T": lambda q, t: tokens[q].step(t),
+        "B": take_second, "C": take_third, "K": take_core, "R": turn,
+    }
+    small.start()
+    head, tail, order = split_plan(FORWARD_PLAN)
+    act[head[0][0]](*head[0][1:])
     for m in range(micro):
         masks(m)
-    finish(small, *second[0])
-    start(*third[0])
-    finish(tokens[0])
-    start(zs[1])
-    finish(*third[0])
-    swap(0)
-    finish(zs[1])
-    start(*second[1], zs[2])
-    swapped(0)
-    units(0, 0, middle)
-    finish(*second[1])
-    start(*third[1])
-    finish(zs[2])
-    for m in range(1, micro):
-        start(tokens[m])
-    done.append(local(weights.at[0], first_ref))
-    units(0, middle, cols)
-    finish(*tokens[1:])
-    finish(*third[1])
-    swap(1)
-    start(*second[2])
-    for m in range(1, micro):
-        units(m, 0, middle)
-        if m == 1:
-            finish(*second[2])
-            start(*third[2])
-        units(m, middle, cols)
-    for m in range(micro):
-        @pl.loop(low, high)
-        def _(block, m=m):
-            copy = pltpu.make_async_copy(tokens_buf.at[m, block], every_ref.at[m, block], local_sems.at[used[0] + m])
-            copy.start()
-            copy.wait()
-    used[0] += micro
-    for source, target in ((bias_buf, biases_ref), (mixed_buf, mixed_ref), (lse_buf, lse_ref), (q_buf, q_ref), (k_buf, k_ref), (v_buf, v_ref)):
+    for task in head[1:]:
+        act[task[0]](*task[1:])
+
+    @pl.loop(0, len(order))
+    def _(step):
+        unit(pick(step, [m for m, _ in order]), pick(step, [c for _, c in order]))
+        for i, tasks in enumerate(tail[:-1]):
+            if tasks:
+                @pl.when(step == i)
+                def _(tasks=tasks):
+                    for task in tasks:
+                        act[task[0]](*task[1:])
+
+    for source, target in (*keeps, (bias_buf, biases_ref), (mixed_buf, mixed_ref), (turned, turned_ref)):
         done.append(local(source, target))
-    if micro == 1:
-        finish(*second[2])
-        start(*third[2])
-    finish(*third[2])
-    swap(2)
-    swapped(1)
-    swapped(2)
+    for task in tail[-1]:
+        act[task[0]](*task[1:])
     for copy in done:
         copy.wait()
     post.close()
@@ -821,12 +895,12 @@
     _, rb, w = shard.shape
     halves, floats = own.dtype, jnp.float32
     reach = min(nc - 1, -(-(DOC_MOST - 1) // rows))
-    count = (3 + 1) * 2 * (nc - 1) + micro * 2 * reach + 3 * (4 * (ny - 1) + 4 * (ns - 1) + 1)
+    count = (6 + 1) * 2 * (nc - 1) + micro * 4 * reach + 6 * (4 * (ny - 1) + 4 * (ns - 1) + 1)
     anywhere = pl.BlockSpec(memory_space=pl.ANY)
     vmem = pl.BlockSpec(memory_space=pltpu.VMEM)
     length = nc * rows
     arrays = [
-        ((2, nc, ns, ny, 2, rb, w), halves), ((nc, ns, ny, 2, rb, w), halves), ((micro, nc, rows, model), halves),
+        ((2, nc, ns, ny, 2, rb, w), halves), ((nc, ns, ny, 2, rb, w), halves), ((model, micro * length), halves),
         ((nc, *bias.shape), floats), ((nc, micro, rows, WINDOW), halves), ((micro, nc, 8, rows), floats),
         ((micro, nc, rows, WINDOW), halves), ((micro, nc, nc, rows, WINDOW), halves), ((micro, nc, nc, rows, WINDOW), halves),
     ]
@@ -839,7 +913,7 @@
         scratch_shapes=[
             pltpu.VMEM((1, nc, ns, ny, 2, rb, w), halves),
             shapes[2], shapes[3], pltpu.VMEM((micro, nc, rows, rows), floats), *shapes[4:],
-            pltpu.VMEM((WINDOW, rows), floats), pltpu.VMEM((8, rows), floats), pltpu.VMEM((8, rows), floats),
+            pltpu.VMEM((micro, nc, rows, model), halves), pltpu.VMEM((WINDOW, rows), floats), pltpu.VMEM((8, rows), floats), pltpu.VMEM((8, rows), floats),
             pltpu.SemaphoreType.DMA((count,)), pltpu.SemaphoreType.DMA((count,)), pltpu.SemaphoreType.DMA((20,)),
         ],
         compiler_params=pltpu.CompilerParams(collective_id=2, has_side_effects=True, vmem_limit_bytes=60 << 20),
@@ -975,12 +1049,12 @@
         return self.ref.at[0 if self.size == 2 else (1 - way) // 2, e]
 
 
-def backward_kernel(sizes, micro, grad_ref, share_ref, first_ref, every_ref, mixed_ref, lse_ref, q_ref, k_ref, v_ref,
+def backward_kernel(sizes, micro, grad_ref, share_ref, first_ref, turned_ref, mixed_ref, lse_ref, q_ref, k_ref, v_ref,
                     segq_ref, segk_ref, part_ref, vec_ref,
                     back_ref, block_ref, sums_ref,
                     mine_buf, core_buf, stage_buf, in_a, in_b, in_c, in_d, in_z, tok_buf, tok_in, vec_buf,
-                    weights, mixed_buf, q_buf, k_buf, v_buf, every_t, grad_t, x_buf, mask, acc, spread, block_sum,
-                    send_sems, recv_sems, local_sems):
+                    weights, mixed_buf, q_buf, k_buf, v_buf, every_t, grad_t, mask, acc, spread, block_sum,
+                    send_sems, recv_sems, local_sems, free_sem):
     floats, halves = jnp.float32, jnp.bfloat16
     lines, device = place(sizes)
     (x, ns), (y, ny), (k, _), (z, cols) = (lines[a] for a in "xykz")
@@ -999,15 +1073,19 @@
         copy.start()
         return copy
 
-    loads = [local(*pair) for pair in ((first_ref, weights), (mixed_ref, mixed_buf), (q_ref, q_buf))]
-    loads += [local(k_ref.at[0], k_buf.at[0]), local(v_ref.at[0], v_buf.at[0])]
-    loads += [local(share_ref, back_ref)]
-    planes = [local(part_ref.at[j, :, :, :, k], mine_buf.at[j + 1]) for j in range(2)]
-    more = [[local(k_ref.at[m], k_buf.at[m]), local(v_ref.at[m], v_buf.at[m])] for m in range(1, micro)]
+    def rows_of(n):
+        return pl.ds(n % 2 * (rb // 2), rb // 2)
+
+    planes = [local(part_ref.at[n // 2, :, :, :, k, rows_of(n)], mine_buf.at[n // 2 + 1, :, :, :, rows_of(n)]) for n in range(4)]
+    loads = [local(*pair) for pair in ((first_ref, weights), (mixed_ref, mixed_buf), (q_ref, q_buf), (share_ref, back_ref))]
+    loads += [local(k_ref, k_buf), local(v_ref, v_buf)]
+    loads += [local(turned_ref, every_t)]
     greet(lines, device)
     post = Post(device, send_sems, recv_sems)
-    for j in range(2):
-        post.send(("k", j + 1), "k", 1 - k, part_ref.at[j, :, :, :, 1 - k], core_buf.at[j + 1])
+
+    def give(n):
+        post.send(("k", n), lambda: (
+            "k", 1 - k, part_ref.at[n // 2, :, :, :, 1 - k, rows_of(n)], core_buf.at[n // 2, :, :, :, rows_of(n)], None))
 
     def plus(target, source):
         target[...] = (target[...].astype(floats) + source[...].astype(floats)).astype(halves)
@@ -1024,42 +1102,39 @@
             plus(target.at[n], source.at[n])
 
     class Stream:
-        def __init__(self, name, j, begin, size):
+        def __init__(self, name, j, begin, size, r):
             cs = pl.ds(begin, size)
-            self.j, self.begin, self.size = j, begin, size
             self.second = [
-                LineReduce(post, (name, "a"), "x", lines["x"], lambda i: mine_buf.at[j, cs, i, :, :, parts[0]],
-                           lambda way, e: Inbox(in_a.at[j], ns)(way, e).at[cs], lambda t, s: plus_grid(t, s, size, ny)),
-                LineReduce(post, (name, "b"), "y", lines["y"], lambda i: mine_buf.at[j, cs, :, i, :, parts[1]],
-                           lambda way, e: Inbox(in_b.at[j], ny)(way, e).at[cs], lambda t, s: plus_grid(t, s, size, ns)),
+                LineReduce(post, (name, "a"), "x", lines["x"], lambda i: mine_buf.at[j, cs, i, :, r, parts[0]],
+                           lambda way, e: Inbox(in_a.at[j], ns)(way, e).at[cs, :, r], lambda t, s: plus_grid(t, s, size, ny)),
+                LineReduce(post, (name, "b"), "y", lines["y"], lambda i: mine_buf.at[j, cs, :, i, r, parts[1]],
+                           lambda way, e: Inbox(in_b.at[j], ny)(way, e).at[cs, :, r], lambda t, s: plus_grid(t, s, size, ns)),
             ]
             self.third = [
-                LineReduce(post, (name, "c"), "y", lines["y"], lambda i: mine_buf.at[j, cs, x, i, :, parts[0]],
-                           lambda way, e: Inbox(in_c.at[j], ny)(way, e).at[cs], lambda t, s: plus_row(t, s, size)),
-                LineReduce(post, (name, "d"), "x", lines["x"], lambda i: mine_buf.at[j, cs, i, y, :, parts[1]],
-                           lambda way, e: Inbox(in_d.at[j], ns)(way, e).at[cs], lambda t, s: plus_row(t, s, size)),
+                LineReduce(post, (name, "c"), "y", lines["y"], lambda i: mine_buf.at[j, cs, x, i, r, parts[0]],
+                           lambda way, e: Inbox(in_c.at[j], ny)(way, e).at[cs, r], lambda t, s: plus_row(t, s, size)),
+                LineReduce(post, (name, "d"), "x", lines["x"], lambda i: mine_buf.at[j, cs, i, y, r, parts[1]],
+                           lambda way, e: Inbox(in_d.at[j], ns)(way, e).at[cs, r], lambda t, s: plus_row(t, s, size)),
             ]
 
-    ffn = [None] + [Stream(("s", j), j, 0, cols) for j in (1, 2)]
-    cut = max(cols // 2, 1)
-    attn = [Stream(("s", 0, begin), 0, begin, min(cut, cols - begin)) for begin in range(0, cols, cut)]
-    last = [
-        LineReduce(post, ("z", j), "z", lines["z"], lambda i, j=j: mine_buf.at[j, i, x, y],
-                   lambda way, e, j=j: in_z.at[j, (1 - way) // 2, e], plus)
-        for j in range(3)
-    ]
-
-    def plus_back(m):
-        def add(target, source):
-            back_ref[m] += source[...].astype(floats)
-
-        return add
-
-    tokens = [
-        LineReduce(post, ("t", m), "z", lines["z"], lambda i, m=m: tok_buf.at[m, i],
-                   lambda way, e, m=m: tok_in.at[m, (1 - way) // 2, e], plus, reach)
-        for m in range(micro)
-    ]
+    def line_z(name, j, r):
+        return LineReduce(post, ("z", name), "z", lines["z"], lambda i: mine_buf.at[j, i, x, y, r],
+                          lambda way, e: in_z.at[j, (1 - way) // 2, e, r], plus)
+
+    ffn = [Stream(("s", n), n // 2 + 1, 0, cols, rows_of(n)) for n in range(4)]
+    ffn_z = [line_z(n, n // 2 + 1, rows_of(n)) for n in range(4)]
+    attn = [Stream(("u", c), 0, c, 1, pl.ds(0, rb)) for c in range(cols)]
+    attn_z = line_z("u", 0, pl.ds(0, rb))
+
+    def half_of(h):
+        return pl.ds(h * (rows // 2), rows // 2)
+
+    def line_tokens(m, h):
+        at = half_of(h)
+        return LineReduce(post, ("t", m, h), "z", lines["z"], lambda i: tok_buf.at[m, i, at],
+                          lambda way, e: tok_in.at[m, (1 - way) // 2, e, at], plus, reach)
+
+    tokens = [[line_tokens(m, h) for h in range(2)] for m in range(micro)]
 
     def start(*group):
         for line in group:
@@ -1069,27 +1144,22 @@
         for line in group:
             line.finish()
 
-    def tokens_finish(m):
-        tokens[m].finish(last=False)
-        tokens[m].add = plus_back(m)
-        for way in (1, -1):
-            if tokens[m].reach >= 1:
-                tokens[m].take(way, 0)
-
-    def core(j):
-        planes[j - 1].wait()
-        post.wait(("k", j), "k", 1 - k, core_buf.at[j])
+    def core(n):
+        planes[n].wait()
+        r = rows_of(n)
+        post.wait(("k", n), "k", 1 - k, core_buf.at[n // 2, :, :, :, r])
 
         @pl.loop(0, cols * ns * ny)
-        def _(n):
-            at = (n // (ns * ny), lax.rem(n // ny, ns), lax.rem(n, ny))
-            plus(mine_buf.at[(j, *at)], core_buf.at[(j, *at)])
+        def _(i):
+            at = (i // (ns * ny), lax.rem(i // ny, ns), lax.rem(i, ny), r)
+            plus(mine_buf.at[(n // 2 + 1, *at)], core_buf.at[(n // 2, *at)])
 
     def vector_start(stage, axis):
         mine, size = lines[axis]
         vec_buf[stage, 1 + mine] = vec_buf[stage, 0]
         for t in range(1, size):
-            post.send(("v", stage, t), axis, lax.rem(mine + t, size), vec_buf.at[stage, 0], vec_buf.at[stage, 1 + mine])
+            post.send(("v", stage, t), lambda t=t: (
+                axis, lax.rem(mine + t, size), vec_buf.at[stage, 0], vec_buf.at[stage, 1 + mine], None))
 
     def vector_finish(stage, axis, out):
         mine, size = lines[axis]
@@ -1110,29 +1180,18 @@
         @pl.loop(low, high)
         def _(block):
             same = jnp.broadcast_to(segk_ref[m, pl.ds(block, 1), :], (rows, rows)).T == segq_ref[m, 0:1]
-            mask[block] = jnp.where(same, 0.0, MASK_VALUE)
-
-    def turn(m):
+            mask[m, block] = jnp.where(same, 0.0, MASK_VALUE).astype(halves)
+
+    def clear():
         for block in range(cols):
-            inside = (low <= block) & (block < high)
-            at = pl.ds((m * cols + block) * rows, rows)
-
-            @pl.when(inside)
-            def _():
-                copy = pltpu.make_async_copy(every_ref.at[m, block], x_buf, local_sems.at[used[0] + m])
-                copy.start()
-                copy.wait()
-                every_t[:, at] = x_buf[...].T
-
             if block > reach or cols - 1 - block > reach:
-                @pl.when(jnp.logical_not(inside))
+                @pl.when(jnp.logical_not((low <= block) & (block < high)))
                 def _():
-                    every_t[:, at] = jnp.zeros((model, rows), halves)
-
-                    @pl.loop(0, cols)
-                    def _(c):
-                        k_buf[m, c, block] = jnp.zeros((rows, WINDOW), halves)
-                        v_buf[m, c, block] = jnp.zeros((rows, WINDOW), halves)
+                    @pl.loop(0, micro * cols)
+                    def _(n):
+                        at = (n // cols, lax.rem(n, cols), block)
+                        k_buf[at] = jnp.zeros((rows, WINDOW), halves)
+                        v_buf[at] = jnp.zeros((rows, WINDOW), halves)
 
     def unit(m, c):
         mixed_grad = jnp.dot(grad_ref[m], weights[c, :, O_AT : O_AT + WINDOW], preferred_element_type=floats).astype(halves)
@@ -1156,7 +1215,7 @@
             keys = k_buf[m, c, block]
             values = v_buf[m, c, block]
             keys_t = keys.T
-            hidden = mask[block]
+            hidden = mask[m, block].astype(floats)
             key_grad = jnp.zeros((rows, WINDOW), floats)
             value_grad = jnp.zeros((rows, WINDOW), floats)
             for h in range(3):
@@ -1170,7 +1229,7 @@
             key_low, value_low = key_grad.astype(halves), value_grad.astype(halves)
             k_buf[m, c, block] = key_low
             v_buf[m, c, block] = value_low
-            spread[block] += contract_cols(key_low, key_weight) + contract_cols(value_low, value_weight)
+            spread[m, block] += contract_cols(key_low, key_weight) + contract_cols(value_low, value_weight)
             return value_bias + jnp.sum(value_low.astype(floats), 0, keepdims=True)
 
         value_bias = lax.fori_loop(low, high, step, jnp.zeros((1, WINDOW), floats))
@@ -1180,130 +1239,150 @@
         vec_buf[0, 0, pl.ds(small + c, 1), WINDOW : 2 * WINDOW] += value_bias
         back_ref[m] += contract_cols(query_low, weights[c, :, Q_AT : Q_AT + WINDOW])
 
-    def units(m, first, last_):
-        @pl.loop(first, last_)
-        def _(c):
-            unit(m, c)
-
     def send_tokens(m):
-        back_ref[m] += spread[z]
+        back_ref[m] += spread[m, z]
 
         @pl.loop(low, high)
         def _(block):
-            tok_buf[m, block] = spread[block].astype(halves)
-
-        start(tokens[m])
+            tok_buf[m, block] = spread[m, block].astype(halves)
+
+        start(*tokens[m])
 
     def weight_grads(c):
-        for begin in range(0, model, 256):
-            side = pl.ds(begin, 256)
-            block_sum[side] = jnp.zeros((256, 4 * (WINDOW - HEAD_DIM)), floats)
-            out = 0
+        strip = block_sum.shape[0]
+
+        @pl.loop(0, model // strip)
+        def _(part):
+            base = pl.multiple_of(part * strip, strip)
+            side = pl.ds(base, strip)
+            block_sum[...] = jnp.zeros_like(block_sum)
             for m in range(micro):
                 mine_at = pl.ds(pl.multiple_of((m * cols + z) * rows, rows), rows)
-                block_sum[side, Q_AT : Q_AT + WINDOW] += jnp.dot(every_t[side, mine_at], q_buf[m, c], preferred_element_type=floats)
+                block_sum[:, Q_AT : Q_AT + WINDOW] += jnp.dot(every_t[side, mine_at], q_buf[m, c], preferred_element_type=floats)
                 all_at = pl.ds(m * cols * rows, cols * rows)
-                block_sum[side, K_AT : K_AT + WINDOW] += jnp.dot(
+                block_sum[:, K_AT : K_AT + WINDOW] += jnp.dot(
                     every_t[side, all_at], k_buf[m, c].reshape(-1, WINDOW), preferred_element_type=floats)
-                block_sum[side, V_AT : V_AT + WINDOW] += jnp.dot(
+                block_sum[:, V_AT : V_AT + WINDOW] += jnp.dot(
                     every_t[side, all_at], v_buf[m, c].reshape(-1, WINDOW), preferred_element_type=floats)
-                block_sum[side, O_AT : O_AT + WINDOW] += jnp.dot(
+                block_sum[:, O_AT : O_AT + WINDOW] += jnp.dot(
                     grad_t[side, m * rows : (m + 1) * rows], mixed_buf[c, m], preferred_element_type=floats)
-        for i in range(ns * ny):
-            ours = pl.ds(pl.multiple_of((2 * i + k) * rb, 16), rb)
-            theirs = pl.ds(pl.multiple_of((2 * i + 1 - k) * rb, 16), rb)
-            mine_buf[0, c, i // ny, i % ny] = block_sum[ours].astype(halves)
-            stage_buf[c, i // ny, i % ny] = block_sum[theirs].astype(halves)
-
-    def attn_core(stream):
-        cs = pl.ds(stream.begin, stream.size)
-
-        @pl.loop(stream.begin, stream.begin + stream.size)
-        def _(c):
+            for i in range(strip // (2 * rb)):
+                ours = pl.ds(pl.multiple_of((2 * i + k) * rb, 16), rb)
+                theirs = pl.ds(pl.multiple_of((2 * i + 1 - k) * rb, 16), rb)
+                chip = part * (strip // (2 * rb)) + i
+                mine_buf[0, c, chip // ny, lax.rem(chip, ny)] = block_sum[ours].astype(halves)
+                stage_buf[c, chip // ny, lax.rem(chip, ny)] = block_sum[theirs].astype(halves)
+
+    waited = []
+
+    def attn_give(c):
+        if not waited:
+            pl.semaphore_wait(free_sem, 1)
+            waited.append(c)
+        post.send(("g", c), lambda: ("k", 1 - k, stage_buf.at[c], core_buf.at[0, c], None))
+
+    def attn_add(c):
+        post.wait(("g", c), "k", 1 - k, core_buf.at[0, c])
+
+        @pl.loop(0, ns * ny)
+        def _(n):
+            at = (c, n // ny, lax.rem(n, ny))
+            plus(mine_buf.at[(0, *at)], core_buf.at[(0, *at)])
+
+    streams = ffn + attn
+    added = set()
+
+    def take_core(n):
+        if n < 4:
+            core(n)
+            added.add(n)
+            if added >= {0, 1} and n in (0, 1):
+                pl.semaphore_signal(free_sem, 1, device_id=device("k", 1 - k), device_id_type=MESH)
+        else:
+            attn_add(n - 4)
+        start(*streams[n].second)
+
+    def take_second(n):
+        finish(*streams[n].second)
+        start(*streams[n].third)
+
+    def take_third(n):
+        finish(*streams[n].third)
+        if n < 4:
+            start(ffn_z[n])
+
+    def along(line, e):
+        for way in (1, -1):
+            line.take(way, e)
+            if e:
+                line.forward(way, e)
+
+    def take_tokens(m, h, e):
+        line = tokens[m][h]
+        if e == 0:
+            at = half_of(h)
+
+            def add(target, source):
+                back_ref[m, at] += source[...].astype(floats)
+
+            line.add = add
+        along(line, e)
+
+    def vectors(stage):
+        if stage:
+            vector_finish(stage - 1, "kyxz"[stage - 1], vec_buf.at[stage, 0] if stage < 4 else sums_ref)
+        if stage < 4:
+            vector_start(stage, "kyxz"[stage])
+
+    def load():
+        for copy in loads:
+            copy.wait()
+        clear()
+
+    act = {
+        "L": load, "G": lambda n: give(n) if n < 4 else attn_give(n - 4), "A": take_core, "B": take_second, "C": take_third,
+        "Z": lambda n, e: along(ffn_z[n], e), "S": send_tokens, "T": take_tokens, "Ys": lambda: start(attn_z),
+        "Y": lambda e: along(attn_z, e), "V": vectors,
+    }
+    head, tail, order = split_plan([("U", "W", task[1], 0) if task[0] == "W" else task for task in BACKWARD_PLAN])
+    kinds = [item[0] == "W" for item in order]
+    heads = [item[1] if item[0] == "W" else item[0] for item in order]
+    micros = [0 if item[0] == "W" else item[1] for item in order]
+    act[head[0][0]](*head[0][1:])
+    spread[...] = jnp.zeros_like(spread)
+    for m in range(micro):
+        masks(m)
+        grad_t[:, m * rows : (m + 1) * rows] = grad_ref[m].T
+    for task in head[1:]:
+        act[task[0]](*task[1:])
+
+    @pl.loop(0, len(order))
+    def _(step):
+        c, m, kind = pick(step, heads), pick(step, micros), pick(step, [int(k_) for k_ in kinds])
+
+        @pl.when(kind == 0)
+        def _():
+            unit(m, c)
+
+        @pl.when(kind == 1)
+        def _():
             weight_grads(c)
 
-        post.send(("k", 0, stream.begin), "k", 1 - k, stage_buf.at[cs], core_buf.at[0, cs])
-
-    def attn_add(stream):
-        cs = pl.ds(stream.begin, stream.size)
-        post.wait(("k", 0, stream.begin), "k", 1 - k, core_buf.at[0, cs])
-
-        @pl.loop(0, stream.size * ns * ny)
-        def _(n):
-            at = (stream.begin + n // (ns * ny), lax.rem(n // ny, ns), lax.rem(n, ny))
-            plus(mine_buf.at[(0, *at)], core_buf.at[(0, *at)])
-
-    for copy in loads:
-        copy.wait()
-    masks(0)
-    spread[...] = jnp.zeros_like(spread)
-    units(0, 0, 1)
-    core(1)
-    start(*ffn[1].second)
-    for m in range(micro):
-        for copy in more[m - 1] if m else ():
-            copy.wait()
-        turn(m)
-        grad_t[:, m * rows : (m + 1) * rows] = grad_ref[m].T
-    core(2)
-    start(*ffn[2].second)
-    units(0, 1, 3)
-    finish(*ffn[1].second)
-    start(*ffn[1].third)
-    units(0, 3, cols)
-    send_tokens(0)
-    for m in range(1, micro):
-        masks(m)
-        spread[...] = jnp.zeros_like(spread)
-        units(m, 0, 1)
-        if m == 1:
-            finish(*ffn[2].second)
-            start(*ffn[2].third)
-            finish(*ffn[1].third)
-            start(last[1])
-        units(m, 1, 2)
-        if m == 1:
-            tokens_finish(0)
-        units(m, 2, 3)
-        if m == 1:
-            finish(*ffn[2].third)
-            start(last[2])
-        units(m, 3, cols)
-        send_tokens(m)
-    vector_start(0, "k")
-    attn_core(attn[0])
-    vector_finish(0, "k", vec_buf.at[1, 0])
-    vector_start(1, "y")
-    for stream in attn[1:]:
-        attn_core(stream)
-    attn_add(attn[0])
-    start(*attn[0].second)
-    vector_finish(1, "y", vec_buf.at[2, 0])
-    vector_start(2, "x")
-    finish(last[1])
-    for stream in attn[1:]:
-        attn_add(stream)
-        start(*stream.second)
-    vector_finish(2, "x", vec_buf.at[3, 0])
-    vector_start(3, "z")
-    for m in range(1, micro):
-        tokens_finish(m)
-    finish(last[2])
-    for stream in attn:
-        finish(*stream.second)
-        start(*stream.third)
-    vector_finish(3, "z", sums_ref)
-    for stream in attn:
-        finish(*stream.third)
-    start(last[0])
-    for j in (1, 2):
+        for i, tasks in enumerate(tail[:-1]):
+            if tasks:
+                @pl.when(step == i)
+                def _(tasks=tasks):
+                    for task in tasks:
+                        act[task[0]](*task[1:])
+
+    for task in tail[-1]:
+        act[task[0]](*task[1:])
+    for j in range(3):
         block_ref[j] = mine_buf[j, z, x, y].astype(floats)
-    finish(last[0])
-    block_ref[0] = mine_buf[0, z, x, y].astype(floats)
     post.close()
 
 
-def backward(sizes, grad, share, first, every, mixed, lse, q, k, v, seg_own, seg_all, part, vectors):
+def backward(sizes, grad, share, first, turned, mixed, lse, q, k, v, seg_own, seg_all, part, vectors):
     ns, nr, nc = sizes
     ny = nr // 2
     micro, rows, model = grad.shape
@@ -1311,8 +1390,8 @@
     rb = model // (ns * nr)
     halves, floats = jnp.bfloat16, jnp.float32
     reach = min(nc - 1, -(-(DOC_MOST - 1) // rows))
-    streams = 2 + -(-nc // max(nc // 2, 1))
-    count = 2 + nc + 4 * (ny - 1 + ns - 1) * streams + 3 * 2 * (nc - 1) + micro * 2 * reach + (1 + ny - 1 + ns - 1 + nc - 1)
+    streams = 4 + nc
+    count = 4 + nc + 4 * (ny - 1 + ns - 1) * streams + 5 * 2 * (nc - 1) + micro * 4 * reach + (1 + ny - 1 + ns - 1 + nc - 1)
     widest = max(ns, ny, nc, 2)
     ways = lambda n: 1 if n == 2 else 2
     vec_shape = (vectors.shape[0] + nc + -nc % 8, model)
@@ -1329,20 +1408,20 @@
         in_specs=[vmem, anywhere, anywhere, anywhere, anywhere, vmem, anywhere, anywhere, anywhere, vmem, vmem, anywhere, vmem],
         out_specs=[vmem] * 3,
         scratch_shapes=[
-            buf(3, nc, ns, ny, rb, w), buf(3, nc, ns, ny, rb, w), buf(nc, ns, ny, rb, w),
+            buf(3, nc, ns, ny, rb, w), buf(2, nc, ns, ny, rb, w), buf(nc, ns, ny, rb, w),
             buf(3, ways(ns), max(ns - 1, 1), nc, ny, rb, w // 2), buf(3, ways(ny), max(ny - 1, 1), nc, ns, rb, w // 2),
             buf(3, ways(ny), max(ny - 1, 1), nc, rb, w // 2), buf(3, ways(ns), max(ns - 1, 1), nc, rb, w // 2),
             buf(3, 2, max(nc - 1, 1), rb, w), buf(micro, nc, rows, model), buf(micro, 2, max(reach, 1), rows, model),
             buf(4, 1 + widest, *vec_shape, kind=floats),
             buf(nc, model, w), buf(nc, micro, rows, WINDOW), buf(micro, nc, rows, WINDOW),
             buf(micro, nc, nc, rows, WINDOW), buf(micro, nc, nc, rows, WINDOW),
-            buf(model, micro * nc * rows), buf(model, micro * rows), buf(rows, model),
-            buf(nc, rows, rows, kind=floats), buf(WINDOW, rows, kind=floats), buf(nc, rows, model, kind=floats), buf(model, w, kind=floats),
-            pltpu.SemaphoreType.DMA((count,)), pltpu.SemaphoreType.DMA((count,)), pltpu.SemaphoreType.DMA((24,)),
+            buf(model, micro * nc * rows), buf(model, micro * rows),
+            buf(micro, nc, rows, rows), buf(WINDOW, rows, kind=floats), buf(micro, nc, rows, model, kind=floats), buf(model // 2, w, kind=floats),
+            pltpu.SemaphoreType.DMA((count,)), pltpu.SemaphoreType.DMA((count,)), pltpu.SemaphoreType.DMA((24,)), pltpu.SemaphoreType.REGULAR,
         ],
         compiler_params=pltpu.CompilerParams(collective_id=3, has_side_effects=True, vmem_limit_bytes=62 << 20),
         name="backward",
-    )(grad, share, first, every, mixed, lse, q, k, v, seg_own.astype(floats)[:, None], seg_all.astype(floats).reshape(micro, nc, rows),
+    )(grad, share, first, turned, mixed, lse, q, k, v, seg_own.astype(floats)[:, None], seg_all.astype(floats).reshape(micro, nc, rows),
       part.reshape(2, nc, ns, ny, 2, rb, w), vectors)
 
 
@@ -1463,7 +1542,7 @@
     bias = jnp.stack([pad(hidden_bias), pad(query_bias), pad(value_bias)] + [jnp.zeros((model,), floats)] * 5)
     seg_all = segment_ids[:, 0]
     seg_own = lax.dynamic_slice_in_dim(seg_all, here * rows, rows, 1)
-    rest, first, everything, biases, mixed, lse, q, k, v = forward(sizes, own, shard, bias, seg_own, seg_all)
+    rest, first, turned, biases, mixed, lse, q, k, v = forward(sizes, own, shard, bias, seg_own, seg_all)
     first = first.reshape(cols, model, 4 * width)
     total = micro * rows
     flat = lambda a: a.reshape(total, -1)
@@ -1472,7 +1551,7 @@
     outputs, first_grad, attn_grad, part, sums = middle(
         flat(own), mixed.reshape(cols, total, WINDOW), first, rest.reshape(2, cols, model, -1), biases, vectors, flat(cotangent[:, 0]))
     parted = lambda a: a.reshape(micro, rows, model)
-    input_grad, reduced, sums = backward(sizes, parted(attn_grad), parted(first_grad), first, everything, mixed, lse, q, k, v,
+    input_grad, reduced, sums = backward(sizes, parted(attn_grad), parted(first_grad), first, turned, mixed, lse, q, k, v,
                                          seg_own, seg_all, part, sums)
     piece = lambda i: reduced[0, :, i * width : (i + 1) * width]
     mine = lambda first_row, at, size: lax.dynamic_slice(sums, (first_row + here, at), (1, size))[0]
@@ -1486,7 +1565,9 @@
 
 
 def per_device(sizes, inputs, segment_ids, query_weight, *rest):
-    fits = query_weight.shape == (query_weight.shape[0] // 16 * 16, 3 * HEAD_DIM)
+    micro, _, rows, _ = inputs.shape
+    fits = (query_weight.shape == (query_weight.shape[0] // 32 * 32, 3 * HEAD_DIM) and micro == 2 and sizes[2] == 4
+            and DOC_MOST // 2 == rows)
     return (per_device_fused if fits else per_device_plain)(sizes, inputs, segment_ids, query_weight, *rest)
 
 

time: 315 us -> 260 us (0.83)
  Pallas kernels: 290 us -> 235 us
    pallas_call x1, Pallas kernels: 154 us -> 111 us  [backward(): pl.pallas_call(functools.partial(backward_kernel, sizes, micro), out_shap...]
    pallas_call x1, Pallas kernels: 108 us -> 95.2 us  [forward(): pl.pallas_call(functools.partial(forward_kernel, sizes, micro), out_shape...]
where the time goes in v4:
time: 260 us; the launch traced here: 259 us
  Pallas kernels  235 us (90%)
  local copies, waits for them, and re-layouts  17.6 us (7%)
  other arithmetic  6.06 us (2%)
    pallas_call x1, Pallas kernels, backward(): pl.pallas_call(functools.partial(backward_kernel, sizes, micro), out_shap...  111 us
    pallas_call x1, Pallas kernels, forward(): pl.pallas_call(functools.partial(forward_kernel, sizes, micro), out_shape...  95.2 us
    pallas_call x1, Pallas kernels, middle(): pl.pallas_call(functools.partial(middle_kernel, cols), grid=(2 * cols,),...  28 us

profile of v4, /device:TPU:0, one launch (start us, length us, event | category | flops | bytes accessed | tf_op | source)
XLA Modules:
  0.0 259.0 jit_solution(15304942546475591484)
XLA Ops:
  0.7 1.3 dynamic-slice_convert_fusion.segq_ref
  1.9 0.7 convert_reduce_fusion
  3.3 0.9 copy.35
  4.2 1.0 maximum_bitcast_fusion
  5.1 1.8 pad_maximum_fusion.shard_ref
  6.9 0.7 pad_convert_fusion.1
  7.6 0.7 pad_convert_fusion
  8.2 0.7 reshape.67
  9.6 95.2 %forward.1 = (bf16[2,4,2,2,2,96,768]{6,5,4,3,2,1,0:T(8,128)(2,1)}, bf16[4,2,2,2,96,768]{5,4,3,2,1,0:T(8,128)(2,1)}, bf16[768,2048]{1,0:T(8,128)(2,1)}, f32[4,8,7...) custom-call(bf16[2,256,768]{2,1,0:T(8,128)(2,1)} %bitcast.46, ...), custom_call_target="tpu_custom_call" | custom-call | tf_op jit(solution)/shard_map/forward/pallas_call | solution.py:908
  104.8 0.7 reshape.70
  105.5 0.7 reshape.71
  106.2 0.7 reshape.72
  106.9 0.7 reshape.73
  107.6 0.7 reshape.74
  108.3 0.7 reshape.75
  108.9 0.6 stack.103.vector_ref
  109.6 28.0 %middle.1 = (bf16[512,768]{1,0:T(8,128)(2,1)}, f32[512,768]{1,0:T(8,128)}, bf16[512,768]{1,0:T(8,128)(2,1)}, bf16[2,4,768,768]{3,2,1,0:T(8,128)(2,1)}, f32[16,768]{1,0:T(8,128)}) custom-call(bf16[512,768]{1,0:T(8,128)(2,1)} %bitcast.47, bf16[4,512,256]{2,1,0:T(8,128)(2,1)} %bitcast.45, bf16[4,768,768]{2,1,0:T(8,128)(2,1)} %bitcast.42, ...), custom_call_target="tpu_custom_call" | custom-call | tf_op jit(solution)/shard_map/middle/pallas_call | solution.py:1013
  137.6 111.4 %backward.1 = (f32[2,256,768]{2,1,0:T(8,128)}, f32[3,96,768]{2,1,0:T(8,128)}, f32[24,768]{1,0:T(8,128)}) custom-call(bf16[2,256,768]{2,1,0:T(8,128)(2,1)} %bitcast.51, f32[2,256,768]{2,1,0:T(8,128)} %bitcast.48, bf16[4,768,768]{2,1,0:T(8,128)(2,1)} %bitcast.43, bf16[768,2048]{1,0:T(8,128)(2,1)} %get-tuple-element.41.turned_ref, ...), custom_call_target="tpu_custom_call" | custom-call | tf_op jit(solution)/shard_map/backward/pallas_call | solution.py:1401
  249.0 1.9 slice_bitcast_fusion
  250.9 1.8 slice_bitcast_fusion.2
  252.7 0.7 copy.38
  253.4 1.6 slice_reduce_fusion
  255.1 1.3 constant_dynamic-slice_fusion.1
  256.3 2.7 %copy.40 = f32[2,1,256,768]{3,2,1,0:T(8,128)} copy(f32[2,1,256,768]{3,2,1,0:T(8,128)} %bitcast.49) | data formatting | bytes 3145728
  (7 shorter events, 1.3 us)

commit v5 on v4

--- a/solution.py
+++ b/solution.py
@@ -48,14 +48,16 @@
     ("U", 1, 0), ("K", 3), ("K", 4), ("B", 5), ("U", 1, 1), ("U", 1, 2), ("C", 5), ("U", 1, 3), ("K", 5),
 )
 BACKWARD_PLAN = (
-    ("G", 3), ("G", 0), ("L",), ("U", 0, 0), ("A", 0), ("A", 3), ("U", 0, 1), ("U", 1, 0), ("B", 0), ("U", 1, 1),
-    ("B", 3), ("C", 0), ("U", 2, 0), ("C", 3), ("Z", 0, 2), ("G", 1), ("U", 3, 0), ("Z", 3, 2), ("S", 0), ("A", 1),
-    ("G", 2), ("U", 2, 1), ("A", 2), ("T", 0, 0, 1), ("W", 0), ("B", 1), ("T", 0, 1, 1), ("G", 4), ("U", 3, 1),
-    ("Z", 0, 1), ("V", 0), ("A", 4), ("S", 1), ("V", 1), ("B", 2), ("W", 1), ("G", 5), ("B", 4), ("W", 2), ("V", 2),
-    ("G", 6), ("T", 1, 0, 1), ("A", 5), ("W", 3), ("A", 6), ("G", 7), ("C", 2), ("C", 1), ("V", 3), ("Z", 2, 2),
-    ("A", 7), ("Z", 3, 1), ("B", 5), ("Z", 1, 2), ("Z", 2, 1), ("B", 6), ("T", 1, 1, 1), ("B", 7), ("T", 0, 0, 0),
-    ("Z", 3, 0), ("C", 4), ("C", 5), ("T", 0, 1, 0), ("Z", 2, 0), ("Z", 0, 0), ("C", 6), ("C", 7), ("Ys",), ("V", 4),
-    ("Y", 2), ("Z", 1, 1), ("T", 1, 0, 0), ("Y", 1), ("T", 1, 1, 0), ("Z", 1, 0), ("Y", 0),
+    ("L",), ("G", 0), ("G", 2), ("U", 1, 0), ("A", 0), ("U", 0, 0), ("U", 2, 0), ("B", 0), ("A", 2), ("G", 1),
+    ("G", 3), ("U", 3, 0), ("C", 0), ("S", 0), ("U", 2, 1), ("B", 2), ("U", 0, 1), ("Z", 0, 2), ("A", 1), ("A", 3),
+    ("C", 2), ("T", 0, 1, 1), ("T", 0, 0, 1), ("U", 1, 1), ("U", 3, 1), ("S", 1), ("B", 1), ("V", 0), ("W", 2),
+    ("V", 1), ("B", 3), ("G", 6), ("Z", 2, 2), ("W", 0), ("G", 4), ("V", 2), ("A", 6), ("C", 1), ("W", 3),
+    ("T", 1, 0, 1), ("G", 7), ("A", 4), ("W", 1), ("G", 5), ("A", 7), ("T", 1, 1, 1), ("B", 6), ("C", 3), ("A", 5),
+    ("Z", 2, 1), ("T", 0, 1, 0), ("Z", 1, 2), ("Z", 3, 2), ("B", 4), ("V", 3), ("Z", 0, 1), ("B", 7), ("B", 5),
+    ("Z", 2, 0), ("C", 6), ("C", 4), ("T", 1, 0, 0), ("C", 7), ("Y", 3, 3), ("Y", 2, 2), ("Y", 0, 3), ("Z", 1, 1),
+    ("T", 0, 0, 0), ("C", 5), ("Y", 1, 2), ("V", 4), ("Y", 3, 2), ("Y", 2, 1), ("Y", 0, 2), ("Z", 3, 1), ("Z", 1, 0),
+    ("Y", 0, 1), ("T", 1, 1, 0), ("Y", 1, 1), ("Y", 3, 1), ("Z", 0, 0), ("Y", 2, 0), ("Z", 3, 0), ("Y", 0, 0),
+    ("Y", 3, 0), ("Y", 1, 0),
 )
 def attend_kernel(bounds, own_ref, all_ref, wq_ref, wk_ref, wv_ref, bq_ref, bv_ref,
                   segq_ref, segk_ref, mixed_ref, lse_ref, q_ref, k_ref, v_ref, bias, acc, top, total):
@@ -485,6 +487,25 @@
             for way in (1, -1):
                 if self.reach >= 1:
                     self.take(way, 0)
+
+
+def reduce_to(post, name, axis, line, goal, e, region, inbox, add):
+    mine, size = line
+    for way in (1, -1):
+        behind = mine - way
+        arrives = (way * (goal - mine) == e) & (behind >= 0) & (behind < size)
+        slot = inbox(way, min(e, size - 2))
+        post.wait((name, way), axis, clip(behind, size), slot, arrives)
+
+        @pl.when(arrives)
+        def _():
+            add(region, slot)
+
+        def make(way=way):
+            return axis, clip(mine + way, size), region, inbox(way, e - 1), way * (goal - mine) == e
+
+        if e:
+            post.send((name, way), make)
 
 
 def reduce_kernel(sizes, micro, own_ref, spread_ref, part_ref, vec_ref, back_ref, block_ref, sums_ref,
@@ -697,8 +718,8 @@
     return jnp.where(places == wanted, value, jnp.zeros_like(value))
 
 
-def forward_kernel(sizes, micro, own_ref, shard_ref, bias_ref, segq_ref, segk_ref,
-                   rest_ref, first_ref, turned_ref, biases_ref, mixed_ref, lse_ref, q_ref, k_ref, v_ref,
+def forward_kernel(sizes, micro, own_ref, shard_ref, hidden_bias_ref, query_bias_ref, value_bias_ref, seg_ref,
+                   rest_ref, first_ref, turned_ref, mask_ref, biases_ref, mixed_ref, lse_ref, q_ref, k_ref, v_ref,
                    weights, turned, bias_buf, mask, mixed_buf, lse_buf, q_buf, k_buf, v_buf, tokens_buf, acc, top, total,
                    send_sems, recv_sems, local_sems):
     floats, halves = jnp.float32, jnp.bfloat16
@@ -720,7 +741,10 @@
     targets = [weights.at[0], rest_ref.at[0], rest_ref.at[1]]
     begin = [local(shard_ref.at[j], targets[j].at[z, x, y, k]) for j in range(3)]
     begin += [local(own_ref.at[m], tokens_buf.at[m, z]) for m in range(micro)]
-    begin += [local(bias_ref, bias_buf.at[z])]
+    for i, ref in enumerate((hidden_bias_ref, query_bias_ref, value_bias_ref)):
+        bias_buf[z, i : i + 1, 0 : ref.shape[0]] = ref[...].astype(floats).reshape(1, -1)
+        if ref.shape[0] < WINDOW:
+            bias_buf[z, i : i + 1, ref.shape[0] : WINDOW] = jnp.zeros((1, WINDOW - ref.shape[0]), floats)
     greet(lines, device)
     post = Post(device, send_sems, recv_sems)
     for copy in begin:
@@ -777,14 +801,14 @@
         value_weight = plane(weights.at[0], c, V_AT)
         value_bias = bias_buf[c, 2:3, 0:WINDOW]
 
-        def step(block, carry):
+        def step(block):
             rows_at = tokens_buf[m, block]
             keys = jnp.dot(rows_at, key_weight, preferred_element_type=floats).astype(halves)
             values = (jnp.dot(rows_at, value_weight, preferred_element_type=floats) + value_bias).astype(halves)
             k_buf[m, c, block] = keys
             v_buf[m, c, block] = values
             values_t = values.T
-            hidden = mask[m, block]
+            hidden = mask[m, block].astype(floats)
             for h in range(3):
                 s = contract_cols(keys, heads[h]) + hidden
                 old = top[h : h + 1]
@@ -797,9 +821,9 @@
                 acc[at, :] = acc[at, :] * shrink + jnp.dot(
                     values_t[h * HEAD_DIM : (h + 1) * HEAD_DIM], p.astype(halves), preferred_element_type=floats
                 )
-            return carry
-
-        lax.fori_loop(low, high, step, 0)
+
+        for block in range(cols):
+            step(block)
         for h in range(3):
             at = pl.ds((h + 1) * HEAD_DIM, HEAD_DIM)
             acc[at, :] = acc[at, :] / total[h : h + 1]
@@ -812,24 +836,15 @@
             unit(m, c)
 
     def masks(m):
-        @pl.loop(low, high)
-        def _(block):
-            same = jnp.broadcast_to(segk_ref[m, pl.ds(block, 1), :], (rows, rows)).T == segq_ref[m, 0:1]
-            mask[m, block] = jnp.where(same, 0.0, MASK_VALUE)
+        asking = seg_ref[m, 0:1, pl.ds(pl.multiple_of(z * rows, 128), rows)].astype(floats)
+        for block in range(cols):
+            asked = seg_ref[m, 0:1, block * rows : (block + 1) * rows].astype(floats)
+            same = jnp.broadcast_to(asked, (rows, rows)).T == asking
+            mask[m, block] = jnp.where(same, 0.0, MASK_VALUE).astype(halves)
 
     def turn(m):
         for block in range(cols):
-            inside = (low <= block) & (block < high)
-            at = pl.ds((m * cols + block) * rows, rows)
-
-            @pl.when(inside)
-            def _():
-                turned[:, at] = tokens_buf[m, block].T
-
-            if block > reach or cols - 1 - block > reach:
-                @pl.when(jnp.logical_not(inside))
-                def _():
-                    turned[:, at] = jnp.zeros((own_ref.shape[2], rows), halves)
+            turned[:, (m * cols + block) * rows : (m * cols + block + 1) * rows] = tokens_buf[m, block].T
 
     done = []
     keeps = ((q_buf, q_ref), (k_buf, k_ref), (v_buf, v_ref), (lse_buf, lse_ref))
@@ -864,6 +879,12 @@
     small.start()
     head, tail, order = split_plan(FORWARD_PLAN)
     act[head[0][0]](*head[0][1:])
+    for block in range(cols):
+        if block > reach or cols - 1 - block > reach:
+            @pl.when(jnp.logical_not((low <= block) & (block < high)))
+            def _(block=block):
+                for m in range(micro):
+                    tokens_buf[m, block] = jnp.zeros(own_ref.shape[1:], halves)
     for m in range(micro):
         masks(m)
     for task in head[1:]:
@@ -879,7 +900,7 @@
                     for task in tasks:
                         act[task[0]](*task[1:])
 
-    for source, target in (*keeps, (bias_buf, biases_ref), (mixed_buf, mixed_ref), (turned, turned_ref)):
+    for source, target in (*keeps, (bias_buf, biases_ref), (mixed_buf, mixed_ref), (turned, turned_ref), (mask, mask_ref)):
         done.append(local(source, target))
     for task in tail[-1]:
         act[task[0]](*task[1:])
@@ -888,7 +909,7 @@
     post.close()
 
 
-def forward(sizes, own, shard, bias, seg_own, seg_all):
+def forward(sizes, own, shard, hidden_bias, query_bias, value_bias, segments):
     ns, nr, nc = sizes
     ny = nr // 2
     micro, rows, model = own.shape
@@ -900,36 +921,38 @@
     vmem = pl.BlockSpec(memory_space=pltpu.VMEM)
     length = nc * rows
     arrays = [
-        ((2, nc, ns, ny, 2, rb, w), halves), ((nc, ns, ny, 2, rb, w), halves), ((model, micro * length), halves),
-        ((nc, *bias.shape), floats), ((nc, micro, rows, WINDOW), halves), ((micro, nc, 8, rows), floats),
+        ((2, nc, ns, ny, 2, rb, w), halves), ((nc, ns, ny, 2, rb, w), halves), ((model, micro * length), halves), ((micro, nc, rows, rows), halves),
+        ((nc, 8, model), floats), ((nc, micro, rows, WINDOW), halves), ((micro, nc, 8, rows), floats),
         ((micro, nc, rows, WINDOW), halves), ((micro, nc, nc, rows, WINDOW), halves), ((micro, nc, nc, rows, WINDOW), halves),
     ]
     shapes = [pltpu.VMEM(shape, kind) for shape, kind in arrays]
     return pl.pallas_call(
         functools.partial(forward_kernel, sizes, micro),
         out_shape=[jax.ShapeDtypeStruct(shape, kind) for shape, kind in arrays],
-        in_specs=[vmem] * 5,
+        in_specs=[vmem] * 6,
         out_specs=[anywhere] * len(arrays),
         scratch_shapes=[
             pltpu.VMEM((1, nc, ns, ny, 2, rb, w), halves),
-            shapes[2], shapes[3], pltpu.VMEM((micro, nc, rows, rows), floats), *shapes[4:],
+            shapes[2], shapes[4], shapes[3], *shapes[5:],
             pltpu.VMEM((micro, nc, rows, model), halves), pltpu.VMEM((WINDOW, rows), floats), pltpu.VMEM((8, rows), floats), pltpu.VMEM((8, rows), floats),
             pltpu.SemaphoreType.DMA((count,)), pltpu.SemaphoreType.DMA((count,)), pltpu.SemaphoreType.DMA((20,)),
         ],
         compiler_params=pltpu.CompilerParams(collective_id=2, has_side_effects=True, vmem_limit_bytes=60 << 20),
         name="forward",
-    )(own, shard, bias, seg_own.astype(floats)[:, None], seg_all.astype(floats).reshape(micro, nc, rows))
-
-
-def middle_kernel(cols, own_ref, mixed_ref, out_ref, hidden_ref, down_ref, bias_ref, vector_ref, cot_ref,
-                  outputs_ref, first_grad_ref, attn_grad_ref, part_ref, sums_ref,
-                  normal, scale, normed, normed_low, normed_t, grad_low, grad_t, act_buf, slope_buf, total):
+    )(own, shard, hidden_bias, query_bias, value_bias, segments)
+
+
+def middle_kernel(cols, own_ref, mixed_ref, out_ref, hidden_ref, down_ref, bias_ref, *refs):
+    vector_refs = refs[:6]
+    (cot_ref, outputs_ref, first_grad_ref, attn_grad_ref, part_ref, sums_ref,
+     normal, scale, normed, normed_low, normed_t, grad_low, grad_t, act_buf, slope_buf, total) = refs[6:]
     floats, halves = jnp.float32, jnp.bfloat16
     step = pl.program_id(0)
     rows, model = own_ref.shape
     chunks = [pl.ds(r * 256, 256) for r in range(rows // 256)]
+    whole_rows = [pl.ds(0, rows)]
     bands = [pl.ds(n * 256, 256) for n in range(model // 256)]
-    vector = lambda i: vector_ref[i : i + 1]
+    vector = lambda i: vector_refs[i][...].astype(floats).reshape(1, -1)
 
     @pl.when(step == 0)
     def _():
@@ -985,7 +1008,7 @@
         for n, band in enumerate(bands):
             sums_ref[pl.ds(8 + c, 1), band] = bias_total[n]
         for band in bands:
-            for side in bands:
+            for side in [pl.ds(0, model)]:
                 part_ref[0, 0, side, band] = jnp.dot(normed_t[side, :], slope_buf[c, :, band], preferred_element_type=floats).astype(halves)
                 part_ref[1, 0, side, band] = jnp.dot(grad_t[side, :], act_buf[c, :, band], preferred_element_type=floats).astype(halves)
         for chunk in chunks:
@@ -1019,7 +1042,7 @@
             pl.BlockSpec((1, 1, model, rest.shape[-1]), lambda i: (0, lax.rem(i, cols), 0, 0)),
             pl.BlockSpec((1, 1, model, rest.shape[-1]), lambda i: (1, lax.rem(i, cols), 0, 0)),
             pl.BlockSpec((1, *biases.shape[1:]), lambda i: (lax.rem(i, cols), 0, 0)),
-            whole(vectors.shape), whole((rows, model)),
+            *[whole((model,))] * 6, whole((rows, model)),
         ],
         out_specs=[
             whole((rows, model)), whole((rows, model)), whole((rows, model)),
@@ -1038,7 +1061,7 @@
         ],
         compiler_params=pltpu.CompilerParams(vmem_limit_bytes=56 << 20),
         name="middle",
-    )(own, mixed, first, rest, rest, biases, vectors, cot)
+    )(own, mixed, first, rest, rest, biases, *vectors, cot)
 
 
 class Inbox:
@@ -1050,7 +1073,7 @@
 
 
 def backward_kernel(sizes, micro, grad_ref, share_ref, first_ref, turned_ref, mixed_ref, lse_ref, q_ref, k_ref, v_ref,
-                    segq_ref, segk_ref, part_ref, vec_ref,
+                    mask_ref, part_ref, vec_ref,
                     back_ref, block_ref, sums_ref,
                     mine_buf, core_buf, stage_buf, in_a, in_b, in_c, in_d, in_z, tok_buf, tok_in, vec_buf,
                     weights, mixed_buf, q_buf, k_buf, v_buf, every_t, grad_t, mask, acc, spread, block_sum,
@@ -1064,7 +1087,6 @@
     rows = grad_ref.shape[1]
     reach = -(-(DOC_MOST - 1) // rows)
     parts = [pl.ds(p * half, half) for p in (0, 1)]
-    low, high = jnp.maximum(z - reach, 0), jnp.minimum(z + reach + 1, cols)
     used = [0]
 
     def local(source, target):
@@ -1079,7 +1101,8 @@
     planes = [local(part_ref.at[n // 2, :, :, :, k, rows_of(n)], mine_buf.at[n // 2 + 1, :, :, :, rows_of(n)]) for n in range(4)]
     loads = [local(*pair) for pair in ((first_ref, weights), (mixed_ref, mixed_buf), (q_ref, q_buf), (share_ref, back_ref))]
     loads += [local(k_ref, k_buf), local(v_ref, v_buf)]
-    loads += [local(turned_ref, every_t)]
+    loads += [local(mask_ref, mask)]
+    late = [local(turned_ref, every_t)]
     greet(lines, device)
     post = Post(device, send_sems, recv_sems)
 
@@ -1088,7 +1111,7 @@
             "k", 1 - k, part_ref.at[n // 2, :, :, :, 1 - k, rows_of(n)], core_buf.at[n // 2, :, :, :, rows_of(n)], None))
 
     def plus(target, source):
-        target[...] = (target[...].astype(floats) + source[...].astype(floats)).astype(halves)
+        target[...] = target[...] + source[...]
 
     def plus_grid(target, source, first, second):
         @pl.loop(0, first * second)
@@ -1124,7 +1147,9 @@
     ffn = [Stream(("s", n), n // 2 + 1, 0, cols, rows_of(n)) for n in range(4)]
     ffn_z = [line_z(n, n // 2 + 1, rows_of(n)) for n in range(4)]
     attn = [Stream(("u", c), 0, c, 1, pl.ds(0, rb)) for c in range(cols)]
-    attn_z = line_z("u", 0, pl.ds(0, rb))
+
+    def take_y(c, e):
+        reduce_to(post, ("y", c), "z", lines["z"], c, e, mine_buf.at[0, c, x, y], lambda way, e: in_z.at[0, (1 - way) // 2, e], plus)
 
     def half_of(h):
         return pl.ds(h * (rows // 2), rows // 2)
@@ -1175,23 +1200,6 @@
     small = vec_ref.shape[0]
     vec_buf[0, 0] = jnp.zeros_like(vec_buf[0, 0])
     vec_buf[0, 0, 0:small] = vec_ref[...]
-
-    def masks(m):
-        @pl.loop(low, high)
-        def _(block):
-            same = jnp.broadcast_to(segk_ref[m, pl.ds(block, 1), :], (rows, rows)).T == segq_ref[m, 0:1]
-            mask[m, block] = jnp.where(same, 0.0, MASK_VALUE).astype(halves)
-
-    def clear():
-        for block in range(cols):
-            if block > reach or cols - 1 - block > reach:
-                @pl.when(jnp.logical_not((low <= block) & (block < high)))
-                def _():
-                    @pl.loop(0, micro * cols)
-                    def _(n):
-                        at = (n // cols, lax.rem(n, cols), block)
-                        k_buf[at] = jnp.zeros((rows, WINDOW), halves)
-                        v_buf[at] = jnp.zeros((rows, WINDOW), halves)
 
     def unit(m, c):
         mixed_grad = jnp.dot(grad_ref[m], weights[c, :, O_AT : O_AT + WINDOW], preferred_element_type=floats).astype(halves)
@@ -1232,7 +1240,9 @@
             spread[m, block] += contract_cols(key_low, key_weight) + contract_cols(value_low, value_weight)
             return value_bias + jnp.sum(value_low.astype(floats), 0, keepdims=True)
 
-        value_bias = lax.fori_loop(low, high, step, jnp.zeros((1, WINDOW), floats))
+        value_bias = jnp.zeros((1, WINDOW), floats)
+        for block in range(cols):
+            value_bias = step(block, value_bias)
         query_low = (acc[...].T * HEAD_DIM ** -0.5).astype(halves)
         q_buf[m, c] = query_low
         vec_buf[0, 0, pl.ds(small + c, 1), 0:WINDOW] += jnp.sum(query_low.astype(floats), 0, keepdims=True)
@@ -1242,7 +1252,7 @@
     def send_tokens(m):
         back_ref[m] += spread[m, z]
 
-        @pl.loop(low, high)
+        @pl.loop(0, cols)
         def _(block):
             tok_buf[m, block] = spread[m, block].astype(halves)
 
@@ -1337,12 +1347,10 @@
     def load():
         for copy in loads:
             copy.wait()
-        clear()
 
     act = {
         "L": load, "G": lambda n: give(n) if n < 4 else attn_give(n - 4), "A": take_core, "B": take_second, "C": take_third,
-        "Z": lambda n, e: along(ffn_z[n], e), "S": send_tokens, "T": take_tokens, "Ys": lambda: start(attn_z),
-        "Y": lambda e: along(attn_z, e), "V": vectors,
+        "Z": lambda n, e: along(ffn_z[n], e), "S": send_tokens, "T": take_tokens, "Y": take_y, "V": vectors,
     }
     head, tail, order = split_plan([("U", "W", task[1], 0) if task[0] == "W" else task for task in BACKWARD_PLAN])
     kinds = [item[0] == "W" for item in order]
@@ -1351,7 +1359,6 @@
     act[head[0][0]](*head[0][1:])
     spread[...] = jnp.zeros_like(spread)
     for m in range(micro):
-        masks(m)
         grad_t[:, m * rows : (m + 1) * rows] = grad_ref[m].T
     for task in head[1:]:
         act[task[0]](*task[1:])
@@ -1366,6 +1373,11 @@
 
         @pl.when(kind == 1)
         def _():
+            @pl.when(step == kinds.index(True))
+            def _():
+                for copy in late:
+                    copy.wait()
+
             weight_grads(c)
 
         for i, tasks in enumerate(tail[:-1]):
@@ -1382,7 +1394,7 @@
     post.close()
 
 
-def backward(sizes, grad, share, first, turned, mixed, lse, q, k, v, seg_own, seg_all, part, vectors):
+def backward(sizes, grad, share, first, turned, mixed, lse, q, k, v, mask, part, vectors):
     ns, nr, nc = sizes
     ny = nr // 2
     micro, rows, model = grad.shape
@@ -1391,7 +1403,7 @@
     halves, floats = jnp.bfloat16, jnp.float32
     reach = min(nc - 1, -(-(DOC_MOST - 1) // rows))
     streams = 4 + nc
-    count = 4 + nc + 4 * (ny - 1 + ns - 1) * streams + 5 * 2 * (nc - 1) + micro * 4 * reach + (1 + ny - 1 + ns - 1 + nc - 1)
+    count = 4 + nc + 4 * (ny - 1 + ns - 1) * streams + 4 * 2 * (nc - 1) + 2 * nc * 2 + micro * 4 * reach + (1 + ny - 1 + ns - 1 + nc - 1)
     widest = max(ns, ny, nc, 2)
     ways = lambda n: 1 if n == 2 else 2
     vec_shape = (vectors.shape[0] + nc + -nc % 8, model)
@@ -1405,7 +1417,7 @@
             jax.ShapeDtypeStruct((3, rb, w), floats),
             jax.ShapeDtypeStruct(vec_shape, floats),
         ],
-        in_specs=[vmem, anywhere, anywhere, anywhere, anywhere, vmem, anywhere, anywhere, anywhere, vmem, vmem, anywhere, vmem],
+        in_specs=[vmem, anywhere, anywhere, anywhere, anywhere, vmem, anywhere, anywhere, anywhere, anywhere, anywhere, vmem],
         out_specs=[vmem] * 3,
         scratch_shapes=[
             buf(3, nc, ns, ny, rb, w), buf(2, nc, ns, ny, rb, w), buf(nc, ns, ny, rb, w),
@@ -1421,7 +1433,7 @@
         ],
         compiler_params=pltpu.CompilerParams(collective_id=3, has_side_effects=True, vmem_limit_bytes=62 << 20),
         name="backward",
-    )(grad, share, first, turned, mixed, lse, q, k, v, seg_own.astype(floats)[:, None], seg_all.astype(floats).reshape(micro, nc, rows),
+    )(grad, share, first, turned, mixed, lse, q, k, v, mask,
       part.reshape(2, nc, ns, ny, 2, rb, w), vectors)
 
 
@@ -1538,21 +1550,16 @@
         hidden_weight,
         down_weight.T,
     ])
-    pad = lambda vector: jnp.pad(vector.astype(floats), (0, model - vector.shape[0]))
-    bias = jnp.stack([pad(hidden_bias), pad(query_bias), pad(value_bias)] + [jnp.zeros((model,), floats)] * 5)
-    seg_all = segment_ids[:, 0]
-    seg_own = lax.dynamic_slice_in_dim(seg_all, here * rows, rows, 1)
-    rest, first, turned, biases, mixed, lse, q, k, v = forward(sizes, own, shard, bias, seg_own, seg_all)
+    rest, first, turned, mask, biases, mixed, lse, q, k, v = forward(sizes, own, shard, hidden_bias, query_bias, value_bias, segment_ids)
     first = first.reshape(cols, model, 4 * width)
     total = micro * rows
     flat = lambda a: a.reshape(total, -1)
-    vectors = jnp.stack([a.astype(floats) for a in (output_bias, first_gain, first_shift, down_bias, second_gain, second_shift)]
-                        + [jnp.zeros((model,), floats)] * 2)
     outputs, first_grad, attn_grad, part, sums = middle(
-        flat(own), mixed.reshape(cols, total, WINDOW), first, rest.reshape(2, cols, model, -1), biases, vectors, flat(cotangent[:, 0]))
+        flat(own), mixed.reshape(cols, total, WINDOW), first, rest.reshape(2, cols, model, -1), biases,
+        (output_bias, first_gain, first_shift, down_bias, second_gain, second_shift), flat(cotangent[:, 0]))
     parted = lambda a: a.reshape(micro, rows, model)
     input_grad, reduced, sums = backward(sizes, parted(attn_grad), parted(first_grad), first, turned, mixed, lse, q, k, v,
-                                         seg_own, seg_all, part, sums)
+                                         mask, part, sums)
     piece = lambda i: reduced[0, :, i * width : (i + 1) * width]
     mine = lambda first_row, at, size: lax.dynamic_slice(sums, (first_row + here, at), (1, size))[0]
     heads_at = sums.shape[0] - (cols + -cols % 8)

time: 260 us -> 242 us (0.931)
  Pallas kernels: 235 us -> 227 us
  local copies, waits for them, and re-layouts: 17.6 us -> 10.9 us
  other arithmetic: 6.06 us -> 2.75 us
    pallas_call x1, Pallas kernels: 111 us -> 102 us  [backward(): pl.pallas_call(functools.partial(backward_kernel, sizes, micro), out_shap...]
    another operation x14 -> x0, local copies, waits for them, and re-layouts: 6.1 us -> none  [the longest x8 4.76 us: per_device_fused(): jnp.stack([a.astype(floats) for a in (output_bias, first_gain, first_shif...]
where the time goes in v5:
time: 242 us; the launch traced here: 241 us
  Pallas kernels  227 us (94%)
  local copies, waits for them, and re-layouts  10.9 us (5%)
  other arithmetic  2.75 us (1%)
    pallas_call x1, Pallas kernels, backward(): pl.pallas_call(functools.partial(backward_kernel, sizes, micro), out_shap...  102 us
    pallas_call x1, Pallas kernels, forward(): pl.pallas_call(functools.partial(forward_kernel, sizes, micro), out_shape...  96.9 us
    pallas_call x1, Pallas kernels, middle(): pl.pallas_call(functools.partial(middle_kernel, cols), grid=(2 * cols,),...  28.1 us

profile of v5, /device:TPU:0, one launch (start us, length us, event | category | flops | bytes accessed | tf_op | source)
XLA Modules:
  0.0 241.2 jit_solution(5569074243718051064)
XLA Ops:
  0.7 0.9 copy.35
  1.5 1.0 maximum_bitcast_fusion
  2.5 1.8 pad_maximum_fusion.shard_ref
  4.3 96.9 %forward.1 = (bf16[2,4,2,2,2,96,768]{6,5,4,3,2,1,0:T(8,128)(2,1)}, bf16[4,2,2,2,96,768]{5,4,3,2,1,0:T(8,128)(2,1)}, bf16[768,2048]{1,0:T(8,128)(2,1)}, bf16[2,4,...) custom-call(bf16[2,256,768]{2,1,0:T(8,128)(2,1)} %bitcast.46, ...), custom_call_target="tpu_custom_call" | custom-call | tf_op jit(solution)/shard_map/forward/pallas_call | solution.py:929
  101.2 28.1 %middle.1 = (bf16[512,768]{1,0:T(8,128)(2,1)}, f32[512,768]{1,0:T(8,128)}, bf16[512,768]{1,0:T(8,128)(2,1)}, bf16[2,4,768,768]{3,2,1,0:T(8,128)(2,1)}, f32[16,768]{1,0:T(8,128)}) custom-call(bf16[512,768]{1,0:T(8,128)(2,1)} %bitcast.47, bf16[4,512,256]{2,1,0:T(8,128)(2,1)} %bitcast.45, bf16[4,768,768]{2,1,0:T(8,128)(2,1)} %bitcast.42, ...), custom_call_target="tpu_custom_call" | custom-call | tf_op jit(solution)/shard_map/middle/pallas_call | solution.py:1036
  129.3 101.8 %backward.1 = (f32[2,256,768]{2,1,0:T(8,128)}, f32[3,96,768]{2,1,0:T(8,128)}, f32[24,768]{1,0:T(8,128)}) custom-call(bf16[2,256,768]{2,1,0:T(8,128)(2,1)} %bitcast.51, f32[2,256,768]{2,1,0:T(8,128)} %bitcast.48, bf16[4,768,768]{2,1,0:T(8,128)(2,1)} %bitcast.43, bf16[768,2048]{1,0:T(8,128)(2,1)} %get-tuple-element.42.turned_ref, ...), custom_call_target="tpu_custom_call" | custom-call | tf_op jit(solution)/shard_map/backward/pallas_call | solution.py:1413
  231.1 1.9 slice_bitcast_fusion
  233.0 1.8 slice_bitcast_fusion.2
  234.9 0.7 copy.38
  235.6 1.6 slice_reduce_fusion
  237.2 1.3 constant_dynamic-slice_fusion
  238.5 2.7 %copy.40 = f32[2,1,256,768]{3,2,1,0:T(8,128)} copy(f32[2,1,256,768]{3,2,1,0:T(8,128)} %bitcast.49) | data formatting | bytes 3145728

commit v6 on v5

--- a/solution.py
+++ b/solution.py
@@ -48,16 +48,16 @@
     ("U", 1, 0), ("K", 3), ("K", 4), ("B", 5), ("U", 1, 1), ("U", 1, 2), ("C", 5), ("U", 1, 3), ("K", 5),
 )
 BACKWARD_PLAN = (
-    ("L",), ("G", 0), ("G", 2), ("U", 1, 0), ("A", 0), ("U", 0, 0), ("U", 2, 0), ("B", 0), ("A", 2), ("G", 1),
-    ("G", 3), ("U", 3, 0), ("C", 0), ("S", 0), ("U", 2, 1), ("B", 2), ("U", 0, 1), ("Z", 0, 2), ("A", 1), ("A", 3),
-    ("C", 2), ("T", 0, 1, 1), ("T", 0, 0, 1), ("U", 1, 1), ("U", 3, 1), ("S", 1), ("B", 1), ("V", 0), ("W", 2),
-    ("V", 1), ("B", 3), ("G", 6), ("Z", 2, 2), ("W", 0), ("G", 4), ("V", 2), ("A", 6), ("C", 1), ("W", 3),
-    ("T", 1, 0, 1), ("G", 7), ("A", 4), ("W", 1), ("G", 5), ("A", 7), ("T", 1, 1, 1), ("B", 6), ("C", 3), ("A", 5),
-    ("Z", 2, 1), ("T", 0, 1, 0), ("Z", 1, 2), ("Z", 3, 2), ("B", 4), ("V", 3), ("Z", 0, 1), ("B", 7), ("B", 5),
-    ("Z", 2, 0), ("C", 6), ("C", 4), ("T", 1, 0, 0), ("C", 7), ("Y", 3, 3), ("Y", 2, 2), ("Y", 0, 3), ("Z", 1, 1),
-    ("T", 0, 0, 0), ("C", 5), ("Y", 1, 2), ("V", 4), ("Y", 3, 2), ("Y", 2, 1), ("Y", 0, 2), ("Z", 3, 1), ("Z", 1, 0),
-    ("Y", 0, 1), ("T", 1, 1, 0), ("Y", 1, 1), ("Y", 3, 1), ("Z", 0, 0), ("Y", 2, 0), ("Z", 3, 0), ("Y", 0, 0),
-    ("Y", 3, 0), ("Y", 1, 0),
+    ("L",), ("G", 2), ("G", 1), ("G", 0), ("U", 0, 0), ("U", 1, 0), ("G", 3), ("A", 0), ("A", 2), ("U", 3, 0),
+    ("U", 2, 0), ("S", 0), ("B", 0), ("U", 2, 1), ("B", 2), ("A", 1), ("T", 0, 0, 1), ("U", 0, 1), ("C", 0), ("A", 3),
+    ("C", 2), ("T", 0, 1, 1), ("U", 1, 1), ("Z", 2, 2), ("U", 3, 1), ("S", 1), ("B", 1), ("V", 0), ("B", 3), ("W", 2),
+    ("G", 6), ("W", 0), ("C", 1), ("V", 1), ("A", 6), ("G", 4), ("Z", 0, 2), ("W", 3), ("A", 4), ("V", 2), ("G", 7),
+    ("T", 1, 0, 1), ("W", 1), ("C", 3), ("G", 5), ("A", 7), ("T", 1, 1, 1), ("A", 5), ("Z", 0, 1), ("B", 4), ("B", 7),
+    ("Z", 1, 2), ("Z", 2, 1), ("V", 3), ("B", 5), ("C", 4), ("Z", 1, 1), ("B", 6), ("Z", 2, 0), ("T", 0, 0, 0),
+    ("C", 7), ("Y", 3, 3), ("Y", 0, 3), ("Z", 3, 2), ("C", 5), ("T", 1, 0, 0), ("C", 6), ("Y", 2, 2), ("Y", 1, 2),
+    ("V", 4), ("Y", 0, 2), ("Y", 3, 2), ("Z", 3, 1), ("Z", 1, 0), ("T", 1, 1, 0), ("Y", 1, 1), ("Y", 3, 1),
+    ("Y", 2, 1), ("Y", 0, 1), ("Z", 3, 0), ("Z", 0, 0), ("T", 0, 1, 0), ("Y", 2, 0), ("Y", 0, 0), ("Y", 3, 0),
+    ("Y", 1, 0),
 )
 def attend_kernel(bounds, own_ref, all_ref, wq_ref, wk_ref, wv_ref, bq_ref, bv_ref,
                   segq_ref, segk_ref, mixed_ref, lse_ref, q_ref, k_ref, v_ref, bias, acc, top, total):
@@ -718,28 +718,39 @@
     return jnp.where(places == wanted, value, jnp.zeros_like(value))
 
 
-def forward_kernel(sizes, micro, own_ref, shard_ref, hidden_bias_ref, query_bias_ref, value_bias_ref, seg_ref,
+def forward_kernel(sizes, micro, own_ref, wq_ref, wk_ref, wv_ref, wo_ref, wh_ref, wd_ref, hidden_bias_ref, query_bias_ref, value_bias_ref, seg_ref,
                    rest_ref, first_ref, turned_ref, mask_ref, biases_ref, mixed_ref, lse_ref, q_ref, k_ref, v_ref,
                    weights, turned, bias_buf, mask, mixed_buf, lse_buf, q_buf, k_buf, v_buf, tokens_buf, acc, top, total,
-                   send_sems, recv_sems, local_sems):
+                   send_sems, recv_sems, local_sems, unit_sems, turn_buf):
     floats, halves = jnp.float32, jnp.bfloat16
     lines, device = place(sizes)
     (x, _), (y, _), (k, _), (z, cols) = (lines[a] for a in "xykz")
-    half = shard_ref.shape[-1] // 2
+    half = wh_ref.shape[-1] // 2
     rows = own_ref.shape[1]
     reach = -(-(DOC_MOST - 1) // rows)
     parts = [pl.ds(p * half, half) for p in (0, 1)]
     low, high = jnp.maximum(z - reach, 0), jnp.minimum(z + reach + 1, cols)
     used = [0]
 
-    def local(source, target):
-        copy = pltpu.make_async_copy(source, target, local_sems.at[used[0]])
-        used[0] += 1
-        copy.start()
-        return copy
-
+    class Local:
+        def __init__(self, source, target):
+            self.source, self.target, self.n = source, target, used[0]
+            used[0] += 1
+            self.describe().start()
+
+        def describe(self):
+            source = self.source() if callable(self.source) else self.source
+            return pltpu.make_async_copy(source, self.target, local_sems.at[self.n])
+
+        def wait(self):
+            self.describe().wait()
+
+    local = Local
     targets = [weights.at[0], rest_ref.at[0], rest_ref.at[1]]
-    begin = [local(shard_ref.at[j], targets[j].at[z, x, y, k]) for j in range(3)]
+    packed = [wq_ref[...], wk_ref[...], wv_ref[...], wo_ref[...].astype(floats).T.astype(halves)]
+    weights[0, z, x, y, k] = jnp.concatenate(packed, 1)
+    turn_buf[...] = wd_ref[...].astype(floats).T.astype(halves)
+    begin = [local(wh_ref, targets[1].at[z, x, y, k]), local(turn_buf, targets[2].at[z, x, y, k])]
     begin += [local(own_ref.at[m], tokens_buf.at[m, z]) for m in range(micro)]
     for i, ref in enumerate((hidden_bias_ref, query_bias_ref, value_bias_ref)):
         bias_buf[z, i : i + 1, 0 : ref.shape[0]] = ref[...].astype(floats).reshape(1, -1)
@@ -755,7 +766,7 @@
         for q in range(2 * micro)
     ]
     small = LineGather(post, "bias", "z", lines["z"], lambda i: bias_buf.at[i])
-    rb = shard_ref.shape[1]
+    rb = wh_ref.shape[0]
     zs, second, third = {}, {}, {}
     for n in range(6):
         j, r = n // 2, pl.ds(n % 2 * (rb // 2), rb // 2)
@@ -842,11 +853,14 @@
             same = jnp.broadcast_to(asked, (rows, rows)).T == asking
             mask[m, block] = jnp.where(same, 0.0, MASK_VALUE).astype(halves)
 
+    done = []
+
     def turn(m):
         for block in range(cols):
             turned[:, (m * cols + block) * rows : (m * cols + block + 1) * rows] = tokens_buf[m, block].T
-
-    done = []
+        if m == micro - 1:
+            done.append(local(turned, turned_ref))
+
     keeps = ((q_buf, q_ref), (k_buf, k_ref), (v_buf, v_ref), (lse_buf, lse_ref))
 
     def take_z(n, t):
@@ -870,7 +884,7 @@
         swapped(n)
         swaps.add(n)
         if n < 2 and swaps >= {0, 1}:
-            done.append(local(weights.at[0], first_ref))
+            done.append(local(lambda: weights.at[0], first_ref))
 
     act = {
         "Zs": lambda n: zs[n].start(), "Z": take_z, "Ts": lambda q: tokens[q].start(), "T": lambda q, t: tokens[q].step(t),
@@ -890,9 +904,15 @@
     for task in head[1:]:
         act[task[0]](*task[1:])
 
+    def leave(m, c, step, go):
+        for i, (source, target) in enumerate(keeps):
+            go(pltpu.make_async_copy(source.at[m, c], target.at[m, c], unit_sems.at[i, step]))
+
     @pl.loop(0, len(order))
     def _(step):
-        unit(pick(step, [m for m, _ in order]), pick(step, [c for _, c in order]))
+        m, c = pick(step, [m for m, _ in order]), pick(step, [c for _, c in order])
+        unit(m, c)
+        leave(m, c, step, lambda copy: copy.start())
         for i, tasks in enumerate(tail[:-1]):
             if tasks:
                 @pl.when(step == i)
@@ -900,20 +920,22 @@
                     for task in tasks:
                         act[task[0]](*task[1:])
 
-    for source, target in (*keeps, (bias_buf, biases_ref), (mixed_buf, mixed_ref), (turned, turned_ref), (mask, mask_ref)):
+    for source, target in ((bias_buf, biases_ref), (mixed_buf, mixed_ref), (mask, mask_ref)):
         done.append(local(source, target))
     for task in tail[-1]:
         act[task[0]](*task[1:])
+    for step, (m, c) in enumerate(order):
+        leave(m, c, step, lambda copy: copy.wait())
     for copy in done:
         copy.wait()
     post.close()
 
 
-def forward(sizes, own, shard, hidden_bias, query_bias, value_bias, segments):
+def forward(sizes, own, shards, hidden_bias, query_bias, value_bias, segments):
     ns, nr, nc = sizes
     ny = nr // 2
     micro, rows, model = own.shape
-    _, rb, w = shard.shape
+    rb, w = shards[4].shape
     halves, floats = own.dtype, jnp.float32
     reach = min(nc - 1, -(-(DOC_MOST - 1) // rows))
     count = (6 + 1) * 2 * (nc - 1) + micro * 4 * reach + 6 * (4 * (ny - 1) + 4 * (ns - 1) + 1)
@@ -929,17 +951,17 @@
     return pl.pallas_call(
         functools.partial(forward_kernel, sizes, micro),
         out_shape=[jax.ShapeDtypeStruct(shape, kind) for shape, kind in arrays],
-        in_specs=[vmem] * 6,
+        in_specs=[vmem] * 11,
         out_specs=[anywhere] * len(arrays),
         scratch_shapes=[
             pltpu.VMEM((1, nc, ns, ny, 2, rb, w), halves),
             shapes[2], shapes[4], shapes[3], *shapes[5:],
             pltpu.VMEM((micro, nc, rows, model), halves), pltpu.VMEM((WINDOW, rows), floats), pltpu.VMEM((8, rows), floats), pltpu.VMEM((8, rows), floats),
-            pltpu.SemaphoreType.DMA((count,)), pltpu.SemaphoreType.DMA((count,)), pltpu.SemaphoreType.DMA((20,)),
+            pltpu.SemaphoreType.DMA((count,)), pltpu.SemaphoreType.DMA((count,)), pltpu.SemaphoreType.DMA((20,)), pltpu.SemaphoreType.DMA((4, micro * nc)), pltpu.VMEM((rb, w), halves),
         ],
         compiler_params=pltpu.CompilerParams(collective_id=2, has_side_effects=True, vmem_limit_bytes=60 << 20),
         name="forward",
-    )(own, shard, hidden_bias, query_bias, value_bias, segments)
+    )(own, *shards, hidden_bias, query_bias, value_bias, segments)
 
 
 def middle_kernel(cols, own_ref, mixed_ref, out_ref, hidden_ref, down_ref, bias_ref, *refs):
@@ -1535,6 +1557,42 @@
     )
 
 
+def deliver_kernel(sizes, width, back_ref, block_ref, sums_ref, *outs):
+    (input_grad, query, key, value, query_bias, value_bias, output, output_bias, first_gain, first_shift, hidden, hidden_bias, down,
+     down_bias, second_gain, second_shift) = outs
+    here = lax.axis_index("col")
+    input_grad[...] = back_ref[...]
+    for i, ref in enumerate((query, key, value)):
+        ref[...] = block_ref[0, :, i * width : (i + 1) * width]
+    output[...] = block_ref[0, :, 3 * width : 4 * width].T
+    hidden[...] = block_ref[1]
+    down[...] = block_ref[2].T
+    for i, ref in enumerate((output_bias, first_gain, first_shift, down_bias, second_gain, second_shift)):
+        ref[...] = sums_ref[i : i + 1].reshape(-1)
+    hidden_bias[...] = sums_ref[pl.ds(8 + here, 1)].reshape(-1)
+    heads_at = sums_ref.shape[0] - (sizes[2] + -sizes[2] % 8)
+    row = sums_ref[pl.ds(heads_at + here, 1)]
+    query_bias[...] = row[:, 0:width].reshape(-1)
+    value_bias[...] = row[:, WINDOW : WINDOW + width].reshape(-1)
+
+
+def deliver(sizes, width, back, blocks, sums):
+    model = sums.shape[1]
+    _, rb, w = blocks.shape
+    vmem = pl.BlockSpec(memory_space=pltpu.VMEM)
+    square, vector = (rb, width), (model,)
+    shapes = [back.shape, square, square, square, (width,), (width,), (width, rb), vector, vector, vector, (rb, w), (w,), (w, rb),
+              vector, vector, vector]
+    return pl.pallas_call(
+        functools.partial(deliver_kernel, sizes, width),
+        out_shape=[jax.ShapeDtypeStruct(shape, jnp.float32) for shape in shapes],
+        in_specs=[vmem] * 3,
+        out_specs=[vmem] * len(shapes),
+        compiler_params=pltpu.CompilerParams(vmem_limit_bytes=32 << 20),
+        name="deliver",
+    )(back, blocks, sums)
+
+
 def per_device_fused(sizes, inputs, segment_ids, query_weight, key_weight, value_weight, query_bias, value_bias,
                output_weight, output_bias, first_gain, first_shift, hidden_weight, hidden_bias, down_weight,
                down_bias, second_gain, second_shift, cotangent):
@@ -1545,12 +1603,8 @@
     width = query_weight.shape[1]
     here = lax.axis_index("col")
     own = inputs[:, 0]
-    shard = jnp.stack([
-        jnp.concatenate([query_weight, key_weight, value_weight, output_weight.T], 1),
-        hidden_weight,
-        down_weight.T,
-    ])
-    rest, first, turned, mask, biases, mixed, lse, q, k, v = forward(sizes, own, shard, hidden_bias, query_bias, value_bias, segment_ids)
+    rest, first, turned, mask, biases, mixed, lse, q, k, v = forward(
+        sizes, own, (query_weight, key_weight, value_weight, output_weight, hidden_weight, down_weight), hidden_bias, query_bias, value_bias, segment_ids)
     first = first.reshape(cols, model, 4 * width)
     total = micro * rows
     flat = lambda a: a.reshape(total, -1)
@@ -1560,15 +1614,8 @@
     parted = lambda a: a.reshape(micro, rows, model)
     input_grad, reduced, sums = backward(sizes, parted(attn_grad), parted(first_grad), first, turned, mixed, lse, q, k, v,
                                          mask, part, sums)
-    piece = lambda i: reduced[0, :, i * width : (i + 1) * width]
-    mine = lambda first_row, at, size: lax.dynamic_slice(sums, (first_row + here, at), (1, size))[0]
-    heads_at = sums.shape[0] - (cols + -cols % 8)
-    return (
-        outputs.reshape(micro, 1, rows, model), input_grad[:, None],
-        piece(0), piece(1), piece(2), mine(heads_at, 0, width), mine(heads_at, WINDOW, width), piece(3).T,
-        sums[0], sums[1], sums[2], reduced[1], mine(8, 0, hidden_bias.shape[0]), reduced[2].T,
-        sums[3], sums[4], sums[5],
-    )
+    grads = deliver(sizes, width, input_grad, reduced, sums)
+    return (outputs.reshape(micro, 1, rows, model), grads[0][:, None], *grads[1:])
 
 
 def per_device(sizes, inputs, segment_ids, query_weight, *rest):

time: 242 us -> 232 us (0.959)
  local copies, waits for them, and re-layouts: 10.9 us -> 6.05 us
  other arithmetic: 2.75 us -> 0 us
    transpose x2 -> x0, local copies, waits for them, and re-layouts: 3.74 us -> none  [the longest x1 1.9 us: per_device_fused(): reduced[2]]
    pallas_call x1, Pallas kernels: 96.9 us -> 93.4 us  [forward(): pl.pallas_call(functools.partial(forward_kernel, sizes, micro), out_shape...]
    another operation x2 -> x0, other arithmetic: 2.75 us -> none  [per_device_fused(): jnp.stack([jnp.concatenate([query_weight, key_weight, value_weight, outpu...]
    unnamed x3 -> x8, local copies, waits for them, and re-layouts: 4.28 us -> 6.05 us
where the time goes in v6:
time: 232 us; the launch traced here: 231 us
  Pallas kernels  225 us (97%)
  local copies, waits for them, and re-layouts  6.05 us (3%)
    pallas_call x1, Pallas kernels, backward(): pl.pallas_call(functools.partial(backward_kernel, sizes, micro), out_shap...  101 us
    pallas_call x1, Pallas kernels, forward(): pl.pallas_call(functools.partial(forward_kernel, sizes, micro), out_shape...  93.4 us
    pallas_call x1, Pallas kernels, middle(): pl.pallas_call(functools.partial(middle_kernel, cols), grid=(2 * cols,),...  28.1 us
    unnamed x8, local copies, waits for them, and re-layouts  6.05 us

profile of v6, /device:TPU:0, one launch (start us, length us, event | category | flops | bytes accessed | tf_op | source)
XLA Modules:
  0.0 231.3 jit_solution(4739840026055675661)
XLA Ops:
  0.7 1.7 copy.35.wd_ref
  2.4 93.4 %forward.1 = (bf16[2,4,2,2,2,96,768]{6,5,4,3,2,1,0:T(8,128)(2,1)}, bf16[4,2,2,2,96,768]{5,4,3,2,1,0:T(8,128)(2,1)}, bf16[768,2048]{1,0:T(8,128)(2,1)}, bf16[2,4,...) custom-call(bf16[2,256,768]{2,1,0:T(8,128)(2,1)} %bitcast.21, ...), custom_call_target="tpu_custom_call" | custom-call | tf_op jit(solution)/shard_map/forward/pallas_call | solution.py:951
  95.8 28.1 %middle.1 = (bf16[512,768]{1,0:T(8,128)(2,1)}, f32[512,768]{1,0:T(8,128)}, bf16[512,768]{1,0:T(8,128)(2,1)}, bf16[2,4,768,768]{3,2,1,0:T(8,128)(2,1)}, f32[16,768]{1,0:T(8,128)}) custom-call(bf16[512,768]{1,0:T(8,128)(2,1)} %bitcast.22, bf16[4,512,256]{2,1,0:T(8,128)(2,1)} %bitcast.20, bf16[4,768,768]{2,1,0:T(8,128)(2,1)} %bitcast.17, ...), custom_call_target="tpu_custom_call" | custom-call | tf_op jit(solution)/shard_map/middle/pallas_call | solution.py:1058
  123.9 101.4 %backward.1 = (f32[2,256,768]{2,1,0:T(8,128)}, f32[3,96,768]{2,1,0:T(8,128)}, f32[24,768]{1,0:T(8,128)}) custom-call(bf16[2,256,768]{2,1,0:T(8,128)(2,1)} %bitcast.25, f32[2,256,768]{2,1,0:T(8,128)} %bitcast.23, bf16[4,768,768]{2,1,0:T(8,128)(2,1)} %bitcast.18, bf16[768,2048]{1,0:T(8,128)(2,1)} %get-tuple-element.58.turned_ref, ...), custom_call_target="tpu_custom_call" | custom-call | tf_op jit(solution)/shard_map/backward/pallas_call | solution.py:1435
  225.3 0.0 copy-start
  225.3 1.4 copy-done
  226.7 0.0 copy-start.1
  226.7 1.2 copy-done.1
  227.9 0.0 copy-start.2
  227.9 0.9 copy-done.2
  228.8 1.6 deliver.1
  230.4 0.9 copy.38
Async XLA Ops:
  225.3 1.4 copy-start
  226.7 1.2 copy-start.1
  227.9 0.9 copy-start.2

commit v7 on v6

--- a/solution.py
+++ b/solution.py
@@ -39,25 +39,25 @@
     )
 
 FORWARD_PLAN = (
-    ("Zs", 1), ("Zs", 0), ("Zs", 3), ("Z", 1, 1), ("Z", 0, 1), ("Zs", 2), ("Z", 1, 2), ("Zs", 4), ("Z", 1, 3),
-    ("Z", 0, 2), ("Z", 0, 3), ("Z", 2, 1), ("Z", 4, 1), ("Ts", 1), ("Z", 2, 2), ("B", 1), ("Z", 3, 1), ("Ts", 0),
-    ("Z", 4, 2), ("B", 0), ("T", 1, 1), ("T", 0, 1), ("Z", 2, 3), ("Z", 3, 2), ("Ts", 3), ("C", 1), ("C", 0),
-    ("Ts", 2), ("Z", 4, 3), ("K", 0), ("B", 2), ("T", 1, 2), ("T", 0, 2), ("R", 0), ("Zs", 5), ("K", 1), ("Z", 3, 3),
-    ("B", 4), ("U", 0, 0), ("T", 3, 1), ("U", 0, 1), ("B", 3), ("U", 0, 2), ("T", 2, 1), ("C", 2), ("T", 3, 2),
-    ("Z", 5, 1), ("C", 4), ("U", 0, 3), ("T", 2, 2), ("R", 1), ("C", 3), ("Z", 5, 2), ("K", 2), ("Z", 5, 3),
-    ("U", 1, 0), ("K", 3), ("K", 4), ("B", 5), ("U", 1, 1), ("U", 1, 2), ("C", 5), ("U", 1, 3), ("K", 5),
+    ("Zs", 1), ("Zs", 3), ("Zs", 0), ("Z", 1, 1), ("Z", 3, 1), ("Z", 1, 2), ("Z", 1, 3), ("Zs", 2), ("Z", 3, 2),
+    ("Zs", 5), ("Z", 3, 3), ("Z", 0, 1), ("B", 1), ("Z", 0, 2), ("Z", 0, 3), ("Z", 2, 1), ("Zs", 4), ("Ts", 0),
+    ("Z", 2, 2), ("Z", 5, 1), ("B", 3), ("Z", 5, 2), ("Ts", 1), ("B", 0), ("Z", 2, 3), ("Z", 4, 1), ("T", 0, 1),
+    ("T", 0, 2), ("Z", 4, 2), ("T", 1, 1), ("Z", 5, 3), ("Ts", 2), ("Z", 4, 3), ("C", 1), ("C", 0), ("C", 3),
+    ("B", 5), ("Ts", 3), ("K", 1), ("T", 1, 2), ("R", 0), ("K", 0), ("U", 0, 0), ("B", 2), ("T", 2, 1), ("U", 0, 1),
+    ("C", 5), ("T", 3, 1), ("U", 0, 2), ("K", 3), ("B", 4), ("U", 0, 3), ("T", 2, 2), ("K", 5), ("C", 2), ("T", 3, 2),
+    ("R", 1), ("U", 1, 0), ("U", 1, 1), ("C", 4), ("U", 1, 2), ("U", 1, 3), ("K", 2), ("K", 4),
 )
 BACKWARD_PLAN = (
-    ("L",), ("G", 2), ("G", 1), ("G", 0), ("U", 0, 0), ("U", 1, 0), ("G", 3), ("A", 0), ("A", 2), ("U", 3, 0),
-    ("U", 2, 0), ("S", 0), ("B", 0), ("U", 2, 1), ("B", 2), ("A", 1), ("T", 0, 0, 1), ("U", 0, 1), ("C", 0), ("A", 3),
-    ("C", 2), ("T", 0, 1, 1), ("U", 1, 1), ("Z", 2, 2), ("U", 3, 1), ("S", 1), ("B", 1), ("V", 0), ("B", 3), ("W", 2),
-    ("G", 6), ("W", 0), ("C", 1), ("V", 1), ("A", 6), ("G", 4), ("Z", 0, 2), ("W", 3), ("A", 4), ("V", 2), ("G", 7),
-    ("T", 1, 0, 1), ("W", 1), ("C", 3), ("G", 5), ("A", 7), ("T", 1, 1, 1), ("A", 5), ("Z", 0, 1), ("B", 4), ("B", 7),
-    ("Z", 1, 2), ("Z", 2, 1), ("V", 3), ("B", 5), ("C", 4), ("Z", 1, 1), ("B", 6), ("Z", 2, 0), ("T", 0, 0, 0),
-    ("C", 7), ("Y", 3, 3), ("Y", 0, 3), ("Z", 3, 2), ("C", 5), ("T", 1, 0, 0), ("C", 6), ("Y", 2, 2), ("Y", 1, 2),
-    ("V", 4), ("Y", 0, 2), ("Y", 3, 2), ("Z", 3, 1), ("Z", 1, 0), ("T", 1, 1, 0), ("Y", 1, 1), ("Y", 3, 1),
-    ("Y", 2, 1), ("Y", 0, 1), ("Z", 3, 0), ("Z", 0, 0), ("T", 0, 1, 0), ("Y", 2, 0), ("Y", 0, 0), ("Y", 3, 0),
-    ("Y", 1, 0),
+    ("G", 1), ("G", 3), ("L",), ("U", 2, 0), ("A", 1), ("G", 0), ("U", 0, 0), ("A", 3), ("U", 1, 0), ("U", 3, 0),
+    ("S", 0), ("G", 2), ("B", 1), ("A", 0), ("U", 0, 1), ("A", 2), ("B", 3), ("T", 0, 0, 1), ("C", 1), ("U", 2, 1),
+    ("U", 1, 1), ("T", 0, 1, 1), ("U", 3, 1), ("S", 1), ("B", 2), ("W", 2), ("V", 0), ("G", 6), ("B", 0), ("W", 3),
+    ("V", 1), ("Z", 1, 2), ("A", 6), ("G", 7), ("C", 3), ("W", 0), ("C", 2), ("G", 4), ("A", 7), ("T", 1, 1, 1),
+    ("W", 1), ("Z", 3, 2), ("V", 2), ("G", 5), ("C", 0), ("A", 4), ("B", 7), ("V", 3), ("A", 5), ("Z", 1, 1),
+    ("B", 4), ("Z", 2, 2), ("C", 7), ("T", 1, 0, 1), ("B", 6), ("Y", 3, 3), ("B", 5), ("T", 1, 1, 0), ("Z", 3, 1),
+    ("C", 4), ("C", 6), ("Y", 0, 3), ("Z", 0, 2), ("Y", 2, 2), ("T", 0, 1, 0), ("C", 5), ("Y", 1, 2), ("V", 4),
+    ("Y", 3, 2), ("Y", 0, 2), ("Z", 0, 1), ("Z", 1, 0), ("T", 1, 0, 0), ("Z", 2, 1), ("Z", 3, 0), ("Y", 3, 1),
+    ("Y", 2, 1), ("Y", 1, 1), ("T", 0, 0, 0), ("Y", 0, 1), ("Z", 0, 0), ("Z", 2, 0), ("Y", 2, 0), ("Y", 3, 0),
+    ("Y", 1, 0), ("Y", 0, 0),
 )
 def attend_kernel(bounds, own_ref, all_ref, wq_ref, wk_ref, wv_ref, bq_ref, bv_ref,
                   segq_ref, segk_ref, mixed_ref, lse_ref, q_ref, k_ref, v_ref, bias, acc, top, total):
@@ -720,8 +720,8 @@
 
 def forward_kernel(sizes, micro, own_ref, wq_ref, wk_ref, wv_ref, wo_ref, wh_ref, wd_ref, hidden_bias_ref, query_bias_ref, value_bias_ref, seg_ref,
                    rest_ref, first_ref, turned_ref, mask_ref, biases_ref, mixed_ref, lse_ref, q_ref, k_ref, v_ref,
-                   weights, turned, bias_buf, mask, mixed_buf, lse_buf, q_buf, k_buf, v_buf, tokens_buf, acc, top, total,
-                   send_sems, recv_sems, local_sems, unit_sems, turn_buf):
+                   weights, turned, bias_buf, mask, mixed_buf, lse_buf, q_buf, k_buf, v_buf, tokens_buf, acc, score_buf, prob_buf, values_t,
+                   send_sems, recv_sems, local_sems, unit_sems):
     floats, halves = jnp.float32, jnp.bfloat16
     lines, device = place(sizes)
     (x, _), (y, _), (k, _), (z, cols) = (lines[a] for a in "xykz")
@@ -749,8 +749,7 @@
     targets = [weights.at[0], rest_ref.at[0], rest_ref.at[1]]
     packed = [wq_ref[...], wk_ref[...], wv_ref[...], wo_ref[...].astype(floats).T.astype(halves)]
     weights[0, z, x, y, k] = jnp.concatenate(packed, 1)
-    turn_buf[...] = wd_ref[...].astype(floats).T.astype(halves)
-    begin = [local(wh_ref, targets[1].at[z, x, y, k]), local(turn_buf, targets[2].at[z, x, y, k])]
+    begin = [local(wh_ref, targets[1].at[z, x, y, k]), local(wd_ref, targets[2].at[z, x, y, k])]
     begin += [local(own_ref.at[m], tokens_buf.at[m, z]) for m in range(micro)]
     for i, ref in enumerate((hidden_bias_ref, query_bias_ref, value_bias_ref)):
         bias_buf[z, i : i + 1, 0 : ref.shape[0]] = ref[...].astype(floats).reshape(1, -1)
@@ -804,42 +803,35 @@
         queries = pltpu.roll(queries.astype(halves).astype(floats) * HEAD_DIM ** -0.5, HEAD_DIM, 1)
         queries = jnp.where(places > 0, queries, 0.0).astype(halves)
         q_buf[m, c] = queries
-        heads = [keep(queries, places, h + 1) for h in range(3)]
-        acc[...] = jnp.zeros_like(acc)
-        total[...] = jnp.zeros_like(total)
-        top[...] = jnp.full_like(top, 2 * MASK_VALUE)
+        heads = jnp.concatenate([keep(queries, places, h + 1) for h in range(3)], 0)
         key_weight = plane(weights.at[0], c, K_AT)
         value_weight = plane(weights.at[0], c, V_AT)
         value_bias = bias_buf[c, 2:3, 0:WINDOW]
-
-        def step(block):
+        largest = jnp.full((1, 3 * rows), 2 * MASK_VALUE, floats)
+        for block in range(cols):
             rows_at = tokens_buf[m, block]
             keys = jnp.dot(rows_at, key_weight, preferred_element_type=floats).astype(halves)
             values = (jnp.dot(rows_at, value_weight, preferred_element_type=floats) + value_bias).astype(halves)
             k_buf[m, c, block] = keys
             v_buf[m, c, block] = values
-            values_t = values.T
+            values_t[:, block * rows : (block + 1) * rows] = values.T
             hidden = mask[m, block].astype(floats)
-            for h in range(3):
-                s = contract_cols(keys, heads[h]) + hidden
-                old = top[h : h + 1]
-                new = jnp.maximum(old, jnp.max(s, 0, keepdims=True))
-                p = jnp.exp(s - new)
-                shrink = jnp.exp(old - new)
-                top[h : h + 1] = new
-                total[h : h + 1] = total[h : h + 1] * shrink + jnp.sum(p, 0, keepdims=True)
-                at = pl.ds((h + 1) * HEAD_DIM, HEAD_DIM)
-                acc[at, :] = acc[at, :] * shrink + jnp.dot(
-                    values_t[h * HEAD_DIM : (h + 1) * HEAD_DIM], p.astype(halves), preferred_element_type=floats
-                )
-
+            s = contract_cols(keys, heads) + jnp.concatenate([hidden] * 3, 1)
+            score_buf[block] = s
+            largest = jnp.maximum(largest, jnp.max(s, 0, keepdims=True))
+        row_total = jnp.zeros((1, 3 * rows), floats)
         for block in range(cols):
-            step(block)
+            p = jnp.exp(score_buf[block] - largest)
+            row_total = row_total + jnp.sum(p, 0, keepdims=True)
+            prob_buf[block * rows : (block + 1) * rows] = p.astype(halves)
+        log_total = largest + jnp.log(row_total)
+        acc[0:HEAD_DIM] = jnp.zeros((HEAD_DIM, rows), floats)
         for h in range(3):
-            at = pl.ds((h + 1) * HEAD_DIM, HEAD_DIM)
-            acc[at, :] = acc[at, :] / total[h : h + 1]
+            lanes = slice(h * rows, (h + 1) * rows)
+            product = jnp.dot(values_t[h * HEAD_DIM : (h + 1) * HEAD_DIM], prob_buf[:, lanes], preferred_element_type=floats)
+            acc[pl.ds((h + 1) * HEAD_DIM, HEAD_DIM), :] = product / row_total[:, lanes]
+            lse_buf[m, c, h : h + 1] = log_total[:, lanes]
         mixed_buf[c, m] = acc[...].T.astype(halves)
-        lse_buf[m, c] = top[...] + jnp.log(jnp.maximum(total[...], 1e-30))
 
     def units(m, first, last):
         @pl.loop(first, last)
@@ -956,8 +948,8 @@
         scratch_shapes=[
             pltpu.VMEM((1, nc, ns, ny, 2, rb, w), halves),
             shapes[2], shapes[4], shapes[3], *shapes[5:],
-            pltpu.VMEM((micro, nc, rows, model), halves), pltpu.VMEM((WINDOW, rows), floats), pltpu.VMEM((8, rows), floats), pltpu.VMEM((8, rows), floats),
-            pltpu.SemaphoreType.DMA((count,)), pltpu.SemaphoreType.DMA((count,)), pltpu.SemaphoreType.DMA((20,)), pltpu.SemaphoreType.DMA((4, micro * nc)), pltpu.VMEM((rb, w), halves),
+            pltpu.VMEM((micro, nc, rows, model), halves), pltpu.VMEM((WINDOW, rows), floats), pltpu.VMEM((nc, rows, 3 * rows), floats), pltpu.VMEM((length, 3 * rows), halves), pltpu.VMEM((WINDOW, length), halves),
+            pltpu.SemaphoreType.DMA((count,)), pltpu.SemaphoreType.DMA((count,)), pltpu.SemaphoreType.DMA((20,)), pltpu.SemaphoreType.DMA((4, micro * nc)),
         ],
         compiler_params=pltpu.CompilerParams(collective_id=2, has_side_effects=True, vmem_limit_bytes=60 << 20),
         name="forward",
@@ -1235,8 +1227,11 @@
         inner = contract_cols(pick, product_high) + contract_cols(pick, product_low)
         value_side = pltpu.roll(mixed_grad, WINDOW - HEAD_DIM, 1).astype(halves)
         queries = q_buf[m, c]
-        query_heads = [keep(queries, places, h + 1) for h in range(3)]
-        grad_heads = [keep(value_side, places, h) for h in range(3)]
+        query_heads = jnp.concatenate([keep(queries, places, h + 1) for h in range(3)], 0)
+        grad_heads = jnp.concatenate([keep(value_side, places, h) for h in range(3)], 0)
+        side_by_side = lambda ref_rows: jnp.concatenate([ref_rows(h) for h in range(3)], 1)
+        log_total = side_by_side(lambda h: lse_ref[m, c, h : h + 1])
+        inner_row = side_by_side(lambda h: inner[h : h + 1])
         acc[...] = jnp.zeros_like(acc)
         key_weight = weights[c, :, K_AT : K_AT + WINDOW]
         value_weight = weights[c, :, V_AT : V_AT + WINDOW]
@@ -1246,16 +1241,15 @@
             values = v_buf[m, c, block]
             keys_t = keys.T
             hidden = mask[m, block].astype(floats)
-            key_grad = jnp.zeros((rows, WINDOW), floats)
-            value_grad = jnp.zeros((rows, WINDOW), floats)
+            hidden = jnp.concatenate([hidden] * 3, 1)
+            p = jnp.exp(contract_cols(keys, query_heads) + hidden - log_total)
+            prob_grad = contract_cols(values, grad_heads)
+            score_grad = (p * (prob_grad - inner_row)).astype(halves)
+            value_grad = jnp.dot(p.astype(halves), grad_heads, preferred_element_type=floats)
+            key_grad = jnp.dot(score_grad, query_heads, preferred_element_type=floats)
             for h in range(3):
-                p = jnp.exp(contract_cols(keys, query_heads[h]) + hidden - lse_ref[m, c, h : h + 1])
-                prob_grad = contract_cols(values, grad_heads[h])
-                score_grad = (p * (prob_grad - inner[h : h + 1])).astype(halves)
-                value_grad = value_grad + jnp.dot(p.astype(halves), grad_heads[h], preferred_element_type=floats)
-                key_grad = key_grad + jnp.dot(score_grad, query_heads[h], preferred_element_type=floats)
-                at = pl.ds(h * HEAD_DIM, HEAD_DIM)
-                acc[at, :] += jnp.dot(keys_t[(h + 1) * HEAD_DIM : (h + 2) * HEAD_DIM], score_grad, preferred_element_type=floats)
+                acc[pl.ds(h * HEAD_DIM, HEAD_DIM), :] += jnp.dot(
+                    keys_t[(h + 1) * HEAD_DIM : (h + 2) * HEAD_DIM], score_grad[:, h * rows : (h + 1) * rows], preferred_element_type=floats)
             key_low, value_low = key_grad.astype(halves), value_grad.astype(halves)
             k_buf[m, c, block] = key_low
             v_buf[m, c, block] = value_low
@@ -1557,16 +1551,24 @@
     )
 
 
-def deliver_kernel(sizes, width, back_ref, block_ref, sums_ref, *outs):
+def deliver_kernel(sizes, width, back_hbm, block_hbm, sums_hbm, *refs):
+    *outs, back_ref, block_ref, sums_ref, sems = refs
+    copies = [
+        pltpu.make_async_copy(source, target, sems.at[i])
+        for i, (source, target) in enumerate(((block_hbm, block_ref), (sums_hbm, sums_ref), (back_hbm, back_ref)))
+    ]
+    for copy in copies:
+        copy.start()
     (input_grad, query, key, value, query_bias, value_bias, output, output_bias, first_gain, first_shift, hidden, hidden_bias, down,
      down_bias, second_gain, second_shift) = outs
     here = lax.axis_index("col")
-    input_grad[...] = back_ref[...]
+    for copy in copies[:2]:
+        copy.wait()
     for i, ref in enumerate((query, key, value)):
         ref[...] = block_ref[0, :, i * width : (i + 1) * width]
     output[...] = block_ref[0, :, 3 * width : 4 * width].T
     hidden[...] = block_ref[1]
-    down[...] = block_ref[2].T
+    down[...] = block_ref[2]
     for i, ref in enumerate((output_bias, first_gain, first_shift, down_bias, second_gain, second_shift)):
         ref[...] = sums_ref[i : i + 1].reshape(-1)
     hidden_bias[...] = sums_ref[pl.ds(8 + here, 1)].reshape(-1)
@@ -1574,6 +1576,8 @@
     row = sums_ref[pl.ds(heads_at + here, 1)]
     query_bias[...] = row[:, 0:width].reshape(-1)
     value_bias[...] = row[:, WINDOW : WINDOW + width].reshape(-1)
+    copies[2].wait()
+    input_grad[...] = back_ref[...]
 
 
 def deliver(sizes, width, back, blocks, sums):
@@ -1581,13 +1585,14 @@
     _, rb, w = blocks.shape
     vmem = pl.BlockSpec(memory_space=pltpu.VMEM)
     square, vector = (rb, width), (model,)
-    shapes = [back.shape, square, square, square, (width,), (width,), (width, rb), vector, vector, vector, (rb, w), (w,), (w, rb),
+    shapes = [back.shape, square, square, square, (width,), (width,), (width, rb), vector, vector, vector, (rb, w), (w,), (rb, w),
               vector, vector, vector]
     return pl.pallas_call(
         functools.partial(deliver_kernel, sizes, width),
         out_shape=[jax.ShapeDtypeStruct(shape, jnp.float32) for shape in shapes],
-        in_specs=[vmem] * 3,
+        in_specs=[pl.BlockSpec(memory_space=pltpu.MemorySpace.HBM)] * 3,
         out_specs=[vmem] * len(shapes),
+        scratch_shapes=[pltpu.VMEM(a.shape, jnp.float32) for a in (back, blocks, sums)] + [pltpu.SemaphoreType.DMA((3,))],
         compiler_params=pltpu.CompilerParams(vmem_limit_bytes=32 << 20),
         name="deliver",
     )(back, blocks, sums)
@@ -1604,7 +1609,7 @@
     here = lax.axis_index("col")
     own = inputs[:, 0]
     rest, first, turned, mask, biases, mixed, lse, q, k, v = forward(
-        sizes, own, (query_weight, key_weight, value_weight, output_weight, hidden_weight, down_weight), hidden_bias, query_bias, value_bias, segment_ids)
+        sizes, own, (query_weight, key_weight, value_weight, output_weight, hidden_weight, down_weight.T), hidden_bias, query_bias, value_bias, segment_ids)
     first = first.reshape(cols, model, 4 * width)
     total = micro * rows
     flat = lambda a: a.reshape(total, -1)
@@ -1615,7 +1620,7 @@
     input_grad, reduced, sums = backward(sizes, parted(attn_grad), parted(first_grad), first, turned, mixed, lse, q, k, v,
                                          mask, part, sums)
     grads = deliver(sizes, width, input_grad, reduced, sums)
-    return (outputs.reshape(micro, 1, rows, model), grads[0][:, None], *grads[1:])
+    return (outputs.reshape(micro, 1, rows, model), grads[0][:, None], *grads[1:12], grads[12].T, *grads[13:])
 
 
 def per_device(sizes, inputs, segment_ids, query_weight, *rest):

time: 232 us -> 220 us (0.948)
  Pallas kernels: 225 us -> 215 us
  local copies, waits for them, and re-layouts: 6.05 us -> 3.45 us
    pallas_call x1, Pallas kernels: 101 us -> 96.2 us  [backward(): pl.pallas_call(functools.partial(backward_kernel, sizes, micro), out_shap...]
    pallas_call x1, Pallas kernels: 93.4 us -> 88.5 us  [forward(): pl.pallas_call(functools.partial(forward_kernel, sizes, micro), out_shape...]
    unnamed x8 -> x6, local copies, waits for them, and re-layouts: 6.05 us -> 3.45 us
where the time goes in v7:
time: 220 us; the launch traced here: 219 us
  Pallas kernels  215 us (98%)
  local copies, waits for them, and re-layouts  3.45 us (2%)
    pallas_call x1, Pallas kernels, backward(): pl.pallas_call(functools.partial(backward_kernel, sizes, micro), out_shap...  96.2 us
    pallas_call x1, Pallas kernels, forward(): pl.pallas_call(functools.partial(forward_kernel, sizes, micro), out_shape...  88.5 us
    pallas_call x1, Pallas kernels, middle(): pl.pallas_call(functools.partial(middle_kernel, cols), grid=(2 * cols,),...  28.1 us

profile of v7, /device:TPU:0, one launch (start us, length us, event | category | flops | bytes accessed | tf_op | source)
XLA Modules:
  0.0 219.4 jit_solution(16364529428228268541)
XLA Ops:
  0.7 88.5 %forward.1 = (bf16[2,4,2,2,2,96,768]{6,5,4,3,2,1,0:T(8,128)(2,1)}, bf16[4,2,2,2,96,768]{5,4,3,2,1,0:T(8,128)(2,1)}, bf16[768,2048]{1,0:T(8,128)(2,1)}, bf16[2,4,...) custom-call(bf16[2,256,768]{2,1,0:T(8,128)(2,1)} %bitcast.23, ...), custom_call_target="tpu_custom_call" | custom-call | tf_op jit(solution)/shard_map/forward/pallas_call | solution.py:943
  89.1 28.1 %middle.1 = (bf16[512,768]{1,0:T(8,128)(2,1)}, f32[512,768]{1,0:T(8,128)}, bf16[512,768]{1,0:T(8,128)(2,1)}, bf16[2,4,768,768]{3,2,1,0:T(8,128)(2,1)}, f32[16,768]{1,0:T(8,128)}) custom-call(bf16[512,768]{1,0:T(8,128)(2,1)} %bitcast.24, bf16[4,512,256]{2,1,0:T(8,128)(2,1)} %bitcast.22, bf16[4,768,768]{2,1,0:T(8,128)(2,1)} %bitcast.19, ...), custom_call_target="tpu_custom_call" | custom-call | tf_op jit(solution)/shard_map/middle/pallas_call | solution.py:1050
  117.3 96.2 %backward.1 = (f32[2,256,768]{2,1,0:T(8,128)}, f32[3,96,768]{2,1,0:T(8,128)}, f32[24,768]{1,0:T(8,128)}) custom-call(bf16[2,256,768]{2,1,0:T(8,128)(2,1)} %bitcast.27, f32[2,256,768]{2,1,0:T(8,128)} %bitcast.25, bf16[4,768,768]{2,1,0:T(8,128)(2,1)} %bitcast.20, bf16[768,2048]{1,0:T(8,128)(2,1)} %get-tuple-element.58.turned_ref, ...), custom_call_target="tpu_custom_call" | custom-call | tf_op jit(solution)/shard_map/backward/pallas_call | solution.py:1429
  213.5 0.0 copy-start
  213.5 1.4 copy-done
  214.9 0.0 copy-start.1
  214.9 1.2 copy-done.1
  216.1 0.0 copy-start.2
  216.1 0.9 copy-done.2
  217.0 2.2 %deliver.1 = (f32[2,256,768]{2,1,0:T(8,128)}, f32[96,192]{1,0:T(8,128)}, f32[96,192]{1,0:T(8,128)}, f32[96,192]{1,0:T(8,128)}, f32[192]{0:T(256)}, /*index=5*/f3...) custom-call(f32[2,256,768]{2,1,0:T(8,128)S(1)} %copy-done, ...), custom_call_target="tpu_custom_call" | custom-call | tf_op jit(solution)/shard_map/deliver/pallas_call | solution.py:1590
Async XLA Ops:
  213.5 1.4 copy-start
  214.9 1.2 copy-start.1
  216.1 0.9 copy-start.2

commit v8 on v7

--- a/solution.py
+++ b/solution.py
@@ -39,13 +39,14 @@
     )
 
 FORWARD_PLAN = (
-    ("Zs", 1), ("Zs", 3), ("Zs", 0), ("Z", 1, 1), ("Z", 3, 1), ("Z", 1, 2), ("Z", 1, 3), ("Zs", 2), ("Z", 3, 2),
-    ("Zs", 5), ("Z", 3, 3), ("Z", 0, 1), ("B", 1), ("Z", 0, 2), ("Z", 0, 3), ("Z", 2, 1), ("Zs", 4), ("Ts", 0),
-    ("Z", 2, 2), ("Z", 5, 1), ("B", 3), ("Z", 5, 2), ("Ts", 1), ("B", 0), ("Z", 2, 3), ("Z", 4, 1), ("T", 0, 1),
-    ("T", 0, 2), ("Z", 4, 2), ("T", 1, 1), ("Z", 5, 3), ("Ts", 2), ("Z", 4, 3), ("C", 1), ("C", 0), ("C", 3),
-    ("B", 5), ("Ts", 3), ("K", 1), ("T", 1, 2), ("R", 0), ("K", 0), ("U", 0, 0), ("B", 2), ("T", 2, 1), ("U", 0, 1),
-    ("C", 5), ("T", 3, 1), ("U", 0, 2), ("K", 3), ("B", 4), ("U", 0, 3), ("T", 2, 2), ("K", 5), ("C", 2), ("T", 3, 2),
-    ("R", 1), ("U", 1, 0), ("U", 1, 1), ("C", 4), ("U", 1, 2), ("U", 1, 3), ("K", 2), ("K", 4),
+    ("Zs", 1), ("Zs", 0), ("Z", 1, 1), ("Z", 0, 1), ("Z", 1, 2), ("Z", 1, 3), ("Zs", 4), ("Z", 0, 2), ("Ts", 1),
+    ("Zs", 2), ("Z", 0, 3), ("Zs", 5), ("B", 1), ("B", 0), ("Z", 4, 1), ("Z", 2, 1), ("Zs", 3), ("Z", 5, 1),
+    ("Z", 4, 2), ("Z", 4, 3), ("Z", 3, 1), ("Z", 2, 2), ("Z", 2, 3), ("T", 1, 1), ("C", 0), ("Ts", 0), ("B", 4),
+    ("C", 1), ("Z", 3, 2), ("Z", 5, 2), ("K", 1), ("Z", 3, 3), ("Z", 5, 3), ("T", 0, 1), ("K", 0), ("C", 4),
+    ("Ts", 3), ("T", 1, 2), ("B", 2), ("P", 0, 0), ("P", 0, 1), ("Ts", 2), ("T", 0, 2), ("R", 0), ("U", 0, 0),
+    ("P", 0, 2), ("U", 0, 1), ("T", 3, 1), ("B", 3), ("U", 0, 2), ("P", 0, 3), ("T", 2, 1), ("P", 1, 0), ("P", 1, 1),
+    ("P", 1, 2), ("K", 4), ("C", 2), ("B", 5), ("P", 1, 3), ("C", 3), ("U", 0, 3), ("T", 3, 2), ("T", 2, 2), ("R", 1),
+    ("U", 1, 0), ("U", 1, 1), ("C", 5), ("U", 1, 2), ("K", 2), ("K", 3), ("U", 1, 3), ("K", 5),
 )
 BACKWARD_PLAN = (
     ("G", 1), ("G", 3), ("L",), ("U", 2, 0), ("A", 1), ("G", 0), ("U", 0, 0), ("A", 3), ("U", 1, 0), ("U", 3, 0),
@@ -798,23 +799,27 @@
 
     places = place_of(rows)
 
-    def unit(m, c):
+    def project(m, c, block):
+        rows_at = tokens_buf[m, block]
+        k_buf[m, c, block] = jnp.dot(rows_at, plane(weights.at[0], c, K_AT), preferred_element_type=floats).astype(halves)
+        values = jnp.dot(rows_at, plane(weights.at[0], c, V_AT), preferred_element_type=floats) + bias_buf[c, 2:3, 0:WINDOW]
+        v_buf[m, c, block] = values.astype(halves)
+
+    def prepare(m, c):
         queries = jnp.dot(own_ref[m], plane(weights.at[0], c, Q_AT), preferred_element_type=floats) + bias_buf[c, 1:2, 0:WINDOW]
         queries = pltpu.roll(queries.astype(halves).astype(floats) * HEAD_DIM ** -0.5, HEAD_DIM, 1)
-        queries = jnp.where(places > 0, queries, 0.0).astype(halves)
-        q_buf[m, c] = queries
+        q_buf[m, c] = jnp.where(places > 0, queries, 0.0).astype(halves)
+        for way in (0, 1, 3):
+            project(m, c, lax.rem(z + way, cols))
+
+    def unit(m, c):
+        project(m, c, lax.rem(z + 2, cols))
+        queries = q_buf[m, c]
         heads = jnp.concatenate([keep(queries, places, h + 1) for h in range(3)], 0)
-        key_weight = plane(weights.at[0], c, K_AT)
-        value_weight = plane(weights.at[0], c, V_AT)
-        value_bias = bias_buf[c, 2:3, 0:WINDOW]
         largest = jnp.full((1, 3 * rows), 2 * MASK_VALUE, floats)
         for block in range(cols):
-            rows_at = tokens_buf[m, block]
-            keys = jnp.dot(rows_at, key_weight, preferred_element_type=floats).astype(halves)
-            values = (jnp.dot(rows_at, value_weight, preferred_element_type=floats) + value_bias).astype(halves)
-            k_buf[m, c, block] = keys
-            v_buf[m, c, block] = values
-            values_t[:, block * rows : (block + 1) * rows] = values.T
+            keys = k_buf[m, c, block]
+            values_t[:, block * rows : (block + 1) * rows] = v_buf[m, c, block].T
             hidden = mask[m, block].astype(floats)
             s = contract_cols(keys, heads) + jnp.concatenate([hidden] * 3, 1)
             score_buf[block] = s
@@ -883,7 +888,9 @@
         "B": take_second, "C": take_third, "K": take_core, "R": turn,
     }
     small.start()
-    head, tail, order = split_plan(FORWARD_PLAN)
+    head, tail, order = split_plan([("U", *task) if task[0] == "P" else task for task in FORWARD_PLAN])
+    kinds = [int(item[0] == "P") for item in order]
+    micros, heads_of = [item[-2] for item in order], [item[-1] for item in order]
     act[head[0][0]](*head[0][1:])
     for block in range(cols):
         if block > reach or cols - 1 - block > reach:
@@ -896,15 +903,23 @@
     for task in head[1:]:
         act[task[0]](*task[1:])
 
-    def leave(m, c, step, go):
+    def leave(m, c, go):
         for i, (source, target) in enumerate(keeps):
-            go(pltpu.make_async_copy(source.at[m, c], target.at[m, c], unit_sems.at[i, step]))
+            go(pltpu.make_async_copy(source.at[m, c], target.at[m, c], unit_sems.at[i, m * cols + c]))
 
     @pl.loop(0, len(order))
     def _(step):
-        m, c = pick(step, [m for m, _ in order]), pick(step, [c for _, c in order])
-        unit(m, c)
-        leave(m, c, step, lambda copy: copy.start())
+        m, c, kind = pick(step, micros), pick(step, heads_of), pick(step, kinds)
+
+        @pl.when(kind == 1)
+        def _():
+            prepare(m, c)
+
+        @pl.when(kind == 0)
+        def _():
+            unit(m, c)
+            leave(m, c, lambda copy: copy.start())
+
         for i, tasks in enumerate(tail[:-1]):
             if tasks:
                 @pl.when(step == i)
@@ -916,8 +931,9 @@
         done.append(local(source, target))
     for task in tail[-1]:
         act[task[0]](*task[1:])
-    for step, (m, c) in enumerate(order):
-        leave(m, c, step, lambda copy: copy.wait())
+    for m in range(micro):
+        for c in range(cols):
+            leave(m, c, lambda copy: copy.wait())
     for copy in done:
         copy.wait()
     post.close()
@@ -956,20 +972,26 @@
     )(own, *shards, hidden_bias, query_bias, value_bias, segments)
 
 
-def middle_kernel(cols, own_ref, mixed_ref, out_ref, hidden_ref, down_ref, bias_ref, *refs):
+def middle_kernel(cols, own_ref, mixed_ref, out_ref, rest_ref, bias_ref, *refs):
     vector_refs = refs[:6]
     (cot_ref, outputs_ref, first_grad_ref, attn_grad_ref, part_ref, sums_ref,
-     normal, scale, normed, normed_low, normed_t, grad_low, grad_t, act_buf, slope_buf, total) = refs[6:]
+     normal, scale, normed, normed_low, normed_t, grad_low, grad_t, act_buf, slope_buf, total, cot_buf, weight_buf, sems) = refs[6:]
     floats, halves = jnp.float32, jnp.bfloat16
     step = pl.program_id(0)
     rows, model = own_ref.shape
     chunks = [pl.ds(r * 256, 256) for r in range(rows // 256)]
     whole_rows = [pl.ds(0, rows)]
     bands = [pl.ds(n * 256, 256) for n in range(model // 256)]
+    loads = [[pltpu.make_async_copy(rest_ref.at[j, c], weight_buf.at[j, c], sems.at[j, c]) for j in range(2)] for c in range(cols)]
+    load_cot = pltpu.make_async_copy(cot_ref, cot_buf, sems.at[0, cols])
     vector = lambda i: vector_refs[i][...].astype(floats).reshape(1, -1)
 
     @pl.when(step == 0)
     def _():
+        for pair in loads:
+            for copy in pair:
+                copy.start()
+        load_cot.start()
         sums_ref[...] = jnp.zeros_like(sums_ref)
         for chunk in chunks:
             first_sum = own_ref[chunk].astype(floats) + vector(0)
@@ -983,24 +1005,31 @@
             normed_low[chunk] = norm_one.astype(halves)
             normed_t[:, chunk] = norm_one.astype(halves).T
 
+    for c in range(cols):
+        @pl.when(step == c)
+        def _(c=c):
+            for copy in loads[c]:
+                copy.wait()
+
     @pl.when(step < cols)
     def _():
         for chunk in chunks:
             for band in bands:
-                hidden = jnp.dot(normed_low[chunk], hidden_ref[0, 0, :, band], preferred_element_type=floats) + bias_ref[0, 0:1, band]
+                hidden = jnp.dot(normed_low[chunk], weight_buf[0, step, :, band], preferred_element_type=floats) + bias_ref[0, 0:1, band]
                 half_erf = 0.5 * lax.erf(hidden * 0.7071067811865476) + 0.5
                 act_buf[step, chunk, band] = (hidden * half_erf).astype(halves)
                 slope_buf[step, chunk, band] = (half_erf + hidden * (jnp.exp(-0.5 * hidden * hidden) * 0.3989422804014327)).astype(halves)
         for chunk in chunks:
             for band in bands:
-                total[chunk, band] += contract_cols(act_buf[step, chunk], down_ref[0, 0, band, :])
+                total[chunk, band] += contract_cols(act_buf[step, chunk], weight_buf[1, step, band, :])
 
     @pl.when(step == cols - 1)
     def _():
+        load_cot.wait()
         for chunk in chunks:
             normal_two, scale_two = norm_parts(total[chunk])
             outputs_ref[chunk] = (normal_two * vector(4) + vector(5)).astype(halves)
-            cot = cot_ref[chunk].astype(floats)
+            cot = cot_buf[chunk].astype(floats)
             second_grad = norm_back(cot * vector(4), normal_two, scale_two)
             total[chunk] = second_grad
             grad_low[chunk] = second_grad.astype(halves)
@@ -1015,7 +1044,7 @@
         bias_total = [jnp.zeros((1, 256), floats) for _ in bands]
         for chunk in chunks:
             for n, band in enumerate(bands):
-                pre = jnp.dot(grad_low[chunk], down_ref[0, 0, :, band], preferred_element_type=floats)
+                pre = jnp.dot(grad_low[chunk], weight_buf[1, c, :, band], preferred_element_type=floats)
                 pre = (pre * slope_buf[c, chunk, band].astype(floats)).astype(halves)
                 slope_buf[c, chunk, band] = pre
                 bias_total[n] = bias_total[n] + jnp.sum(pre.astype(floats), 0, keepdims=True)
@@ -1027,7 +1056,7 @@
                 part_ref[1, 0, side, band] = jnp.dot(grad_t[side, :], act_buf[c, :, band], preferred_element_type=floats).astype(halves)
         for chunk in chunks:
             for band in bands:
-                total[chunk, band] += contract_cols(slope_buf[c, chunk], hidden_ref[0, 0, band, :])
+                total[chunk, band] += contract_cols(slope_buf[c, chunk], weight_buf[0, c, band, :])
 
     @pl.when(step == 2 * cols - 1)
     def _():
@@ -1053,10 +1082,9 @@
         in_specs=[
             whole((rows, model)), whole(mixed.shape),
             pl.BlockSpec((cols, model, WINDOW), lambda i: (0, 0, O_AT // WINDOW)),
-            pl.BlockSpec((1, 1, model, rest.shape[-1]), lambda i: (0, lax.rem(i, cols), 0, 0)),
-            pl.BlockSpec((1, 1, model, rest.shape[-1]), lambda i: (1, lax.rem(i, cols), 0, 0)),
+            pl.BlockSpec(memory_space=pl.ANY),
             pl.BlockSpec((1, *biases.shape[1:]), lambda i: (lax.rem(i, cols), 0, 0)),
-            *[whole((model,))] * 6, whole((rows, model)),
+            *[whole((model,))] * 6, pl.BlockSpec(memory_space=pl.ANY),
         ],
         out_specs=[
             whole((rows, model)), whole((rows, model)), whole((rows, model)),
@@ -1071,11 +1099,12 @@
         scratch_shapes=[
             wide(floats), pltpu.VMEM((rows, 128), floats), wide(floats), wide(halves), pltpu.VMEM((model, rows), halves), wide(halves),
             pltpu.VMEM((model, rows), halves), pltpu.VMEM((cols, rows, rest.shape[-1]), halves),
-            pltpu.VMEM((cols, rows, rest.shape[-1]), halves), wide(floats),
+            pltpu.VMEM((cols, rows, rest.shape[-1]), halves), wide(floats), wide(halves),
+            pltpu.VMEM(rest.shape, halves), pltpu.SemaphoreType.DMA((2, cols + 1)),
         ],
         compiler_params=pltpu.CompilerParams(vmem_limit_bytes=56 << 20),
         name="middle",
-    )(own, mixed, first, rest, rest, biases, *vectors, cot)
+    )(own, mixed, first, rest, biases, *vectors, cot)
 
 
 class Inbox:

time: 220 us -> 217 us (0.986)
  no operation moved by 1% of the time
where the time goes in v8:
time: 217 us
  Pallas kernels  213 us (98%)
  local copies, waits for them, and re-layouts  3.45 us (2%)
    pallas_call x1, Pallas kernels, backward(): pl.pallas_call(functools.partial(backward_kernel, sizes, micro), out_shap...  95.9 us
    pallas_call x1, Pallas kernels, forward(): pl.pallas_call(functools.partial(forward_kernel, sizes, micro), out_shape...  87.7 us
    pallas_call x1, Pallas kernels, middle(): pl.pallas_call(functools.partial(middle_kernel, cols), grid=(2 * cols,),...  26.9 us

profile of v8, /device:TPU:0, one launch (start us, length us, event | category | flops | bytes accessed | tf_op | source)
XLA Modules:
  0.0 217.1 jit_solution(16365465218658810588)
XLA Ops:
  0.7 87.7 %forward.1 = (bf16[2,4,2,2,2,96,768]{6,5,4,3,2,1,0:T(8,128)(2,1)}, bf16[4,2,2,2,96,768]{5,4,3,2,1,0:T(8,128)(2,1)}, bf16[768,2048]{1,0:T(8,128)(2,1)}, bf16[2,4,...) custom-call(bf16[2,256,768]{2,1,0:T(8,128)(2,1)} %bitcast.22, ...), custom_call_target="tpu_custom_call" | custom-call | tf_op jit(solution)/shard_map/forward/pallas_call | solution.py:959
  88.4 26.9 %middle.1 = (bf16[512,768]{1,0:T(8,128)(2,1)}, f32[512,768]{1,0:T(8,128)}, bf16[512,768]{1,0:T(8,128)(2,1)}, bf16[2,4,768,768]{3,2,1,0:T(8,128)(2,1)}, f32[16,768]{1,0:T(8,128)}) custom-call(bf16[512,768]{1,0:T(8,128)(2,1)} %bitcast.23, bf16[4,512,256]{2,1,0:T(8,128)(2,1)} %bitcast.21, bf16[4,768,768]{2,1,0:T(8,128)(2,1)} %bitcast.17, ...), custom_call_target="tpu_custom_call" | custom-call | tf_op jit(solution)/shard_map/middle/pallas_call | solution.py:1079
  115.3 95.9 %backward.1 = (f32[2,256,768]{2,1,0:T(8,128)}, f32[3,96,768]{2,1,0:T(8,128)}, f32[24,768]{1,0:T(8,128)}) custom-call(bf16[2,256,768]{2,1,0:T(8,128)(2,1)} %bitcast.26, f32[2,256,768]{2,1,0:T(8,128)} %bitcast.24, bf16[4,768,768]{2,1,0:T(8,128)(2,1)} %bitcast.18, bf16[768,2048]{1,0:T(8,128)(2,1)} %get-tuple-element.58.turned_ref, ...), custom_call_target="tpu_custom_call" | custom-call | tf_op jit(solution)/shard_map/backward/pallas_call | solution.py:1458
  211.2 0.0 copy-start
  211.2 1.4 copy-done
  212.6 0.0 copy-start.1
  212.6 1.2 copy-done.1
  213.8 0.0 copy-start.2
  213.8 0.9 copy-done.2
  214.7 2.2 %deliver.1 = (f32[2,256,768]{2,1,0:T(8,128)}, f32[96,192]{1,0:T(8,128)}, f32[96,192]{1,0:T(8,128)}, f32[96,192]{1,0:T(8,128)}, f32[192]{0:T(256)}, /*index=5*/f3...) custom-call(f32[2,256,768]{2,1,0:T(8,128)S(1)} %copy-done, ...), custom_call_target="tpu_custom_call" | custom-call | tf_op jit(solution)/shard_map/deliver/pallas_call | solution.py:1619
Async XLA Ops:
  211.2 1.4 copy-start
  212.6 1.2 copy-start.1
  213.8 0.9 copy-start.2

commit v9 on v8

--- a/solution.py
+++ b/solution.py
@@ -900,12 +900,14 @@
                     tokens_buf[m, block] = jnp.zeros(own_ref.shape[1:], halves)
     for m in range(micro):
         masks(m)
+    done.append(local(mask, mask_ref))
     for task in head[1:]:
         act[task[0]](*task[1:])
 
     def leave(m, c, go):
         for i, (source, target) in enumerate(keeps):
             go(pltpu.make_async_copy(source.at[m, c], target.at[m, c], unit_sems.at[i, m * cols + c]))
+        go(pltpu.make_async_copy(mixed_buf.at[c, m], mixed_ref.at[c, m], unit_sems.at[len(keeps), m * cols + c]))
 
     @pl.loop(0, len(order))
     def _(step):
@@ -927,8 +929,7 @@
                     for task in tasks:
                         act[task[0]](*task[1:])
 
-    for source, target in ((bias_buf, biases_ref), (mixed_buf, mixed_ref), (mask, mask_ref)):
-        done.append(local(source, target))
+    done.append(local(bias_buf, biases_ref))
     for task in tail[-1]:
         act[task[0]](*task[1:])
     for m in range(micro):
@@ -965,7 +966,7 @@
             pltpu.VMEM((1, nc, ns, ny, 2, rb, w), halves),
             shapes[2], shapes[4], shapes[3], *shapes[5:],
             pltpu.VMEM((micro, nc, rows, model), halves), pltpu.VMEM((WINDOW, rows), floats), pltpu.VMEM((nc, rows, 3 * rows), floats), pltpu.VMEM((length, 3 * rows), halves), pltpu.VMEM((WINDOW, length), halves),
-            pltpu.SemaphoreType.DMA((count,)), pltpu.SemaphoreType.DMA((count,)), pltpu.SemaphoreType.DMA((20,)), pltpu.SemaphoreType.DMA((4, micro * nc)),
+            pltpu.SemaphoreType.DMA((count,)), pltpu.SemaphoreType.DMA((count,)), pltpu.SemaphoreType.DMA((20,)), pltpu.SemaphoreType.DMA((5, micro * nc)),
         ],
         compiler_params=pltpu.CompilerParams(collective_id=2, has_side_effects=True, vmem_limit_bytes=60 << 20),
         name="forward",
@@ -1117,7 +1118,7 @@
 
 def backward_kernel(sizes, micro, grad_ref, share_ref, first_ref, turned_ref, mixed_ref, lse_ref, q_ref, k_ref, v_ref,
                     mask_ref, part_ref, vec_ref,
-                    back_ref, block_ref, sums_ref,
+                    out_ref,
                     mine_buf, core_buf, stage_buf, in_a, in_b, in_c, in_d, in_z, tok_buf, tok_in, vec_buf,
                     weights, mixed_buf, q_buf, k_buf, v_buf, every_t, grad_t, mask, acc, spread, block_sum,
                     send_sems, recv_sems, local_sems, free_sem):
@@ -1125,6 +1126,13 @@
     lines, device = place(sizes)
     (x, ns), (y, ny), (k, _), (z, cols) = (lines[a] for a in "xykz")
     model = first_ref.shape[1]
+    back_rows = micro * grad_ref.shape[1]
+    block_rows = 3 * part_ref.shape[-2]
+    sums_ref = out_ref.at[pl.ds(back_rows + block_rows, out_ref.shape[0] - back_rows - block_rows)]
+
+    def back(m, begin=0, size=None):
+        return pl.ds(pl.multiple_of(m * grad_ref.shape[1] + begin, 8), size or grad_ref.shape[1])
+
     half = part_ref.shape[-1] // 2
     rb = part_ref.shape[-2]
     rows = grad_ref.shape[1]
@@ -1142,7 +1150,7 @@
         return pl.ds(n % 2 * (rb // 2), rb // 2)
 
     planes = [local(part_ref.at[n // 2, :, :, :, k, rows_of(n)], mine_buf.at[n // 2 + 1, :, :, :, rows_of(n)]) for n in range(4)]
-    loads = [local(*pair) for pair in ((first_ref, weights), (mixed_ref, mixed_buf), (q_ref, q_buf), (share_ref, back_ref))]
+    loads = [local(*pair) for pair in ((first_ref, weights), (mixed_ref, mixed_buf), (q_ref, q_buf), (share_ref, out_ref.at[pl.ds(0, back_rows)]))]
     loads += [local(k_ref, k_buf), local(v_ref, v_buf)]
     loads += [local(mask_ref, mask)]
     late = [local(turned_ref, every_t)]
@@ -1292,10 +1300,10 @@
         q_buf[m, c] = query_low
         vec_buf[0, 0, pl.ds(small + c, 1), 0:WINDOW] += jnp.sum(query_low.astype(floats), 0, keepdims=True)
         vec_buf[0, 0, pl.ds(small + c, 1), WINDOW : 2 * WINDOW] += value_bias
-        back_ref[m] += contract_cols(query_low, weights[c, :, Q_AT : Q_AT + WINDOW])
+        out_ref[back(m)] += contract_cols(query_low, weights[c, :, Q_AT : Q_AT + WINDOW])
 
     def send_tokens(m):
-        back_ref[m] += spread[m, z]
+        out_ref[back(m)] += spread[m, z]
 
         @pl.loop(0, cols)
         def _(block):
@@ -1375,10 +1383,8 @@
     def take_tokens(m, h, e):
         line = tokens[m][h]
         if e == 0:
-            at = half_of(h)
-
             def add(target, source):
-                back_ref[m, at] += source[...].astype(floats)
+                out_ref[back(m, h * (rows // 2), rows // 2)] += source[...].astype(floats)
 
             line.add = add
         along(line, e)
@@ -1435,7 +1441,7 @@
     for task in tail[-1]:
         act[task[0]](*task[1:])
     for j in range(3):
-        block_ref[j] = mine_buf[j, z, x, y].astype(floats)
+        out_ref[pl.ds(back_rows + j * rb, rb)] = mine_buf[j, z, x, y].astype(floats)
     post.close()
 
 
@@ -1455,15 +1461,12 @@
     vmem = pl.BlockSpec(memory_space=pltpu.VMEM)
     anywhere = pl.BlockSpec(memory_space=pl.ANY)
     buf = lambda *shape, kind=halves: pltpu.VMEM(shape, kind)
+    total = micro * rows + 3 * rb + vec_shape[0]
     return pl.pallas_call(
         functools.partial(backward_kernel, sizes, micro),
-        out_shape=[
-            jax.ShapeDtypeStruct((micro, rows, model), floats),
-            jax.ShapeDtypeStruct((3, rb, w), floats),
-            jax.ShapeDtypeStruct(vec_shape, floats),
-        ],
+        out_shape=jax.ShapeDtypeStruct((total, model), floats),
         in_specs=[vmem, anywhere, anywhere, anywhere, anywhere, vmem, anywhere, anywhere, anywhere, anywhere, anywhere, vmem],
-        out_specs=[vmem] * 3,
+        out_specs=vmem,
         scratch_shapes=[
             buf(3, nc, ns, ny, rb, w), buf(2, nc, ns, ny, rb, w), buf(nc, ns, ny, rb, w),
             buf(3, ways(ns), max(ns - 1, 1), nc, ny, rb, w // 2), buf(3, ways(ny), max(ny - 1, 1), nc, ns, rb, w // 2),
@@ -1478,7 +1481,7 @@
         ],
         compiler_params=pltpu.CompilerParams(collective_id=3, has_side_effects=True, vmem_limit_bytes=62 << 20),
         name="backward",
-    )(grad, share, first, turned, mixed, lse, q, k, v, mask,
+    )(grad, share.reshape(micro * rows, model), first, turned, mixed, lse, q, k, v, mask,
       part.reshape(2, nc, ns, ny, 2, rb, w), vectors)
 
 
@@ -1580,18 +1583,24 @@
     )
 
 
-def deliver_kernel(sizes, width, back_hbm, block_hbm, sums_hbm, *refs):
+def deliver_kernel(sizes, width, results, *refs):
     *outs, back_ref, block_ref, sums_ref, sems = refs
+    micro, rows, _ = back_ref.shape
+    rb = block_ref.shape[1]
+    at = micro * rows
+    pieces = [(results.at[pl.ds(at + j * rb, rb)], block_ref.at[j]) for j in range(3)]
+    pieces += [(results.at[pl.ds(at + 3 * rb, sums_ref.shape[0])], sums_ref)]
+    pieces += [(results.at[pl.ds(m * rows, rows)], back_ref.at[m]) for m in range(micro)]
     copies = [
         pltpu.make_async_copy(source, target, sems.at[i])
-        for i, (source, target) in enumerate(((block_hbm, block_ref), (sums_hbm, sums_ref), (back_hbm, back_ref)))
+        for i, (source, target) in enumerate(pieces)
     ]
     for copy in copies:
         copy.start()
     (input_grad, query, key, value, query_bias, value_bias, output, output_bias, first_gain, first_shift, hidden, hidden_bias, down,
      down_bias, second_gain, second_shift) = outs
     here = lax.axis_index("col")
-    for copy in copies[:2]:
+    for copy in copies[:4]:
         copy.wait()
     for i, ref in enumerate((query, key, value)):
         ref[...] = block_ref[0, :, i * width : (i + 1) * width]
@@ -1605,26 +1614,28 @@
     row = sums_ref[pl.ds(heads_at + here, 1)]
     query_bias[...] = row[:, 0:width].reshape(-1)
     value_bias[...] = row[:, WINDOW : WINDOW + width].reshape(-1)
-    copies[2].wait()
+    for copy in copies[4:]:
+        copy.wait()
     input_grad[...] = back_ref[...]
 
 
-def deliver(sizes, width, back, blocks, sums):
-    model = sums.shape[1]
-    _, rb, w = blocks.shape
+def deliver(sizes, width, tokens_shape, block_shape, results):
+    micro, rows, model = tokens_shape
+    rb, w = block_shape
+    sums_rows = results.shape[0] - micro * rows - 3 * rb
     vmem = pl.BlockSpec(memory_space=pltpu.VMEM)
     square, vector = (rb, width), (model,)
-    shapes = [back.shape, square, square, square, (width,), (width,), (width, rb), vector, vector, vector, (rb, w), (w,), (rb, w),
+    shapes = [tokens_shape, square, square, square, (width,), (width,), (width, rb), vector, vector, vector, (rb, w), (w,), (rb, w),
               vector, vector, vector]
     return pl.pallas_call(
         functools.partial(deliver_kernel, sizes, width),
         out_shape=[jax.ShapeDtypeStruct(shape, jnp.float32) for shape in shapes],
-        in_specs=[pl.BlockSpec(memory_space=pltpu.MemorySpace.HBM)] * 3,
+        in_specs=[pl.BlockSpec(memory_space=pltpu.MemorySpace.HBM)],
         out_specs=[vmem] * len(shapes),
-        scratch_shapes=[pltpu.VMEM(a.shape, jnp.float32) for a in (back, blocks, sums)] + [pltpu.SemaphoreType.DMA((3,))],
+        scratch_shapes=[pltpu.VMEM(a, jnp.float32) for a in (tokens_shape, (3, rb, w), (sums_rows, model))] + [pltpu.SemaphoreType.DMA((4 + micro,))],
         compiler_params=pltpu.CompilerParams(vmem_limit_bytes=32 << 20),
         name="deliver",
-    )(back, blocks, sums)
+    )(results)
 
 
 def per_device_fused(sizes, inputs, segment_ids, query_weight, key_weight, value_weight, query_bias, value_bias,
@@ -1646,9 +1657,9 @@
         flat(own), mixed.reshape(cols, total, WINDOW), first, rest.reshape(2, cols, model, -1), biases,
         (output_bias, first_gain, first_shift, down_bias, second_gain, second_shift), flat(cotangent[:, 0]))
     parted = lambda a: a.reshape(micro, rows, model)
-    input_grad, reduced, sums = backward(sizes, parted(attn_grad), parted(first_grad), first, turned, mixed, lse, q, k, v,
+    results = backward(sizes, parted(attn_grad), parted(first_grad), first, turned, mixed, lse, q, k, v,
                                          mask, part, sums)
-    grads = deliver(sizes, width, input_grad, reduced, sums)
+    grads = deliver(sizes, width, own.shape, hidden_weight.shape, results)
     return (outputs.reshape(micro, 1, rows, model), grads[0][:, None], *grads[1:12], grads[12].T, *grads[13:])
 
 

time: 217 us -> 215 us (level)
  no operation moved by 1% of the time
where the time goes in v9:
time: 215 us
  Pallas kernels  212 us (99%)
    pallas_call x1, Pallas kernels, backward(): pl.pallas_call(functools.partial(backward_kernel, sizes, micro), out_shap...  95.6 us
    pallas_call x1, Pallas kernels, forward(): pl.pallas_call(functools.partial(forward_kernel, sizes, micro), out_shape...  87.1 us
    pallas_call x1, Pallas kernels, middle(): pl.pallas_call(functools.partial(middle_kernel, cols), grid=(2 * cols,),...  26.9 us

profile of v9, /device:TPU:0, one launch (start us, length us, event | category | flops | bytes accessed | tf_op | source)
XLA Modules:
  0.0 214.5 jit_solution(11502614029233060503)
XLA Ops:
  0.7 87.1 %forward.1 = (bf16[2,4,2,2,2,96,768]{6,5,4,3,2,1,0:T(8,128)(2,1)}, bf16[4,2,2,2,96,768]{5,4,3,2,1,0:T(8,128)(2,1)}, bf16[768,2048]{1,0:T(8,128)(2,1)}, bf16[2,4,...) custom-call(bf16[2,256,768]{2,1,0:T(8,128)(2,1)} %bitcast.21, ...), custom_call_target="tpu_custom_call" | custom-call | tf_op jit(solution)/shard_map/forward/pallas_call | solution.py:960
  87.8 26.9 %middle.1 = (bf16[512,768]{1,0:T(8,128)(2,1)}, f32[512,768]{1,0:T(8,128)}, bf16[512,768]{1,0:T(8,128)(2,1)}, bf16[2,4,768,768]{3,2,1,0:T(8,128)(2,1)}, f32[16,768]{1,0:T(8,128)}) custom-call(bf16[512,768]{1,0:T(8,128)(2,1)} %bitcast.22, bf16[4,512,256]{2,1,0:T(8,128)(2,1)} %bitcast.20, bf16[4,768,768]{2,1,0:T(8,128)(2,1)} %bitcast.16, ...), custom_call_target="tpu_custom_call" | custom-call | tf_op jit(solution)/shard_map/middle/pallas_call | solution.py:1080
  114.8 95.6 %backward.1.results = f32[824,768]{1,0:T(8,128)} custom-call(bf16[2,256,768]{2,1,0:T(8,128)(2,1)} %bitcast.24, f32[512,768]{1,0:T(8,128)} %get-tuple-element.54.share_ref, bf16[4,768,768]{2,1,0:T(8,128)(2,1)} %bitcast.17, bf16[768,2048]{1,0:T(8,128)(2,1)} %get-tuple-element.55.turned_ref, bf16[4,2,256,256]{3,2,1,0:T(8,128)(2,1)} %get-tuple-element.48.mixed_ref, ...), custom_call_target="tpu_custom_call" | custom-call | tf_op jit(solution)/shard_map/backward/pallas_call | solution.py:1465
  210.4 0.0 copy-start
  210.4 1.7 copy-done
  212.1 2.2 %deliver.1 = (f32[2,256,768]{2,1,0:T(8,128)}, f32[96,192]{1,0:T(8,128)}, f32[96,192]{1,0:T(8,128)}, f32[96,192]{1,0:T(8,128)}, f32[192]{0:T(256)}, /*index=5*/f3...) custom-call(f32[824,768]{1,0:T(8,128)S(1)} %copy-done), custom_call_target="tpu_custom_call" | custom-call | tf_op jit(solution)/shard_map/deliver/pallas_call | solution.py:1630
Async XLA Ops:
  210.4 1.7 copy-start

commit v10 on v9

--- a/solution.py
+++ b/solution.py
@@ -39,14 +39,14 @@
     )
 
 FORWARD_PLAN = (
-    ("Zs", 1), ("Zs", 0), ("Z", 1, 1), ("Z", 0, 1), ("Z", 1, 2), ("Z", 1, 3), ("Zs", 4), ("Z", 0, 2), ("Ts", 1),
-    ("Zs", 2), ("Z", 0, 3), ("Zs", 5), ("B", 1), ("B", 0), ("Z", 4, 1), ("Z", 2, 1), ("Zs", 3), ("Z", 5, 1),
-    ("Z", 4, 2), ("Z", 4, 3), ("Z", 3, 1), ("Z", 2, 2), ("Z", 2, 3), ("T", 1, 1), ("C", 0), ("Ts", 0), ("B", 4),
-    ("C", 1), ("Z", 3, 2), ("Z", 5, 2), ("K", 1), ("Z", 3, 3), ("Z", 5, 3), ("T", 0, 1), ("K", 0), ("C", 4),
-    ("Ts", 3), ("T", 1, 2), ("B", 2), ("P", 0, 0), ("P", 0, 1), ("Ts", 2), ("T", 0, 2), ("R", 0), ("U", 0, 0),
-    ("P", 0, 2), ("U", 0, 1), ("T", 3, 1), ("B", 3), ("U", 0, 2), ("P", 0, 3), ("T", 2, 1), ("P", 1, 0), ("P", 1, 1),
-    ("P", 1, 2), ("K", 4), ("C", 2), ("B", 5), ("P", 1, 3), ("C", 3), ("U", 0, 3), ("T", 3, 2), ("T", 2, 2), ("R", 1),
-    ("U", 1, 0), ("U", 1, 1), ("C", 5), ("U", 1, 2), ("K", 2), ("K", 3), ("U", 1, 3), ("K", 5),
+    ("Zs", 1), ("Zs", 0), ("Z", 1, 1), ("Z", 0, 1), ("Z", 1, 2), ("Z", 1, 3), ("Z", 0, 2), ("Zs", 4), ("Z", 0, 3),
+    ("Zs", 2), ("B", 1), ("Ts", 1), ("Z", 4, 1), ("Z", 2, 1), ("Zs", 5), ("Zs", 3), ("B", 0), ("Z", 4, 2),
+    ("Z", 2, 2), ("Ts", 0), ("Z", 5, 1), ("Z", 4, 3), ("C", 0), ("Z", 2, 3), ("Z", 3, 1), ("B", 4), ("Z", 3, 2),
+    ("Z", 3, 3), ("T", 1, 1), ("T", 0, 1), ("B", 2), ("K", 0), ("C", 1), ("Z", 5, 2), ("T", 1, 2), ("Ts", 3),
+    ("C", 4), ("K", 1), ("T", 0, 2), ("P", 0, 0), ("Ts", 2), ("Z", 5, 3), ("R", 0), ("B", 3), ("U", 0, 0),
+    ("P", 0, 1), ("T", 3, 1), ("U", 0, 1), ("P", 0, 2), ("C", 2), ("P", 0, 3), ("T", 2, 1), ("P", 1, 0), ("B", 5),
+    ("U", 0, 2), ("K", 2), ("P", 1, 1), ("U", 0, 3), ("K", 4), ("P", 1, 2), ("P", 1, 3), ("C", 3), ("T", 3, 2),
+    ("T", 2, 2), ("R", 1), ("U", 1, 0), ("U", 1, 1), ("C", 5), ("U", 1, 2), ("K", 3), ("U", 1, 3), ("K", 5),
 )
 BACKWARD_PLAN = (
     ("G", 1), ("G", 3), ("L",), ("U", 2, 0), ("A", 1), ("G", 0), ("U", 0, 0), ("A", 3), ("U", 1, 0), ("U", 3, 0),

time: 215 us -> 213 us (level)
  no operation moved by 1% of the time
where the time goes in v10:
time: 213 us
  Pallas kernels  210 us (99%)
    pallas_call x1, Pallas kernels, backward(): pl.pallas_call(functools.partial(backward_kernel, sizes, micro), out_shap...  95.7 us
    pallas_call x1, Pallas kernels, forward(): pl.pallas_call(functools.partial(forward_kernel, sizes, micro), out_shape...  85.2 us
    pallas_call x1, Pallas kernels, middle(): pl.pallas_call(functools.partial(middle_kernel, cols), grid=(2 * cols,),...  26.9 us

profile of v10, /device:TPU:0, one launch (start us, length us, event | category | flops | bytes accessed | tf_op | source)
XLA Modules:
  0.0 212.6 jit_solution(302552878417207696)
XLA Ops:
  0.7 85.2 %forward.1 = (bf16[2,4,2,2,2,96,768]{6,5,4,3,2,1,0:T(8,128)(2,1)}, bf16[4,2,2,2,96,768]{5,4,3,2,1,0:T(8,128)(2,1)}, bf16[768,2048]{1,0:T(8,128)(2,1)}, bf16[2,4,...) custom-call(bf16[2,256,768]{2,1,0:T(8,128)(2,1)} %bitcast.21, ...), custom_call_target="tpu_custom_call" | custom-call | tf_op jit(solution)/shard_map/forward/pallas_call | solution.py:960
  85.9 26.9 %middle.1 = (bf16[512,768]{1,0:T(8,128)(2,1)}, f32[512,768]{1,0:T(8,128)}, bf16[512,768]{1,0:T(8,128)(2,1)}, bf16[2,4,768,768]{3,2,1,0:T(8,128)(2,1)}, f32[16,768]{1,0:T(8,128)}) custom-call(bf16[512,768]{1,0:T(8,128)(2,1)} %bitcast.22, bf16[4,512,256]{2,1,0:T(8,128)(2,1)} %bitcast.20, bf16[4,768,768]{2,1,0:T(8,128)(2,1)} %bitcast.16, ...), custom_call_target="tpu_custom_call" | custom-call | tf_op jit(solution)/shard_map/middle/pallas_call | solution.py:1080
  112.8 95.7 %backward.1.results = f32[824,768]{1,0:T(8,128)} custom-call(bf16[2,256,768]{2,1,0:T(8,128)(2,1)} %bitcast.24, f32[512,768]{1,0:T(8,128)} %get-tuple-element.54.share_ref, bf16[4,768,768]{2,1,0:T(8,128)(2,1)} %bitcast.17, bf16[768,2048]{1,0:T(8,128)(2,1)} %get-tuple-element.55.turned_ref, bf16[4,2,256,256]{3,2,1,0:T(8,128)(2,1)} %get-tuple-element.48.mixed_ref, ...), custom_call_target="tpu_custom_call" | custom-call | tf_op jit(solution)/shard_map/backward/pallas_call | solution.py:1465
  208.5 0.0 copy-start
  208.5 1.7 copy-done
  210.2 2.2 %deliver.1 = (f32[2,256,768]{2,1,0:T(8,128)}, f32[96,192]{1,0:T(8,128)}, f32[96,192]{1,0:T(8,128)}, f32[96,192]{1,0:T(8,128)}, f32[192]{0:T(256)}, /*index=5*/f3...) custom-call(f32[824,768]{1,0:T(8,128)S(1)} %copy-done), custom_call_target="tpu_custom_call" | custom-call | tf_op jit(solution)/shard_map/deliver/pallas_call | solution.py:1630
Async XLA Ops:
  208.5 1.7 copy-start
